TPU v7x, 32 devices: a whole 2x2x4 slice. The times are simulated.
32 devices in a mesh: dp: 4 (over z), seq: 8 (over y, x, core).
Axes of the slice: x: 2, y: 2, z: 4, core: 2. Of those that a mesh axis runs over, the one named last changes fastest.
Arguments:
- frames: bfloat16 [4, 1024, 768], P('dp', 'seq'), may hold values from -6 to 6
- segments: int32 [4, 1024], P('dp'), may hold values from 0 to 7, never falling along the last dimension, each value on 1 to 256 neighbouring positions
- conv_weight: float32 [31, 768], replicated, may hold values from -1 to 1
- point_weight: bfloat16 [768, 768], replicated, may hold values from -0.21875 to 0.21875
- router_weight: bfloat16 [768, 8], replicated, may hold values from -0.21875 to 0.21875
- expert_ids: int32 [4, 1024, 2], P('dp', 'seq'), may hold values from 0 to 7, all different within a row; in each aligned block of 128 rows (0 to 127, 128 to 255, ..., all dimensions but the last counted through in order) at most 48 rows name the same one
- expert_in: bfloat16 [8, 768, 3072], P('seq', None, 'dp'), may hold values from -0.21875 to 0.21875
- expert_out: bfloat16 [8, 3072, 768], P('seq', 'dp'), may hold values from -0.109375 to 0.109375
- cotangent: bfloat16 [4, 1024, 768], P('dp', 'seq'), may hold values from -6 to 6
Outputs:
- block_out: bfloat16 [4, 1024, 768], P('dp', 'seq')
- frames_grad: bfloat16 [4, 1024, 768], P('dp', 'seq')
- conv_grad: float32 [31, 768], replicated
- router_grad: float32 [768, 8], replicated
- point_grad: float32 [768, 768], replicated
- expert_in_grad: float32 [8, 768, 3072], P('seq', None, 'dp')
- expert_out_grad: float32 [8, 3072, 768], P('seq', 'dp')
Inputs may be any that keep to these rules, and one draw needn't show every extreme that they name: `segments`: within each pack the utterance number never falls; every utterance holds 1 to 256 frames, one exactly 256. `expert_ids`: A frame's two experts differ. Among the frames of one device (aligned blocks of 128 frames of a pack) no expert is named more than 48 times, a bound that some block reaches; every expert is named somewhere.
All inputs are finite; a program needn't handle non-finite values.
Results may differ from a plain program's by a relative error of at most 0.0069.
Values may be sent and summed in bfloat16 or wider, within the bound.
No kernel may reach another device: no remote copies, remote signals or barrier semaphores. Data moves between devices by JAX's collectives and lax.ppermute only.
A program may use at most 128 MiB of HBM per device.

v0:
```python
import jax
import jax.numpy as jnp
from jax import lax
from jax.sharding import PartitionSpec as P


def padded_2(array, sides, width):
    for axis, dim in sides:
        devices, length = (lax.axis_size(axis), array.shape[dim])
        up = [(i, (i + 1) % devices) for i in range(devices - 1)]
        down = [(j, i) for i, j in up]
        last = lax.slice_in_dim(array, length - width, length, axis=dim)
        leading = lax.slice_in_dim(array, 0, width, axis=dim)
        before = lax.ppermute(last, axis, up)
        after = lax.ppermute(leading, axis, down)
        array = jnp.concatenate([before, array, after], axis=dim)
    return array


def swish_slope(value):
    sigma = jax.nn.sigmoid(value)
    return sigma * (1.0 + value * (1.0 - sigma))


def local(
    frames,
    segments,
    conv_weight,
    point_weight,
    router_weight,
    expert_ids,
    expert_in,
    expert_out,
    cotangent,
):
    tokens_here = frames.shape[1]
    width = frames.shape[2]
    kernel = conv_weight.shape[0]
    reach = (kernel - 1) // 2
    experts = router_weight.shape[1]
    capacity = 3 * tokens_here // experts
    frame_rows = frames[0]
    padded = padded_2(frame_rows, (("seq", 0),), reach)
    seg_line = jnp.pad(segments[0], (reach, reach), constant_values=-1)
    first_row = lax.axis_index("seq") * tokens_here
    seg_pad = lax.dynamic_slice_in_dim(seg_line, first_row, tokens_here + 2 * reach)
    seg_own = seg_pad[reach : reach + tokens_here]
    conv_sum = jnp.zeros((tokens_here, width), jnp.float32)
    for offset in range(kernel):
        same_seg = (seg_pad[offset : offset + tokens_here] == seg_own)[:, None]
        conv_sum = conv_sum + conv_weight[offset] * jnp.where(
            same_seg, padded[offset : offset + tokens_here].astype(jnp.float32), 0.0
        )
    activated = jax.nn.silu(conv_sum).astype(jnp.bfloat16)
    mixed = (
        frame_rows.astype(jnp.float32)
        + jnp.dot(activated, point_weight, preferred_element_type=jnp.float32)
    ).astype(jnp.bfloat16)
    choices_here = expert_ids[0]
    logits_all = jnp.dot(mixed, router_weight, preferred_element_type=jnp.float32)
    pick = (choices_here[:, :, None] == jnp.arange(experts, dtype=jnp.int32)).astype(jnp.float32)
    gating = jax.nn.sigmoid(jnp.sum(pick * logits_all[:, None, :], axis=2))
    flat_expert = choices_here.reshape(-1)
    one_hot = (flat_expert[:, None] == jnp.arange(experts, dtype=jnp.int32)).astype(jnp.int32)
    slot_pos = jnp.sum((jnp.cumsum(one_hot, axis=0) - one_hot) * one_hot, axis=1)
    position = flat_expert * capacity + slot_pos
    table = (position[None, :] == jnp.arange(experts * capacity, dtype=jnp.int32)[:, None]).astype(
        jnp.bfloat16
    )

    def place(rows_rep):
        placed = jnp.dot(table, rows_rep, preferred_element_type=jnp.float32).astype(jnp.bfloat16)
        return placed.reshape(experts, capacity, width)

    def collect(buffer):
        flat_buf = buffer.reshape(experts * capacity, width)
        picked = lax.dot_general(
            table, flat_buf, (((0,), (0,)), ((), ())), preferred_element_type=jnp.float32
        )
        return picked.reshape(tokens_here, 2, width)

    sent_rows = place(jnp.repeat(mixed, 2, axis=0))
    arrived = lax.all_to_all(sent_rows, "seq", split_axis=0, concat_axis=0, tiled=True)
    rows_mine = arrived.reshape(-1, width)
    weight_in = expert_in[0]
    weight_out = expert_out[0]
    rows_all = lax.all_gather(rows_mine, "dp", axis=0, tiled=True)
    pre_act = jnp.dot(rows_all, weight_in, preferred_element_type=jnp.float32)
    hidden = jax.nn.silu(pre_act).astype(jnp.bfloat16)
    piece = hidden
    expert_y = lax.psum_scatter(
        jnp.dot(piece, weight_out, preferred_element_type=jnp.float32),
        "dp",
        scatter_dimension=0,
        tiled=True,
    ).astype(jnp.bfloat16)
    returned = lax.all_to_all(
        expert_y.reshape(experts, capacity, width), "seq", split_axis=0, concat_axis=0, tiled=True
    )
    y_rows = collect(returned)
    block_out = (mixed.astype(jnp.float32) + jnp.sum(gating[:, :, None] * y_rows, axis=1)).astype(
        jnp.bfloat16
    )
    cot_rows = cotangent[0].astype(jnp.float32)
    grad_rep = (gating.reshape(-1)[:, None] * jnp.repeat(cot_rows, 2, axis=0)).astype(jnp.bfloat16)
    grad_sent = place(grad_rep)
    grad_arrived = lax.all_to_all(
        grad_sent, "seq", split_axis=0, concat_axis=0, tiled=True
    ).reshape(-1, width)
    grads_all = lax.all_gather(grad_arrived, "dp", axis=0, tiled=True)
    grad_hidden = jnp.dot(grads_all, weight_out.T, preferred_element_type=jnp.float32)
    grad_pre = (grad_hidden * swish_slope(pre_act)).astype(jnp.bfloat16)
    grad_wout = jnp.dot(hidden.T, grads_all, preferred_element_type=jnp.float32)[None]
    grad_win = jnp.dot(rows_all.T, grad_pre, preferred_element_type=jnp.float32)[None]
    piece = grad_pre
    grad_back = lax.psum_scatter(
        jnp.dot(piece, weight_in.T, preferred_element_type=jnp.float32),
        "dp",
        scatter_dimension=0,
        tiled=True,
    ).astype(jnp.bfloat16)
    back_home = lax.all_to_all(
        grad_back.reshape(experts, capacity, width), "seq", split_axis=0, concat_axis=0, tiled=True
    )
    back_rows = collect(back_home)
    grad_gate = jnp.sum(cot_rows[:, None, :] * y_rows, axis=2)
    grad_logit = grad_gate * gating * (1.0 - gating)
    logit_cols = jnp.sum(pick * grad_logit[:, :, None], axis=1)
    part_router = jnp.dot(mixed.astype(jnp.float32).T, logit_cols, precision=lax.Precision.HIGHEST)
    grad_mixed = (
        cot_rows
        + jnp.sum(back_rows, axis=1)
        + jnp.dot(logit_cols, router_weight.astype(jnp.float32).T, precision=lax.Precision.HIGHEST)
    )
    grad_mixed_low = grad_mixed.astype(jnp.bfloat16)
    part_point = jnp.dot(activated.T, grad_mixed_low, preferred_element_type=jnp.float32)
    grad_act = jnp.dot(grad_mixed_low, point_weight.T, preferred_element_type=jnp.float32)
    grad_conv = (grad_act * swish_slope(conv_sum)).astype(jnp.bfloat16)
    grad_pad = padded_2(grad_conv, (("seq", 0),), reach)
    grad_conv_f = grad_conv.astype(jnp.float32)
    conv_terms = []
    back_sum = jnp.zeros((tokens_here, width), jnp.float32)
    for offset in range(kernel):
        same_seg = (seg_pad[offset : offset + tokens_here] == seg_own)[:, None]
        conv_terms.append(
            jnp.sum(
                grad_conv_f
                * jnp.where(
                    same_seg, padded[offset : offset + tokens_here].astype(jnp.float32), 0.0
                ),
                axis=0,
            )
        )
        start = 2 * reach - offset
        same_back = (seg_pad[start : start + tokens_here] == seg_own)[:, None]
        back_sum = back_sum + conv_weight[offset] * jnp.where(
            same_back, grad_pad[start : start + tokens_here].astype(jnp.float32), 0.0
        )
    part_conv = jnp.stack(conv_terms, axis=0)
    conv_grad, router_grad, point_grad = lax.psum(
        (part_conv, part_router, part_point), ("dp", "seq")
    )
    frames_grad = (grad_mixed + back_sum).astype(jnp.bfloat16)
    return (
        block_out[None],
        frames_grad[None],
        conv_grad,
        router_grad,
        point_grad,
        grad_win,
        grad_wout,
    )


def solution(mesh):
    placed = (
        P("dp", "seq", None),
        P("dp", None),
        P(),
        P(),
        P(),
        P("dp", "seq", None),
        P("seq", None, "dp"),
        P("seq", "dp", None),
        P("dp", "seq", None),
    )
    return jax.shard_map(
        local,
        mesh=mesh,
        in_specs=placed,
        out_specs=(
            P("dp", "seq", None),
            P("dp", "seq", None),
            P(),
            P(),
            P(),
            P("seq", None, "dp"),
            P("seq", "dp", None),
        ),
        check_vma=False,
    )
```

profile of v0, /device:TPU:0, one launch (start us, length us, event | category | flops | bytes accessed | tf_op | source)
XLA Modules:
  0.0 500.1 jit_solution(3648447888111772952)
XLA Ops:
  8.1 2.4 collective-permute-start
  20.3 11.4 %fusion.24 = f32[128,768]{1,0:T(8,128)S(1)} fusion(bf16[128,768]{1,0:T(8,128)(2,1)} %bitcast.76, bf16[15,768]{1,0:T(8,128)(2,1)S(1)} %collective-permute-done.1, bf16[15,768]{1,0:T(8,128)(2,1)S(1)} %collective-permute-done, f32[768]{0:T(1024)S(1)} %get-tuple-element.71, f32[768]{0:T(1024)S(1)} %get-tuple-element.72, f32[768]{0:T(1024)S(1)} %get-tuple-element.43, ...), kind=kLoop, calls=%fused_computation.127 | loop fusion | flops 20840448 | bytes 734976 | tf_op jit(solution)/shard_map/add | solution.py:51
  34.2 17.4 %all_to_all.20 = bf16[8,48,768]{2,1,0:T(8,128)(2,1)} all-to-all(bf16[8,48,768]{2,1,0:T(8,128)(2,1)S(1)} %bitcast.86), channel_id=1, replica_groups=mesh['dp'=4,'seq'=8] {'seq'}, dimensions={0} | all-to-all | bytes 1179648 | tf_op jit(solution)/shard_map/all_to_all | solution.py:83
  56.7 13.5 %all_to_all.21 = bf16[8,48,768]{2,1,0:T(8,128)(2,1)} all-to-all(bf16[8,48,768]{2,1,0:T(8,128)(2,1)S(1)} %bitcast.85), channel_id=1, replica_groups=mesh['dp'=4,'seq'=8] {'seq'}, dimensions={0} | all-to-all | bytes 1179648 | tf_op jit(solution)/shard_map/all_to_all | solution.py:107
  70.3 31.3 %all-gather.3.cloned.1.call-done = bf16[1536,768]{1,0:T(8,128)(2,1)} async-done(((bf16[384,768]{1,0:T(8,128)(2,1)}), bf16[1536,768]{1,0:T(8,128)(2,1)}) %all-gather.3.cloned.1.call-update) | async-done | bytes 2359312 | tf_op jit(solution)/shard_map/all_gather | solution.py:87
  101.7 4.0 fusion.5
  107.8 4.9 fusion.1
  112.9 39.6 %all-gather.5.cloned.1.call-done = bf16[1536,768]{1,0:T(8,128)(2,1)} async-done(((bf16[384,768]{1,0:T(8,128)(2,1)}), bf16[1536,768]{1,0:T(8,128)(2,1)}) %all-gather.5.cloned.1.call-update) | async-done | bytes 2359312 | tf_op jit(solution)/shard_map/all_gather | solution.py:110
  152.6 5.8 %multiply_convert_fusion = bf16[1536,768]{1,0:T(8,128)(2,1)S(1)} fusion(f32[1536,768]{1,0:T(8,128)} %copy-done.94, bf16[1536,768]{1,0:T(8,128)(2,1)} %all-gather.5.cloned.1.call-done, bf16[1,768,768]{2,1,0:T(8,128)(2,1)S(1)} %copy-done), kind=kOutput, calls=%fused_computation | convolution fusion | flops 1822556160 | bytes 10616832 | tf_op jit(solution)/shard_map/dot_general | solution.py:111
  159.8 4.2 fusion.3
  164.9 74.1 %reduce-scatter.3.cloned.1.call-done = f32[384,768]{1,0:T(8,128)} async-done(((f32[1536,768]{1,0:T(8,128)}), f32[384,768]{1,0:T(8,128)}) %reduce-scatter.3.cloned.1.call-update) | async-done | bytes 1179664 | tf_op jit(solution)/shard_map/reduce_scatter | solution.py:91
  241.1 3.7 all-to-all-start.1
  244.7 7.1 %convolution_bitcast_fusion = f32[1,768,768]{2,1,0:T(8,128)} fusion(bf16[1536,768]{1,0:T(8,128)(2,1)} %all-gather.5.cloned.1.call-done, f32[1536,768]{1,0:T(8,128)} %copy-done.94), kind=kOutput, calls=%fused_computation.35 | convolution fusion | flops 1817837568 | bytes 9437184 | tf_op jit(solution)/shard_map/dot_general | solution.py:113
  251.9 75.1 %reduce-scatter.5.cloned.1.call-done = f32[384,768]{1,0:T(8,128)} async-done(((f32[1536,768]{1,0:T(8,128)}), f32[384,768]{1,0:T(8,128)}) %reduce-scatter.5.cloned.1.call-update) | async-done | bytes 1179664 | tf_op jit(solution)/shard_map/reduce_scatter | solution.py:116
  326.9 2.2 convert_element_type.327
  329.9 3.7 all-to-all-start.3
  333.9 5.9 %convolution_bitcast_fusion.1 = f32[1,768,768]{2,1,0:T(8,128)} fusion(bf16[1536,768]{1,0:T(8,128)(2,1)} %all-gather.3.cloned.1.call-done, bf16[1536,768]{1,0:T(8,128)(2,1)} %copy-done.2), kind=kOutput, calls=%fused_computation.36 | convolution fusion | flops 1811939328 | bytes 7077888 | tf_op jit(solution)/shard_map/dot_general | solution.py:114
  340.3 3.6 all-to-all-done.3
  351.4 2.6 stack.127
  355.4 3.0 collective-permute-start.3
  359.3 41.2 %psum.22 = f32[768,8]{0,1:T(8,128)} all-reduce(f32[768,8]{0,1:T(8,128)S(1)} %fusion.149), channel_id=1, replica_groups=mesh['dp'=4,'seq'=8] {'dp','seq'}, use_global_device_ids=true, to_apply=%region_42.43 | all-reduce | flops 6144 | bytes 49152 | tf_op jit(solution)/shard_map/psum | solution.py:160
  400.6 4.9 fusion.140
  405.5 83.3 %all-reduce.4.cloned.1.call-done = (f32[31,768]{1,0:T(8,128)}, f32[768,768]{1,0:T(8,128)}) async-done(((f32[31,768]{1,0:T(8,128)}, f32[768,768]{1,0:T(8,128)}), (f32[31,768]{1,0:T(8,128)}, f32[768,768]{1,0:T(8,128)})) %all-reduce.4.cloned.1.call-update) | async-done | bytes 2454544 | tf_op jit(solution)/shard_map/psum | solution.py:160
  490.4 3.2 copy.46
  (290 shorter events, 36.6 us)
Async XLA Ops:
  7.2 100.7 %copy-start = (bf16[1,768,768]{2,1,0:T(8,128)(2,1)S(1)}, bf16[1,768,768]{2,1,0:T(8,128)(2,1)}, u32[]{:S(2)}) copy-start(bf16[1,768,768]{2,1,0:T(8,128)(2,1)} %param.16) | copy-start | bytes 3538948
  7.2 94.5 %all-gather.3.cloned.1.call-start = ((), (), s32[]{:S(2)}) async-start(), calls=%async_computation.6 | async-start | bytes 2949120 | tf_op jit(solution)/shard_map/all_gather | solution.py:87
  8.1 11.7 %collective-permute-start = (bf16[15,768]{1,0:T(8,128)(2,1)S(1)}, bf16[15,768]{1,0:T(8,128)(2,1)S(1)}, u32[]{:S(2)}, u32[]{:S(2)}) collective-permute-start(bf16[15,768]{1,0:T(8,128)(2,1)S(1)} %get-tuple-element.77), channel_id=1, source_target_pairs={{0,1},{1,2},{2,3},{3,4},{4,5},{5,6},{6,7},{8,9},{9,10},{10,11},{11... | collective-permute-start | bytes 69128 | tf_op jit(solution)/shard_map/ppermute | solution.py:14
  10.4 9.4 %collective-permute-start.1 = (bf16[15,768]{1,0:T(8,128)(2,1)S(1)}, bf16[15,768]{1,0:T(8,128)(2,1)S(1)}, u32[]{:S(2)}, u32[]{:S(2)}) collective-permute-start(bf16[15,768]{1,0:T(8,128)(2,1)S(1)} %get-tuple-element.78), channel_id=1, source_target_pairs={{1,0},{2,1},{3,2},{4,3},{5,4},{6,5},{7,6},{9,8},{10,9},{11,10},{12... | collective-permute-start | bytes 69128 | tf_op jit(solution)/shard_map/ppermute | solution.py:15
  51.6 100.9 %all-gather.5.cloned.1.call-start = ((), (), s32[]{:S(2)}) async-start(), calls=%async_computation.8 | async-start | bytes 2949120 | tf_op jit(solution)/shard_map/all_gather | solution.py:110
  55.4 50.3 %copy-start.90 = (f32[128,2]{0,1:T(2,128)}, f32[128,2]{0,1:T(2,128)S(1)}, u32[]{:S(2)}) copy-start(f32[128,2]{0,1:T(2,128)S(1)} %add_divide_fusion.2) | copy-start | bytes 3076
  70.3 168.7 %reduce-scatter.3.cloned.1.call-start = ((), (), s32[]{:S(2)}) async-start(), calls=%async_computation.7 | async-start | bytes 5898240 | tf_op jit(solution)/shard_map/reduce_scatter | solution.py:91
  112.7 47.1 %copy-start.92 = (bf16[1,768,768]{2,1,0:T(8,128)(2,1)S(1)}, bf16[1,768,768]{2,1,0:T(8,128)(2,1)}, u32[]{:S(2)}) copy-start(bf16[1,768,768]{2,1,0:T(8,128)(2,1)} %param.15) | copy-start | bytes 3538948
  112.7 214.2 %reduce-scatter.5.cloned.1.call-start = ((), (), s32[]{:S(2)}) async-start(), calls=%async_computation.9 | async-start | bytes 5898240 | tf_op jit(solution)/shard_map/reduce_scatter | solution.py:116
  241.1 88.0 %all-to-all-start.1 = ((bf16[8,48,768]{2,1,0:T(8,128)(2,1)}), bf16[8,48,768]{2,1,0:T(8,128)(2,1)S(1)}, u32[]{:S(2)}, u32[]{:S(2)}) async-start(bf16[8,48,768]{2,1,0:T(8,128)(2,1)} %bitcast.12), calls=%async_computation.2 | async-start | bytes 1179648 | tf_op jit(solution)/shard_map/all_to_all | solution.py:97
  329.9 14.1 %all-to-all-start.3 = ((bf16[8,48,768]{2,1,0:T(8,128)(2,1)}), bf16[8,48,768]{2,1,0:T(8,128)(2,1)S(1)}, u32[]{:S(2)}, u32[]{:S(2)}) async-start(bf16[8,48,768]{2,1,0:T(8,128)(2,1)} %bitcast.20), calls=%async_computation.5 | async-start | bytes 1179648 | tf_op jit(solution)/shard_map/all_to_all | solution.py:122
  333.6 155.3 %all-reduce.4.cloned.1.call-start = ((), (), s32[]{:S(2)}) async-start(), calls=%async_computation.10 | async-start | bytes 4915200 | tf_op jit(solution)/shard_map/psum | solution.py:160
  350.0 50.6 %copy-start.11 = (f32[768]{0:T(1024)S(1)}, f32[768]{0:T(1024)}, u32[]{:S(2)}) copy-start(f32[768]{0:T(1024)} %copy-done.10) | copy-start | bytes 9220
  350.0 50.6 %copy-start.13 = (f32[768]{0:T(1024)S(1)}, f32[768]{0:T(1024)}, u32[]{:S(2)}) copy-start(f32[768]{0:T(1024)} %copy-done.12) | copy-start | bytes 9220
  350.0 50.6 %copy-start.15 = (f32[768]{0:T(1024)S(1)}, f32[768]{0:T(1024)}, u32[]{:S(2)}) copy-start(f32[768]{0:T(1024)} %copy-done.14) | copy-start | bytes 9220
  350.0 50.6 %copy-start.17 = (f32[768]{0:T(1024)S(1)}, f32[768]{0:T(1024)}, u32[]{:S(2)}) copy-start(f32[768]{0:T(1024)} %copy-done.16) | copy-start | bytes 9220
  350.0 50.6 %copy-start.19 = (f32[768]{0:T(1024)S(1)}, f32[768]{0:T(1024)}, u32[]{:S(2)}) copy-start(f32[768]{0:T(1024)} %copy-done.18) | copy-start | bytes 9220
  350.0 50.6 %copy-start.21 = (f32[768]{0:T(1024)S(1)}, f32[768]{0:T(1024)}, u32[]{:S(2)}) copy-start(f32[768]{0:T(1024)} %copy-done.20) | copy-start | bytes 9220
  350.0 50.6 %copy-start.23 = (f32[768]{0:T(1024)S(1)}, f32[768]{0:T(1024)}, u32[]{:S(2)}) copy-start(f32[768]{0:T(1024)} %copy-done.22) | copy-start | bytes 9220
  350.0 50.6 %copy-start.25 = (f32[768]{0:T(1024)S(1)}, f32[768]{0:T(1024)}, u32[]{:S(2)}) copy-start(f32[768]{0:T(1024)} %copy-done.24) | copy-start | bytes 9220
  350.0 50.6 %copy-start.27 = (f32[768]{0:T(1024)S(1)}, f32[768]{0:T(1024)}, u32[]{:S(2)}) copy-start(f32[768]{0:T(1024)} %copy-done.26) | copy-start | bytes 9220
  350.1 50.6 %copy-start.29 = (f32[768]{0:T(1024)S(1)}, f32[768]{0:T(1024)}, u32[]{:S(2)}) copy-start(f32[768]{0:T(1024)} %copy-done.28) | copy-start | bytes 9220
  354.1 46.4 %collective-permute-start.2 = (bf16[15,768]{1,0:T(8,128)(2,1)S(1)}, bf16[15,768]{1,0:T(8,128)(2,1)S(1)}, u32[]{:S(2)}, u32[]{:S(2)}) collective-permute-start(bf16[15,768]{1,0:T(8,128)(2,1)S(1)} %get-tuple-element.75), channel_id=1, source_target_pairs={{1,0},{2,1},{3,2},{4,3},{5,4},{6,5},{7,6},{9,8},{10,9},{11,10},{12... | collective-permute-start | bytes 69128 | tf_op jit(solution)/shard_map/ppermute | solution.py:15
  355.4 45.2 %collective-permute-start.3 = (bf16[15,768]{1,0:T(8,128)(2,1)S(1)}, bf16[15,768]{1,0:T(8,128)(2,1)S(1)}, u32[]{:S(2)}, u32[]{:S(2)}) collective-permute-start(bf16[15,768]{1,0:T(8,128)(2,1)S(1)} %get-tuple-element.76), channel_id=1, source_target_pairs={{0,1},{1,2},{2,3},{3,4},{4,5},{5,6},{6,7},{8,9},{9,10},{10,11},{11... | collective-permute-start | bytes 69128 | tf_op jit(solution)/shard_map/ppermute | solution.py:14
  (82 other events, 393.5 us)
Sparse Core Ops, SparseCore 0:
  51.8 49.8 all-gather.2
  103.2 49.2 all-gather.4
  154.9 84.0 reduce-scatter.2
  241.1 85.7 reduce-scatter.4
  354.2 134.6 all-reduce.3
where the time goes:
time: 501 us; the launch traced here: 500 us
  waiting for transfers between devices  307 us (61%)
  blocking collectives  72.2 us (14%)
  matrix products  39.9 us (8%)
  other arithmetic  27 us (5%)
  local copies, waits for them, and re-layouts  22.7 us (5%)
  starting transfers between devices  15.9 us (3%)
  between operations  15.4 us (3%)
    psum x1, waiting for transfers between devices, local(): lax.psum((part_conv, part_router, part_point), ('dp', 'seq'))  83.3 us
    reduce_scatter x1, waiting for transfers between devices, local(): lax.psum_scatter(jnp.dot(piece, weight_in.T, preferred_element_type=jnp.f...  75.1 us
    reduce_scatter x1, waiting for transfers between devices, local(): lax.psum_scatter(jnp.dot(piece, weight_out, preferred_element_type=jnp.fl...  74.1 us
    psum x1, blocking collectives, local(): lax.psum((part_conv, part_router, part_point), ('dp', 'seq'))  41.2 us
    all_gather x1, waiting for transfers between devices, local(): grads_all = lax.all_gather(grad_arrived, 'dp', axis=0, tiled=True)  39.6 us
    all_gather x1, waiting for transfers between devices, local(): rows_all = lax.all_gather(rows_mine, 'dp', axis=0, tiled=True)  31.3 us
    all_to_all x1, blocking collectives, local(): lax.all_to_all(sent_rows, 'seq', split_axis=0, concat_axis=0, tiled=True)  17.4 us
    all_to_all x1, blocking collectives, local(): lax.all_to_all(grad_sent, 'seq', split_axis=0, concat_axis=0, tiled=True)  13.5 us
  transfers between devices with their start and end apart: 11, of which 6 were waited for; matrix products, arithmetic and copies ran while one was open for 11% of the time, Pallas kernels for 0%

commit v1 on v0

v1 whole, which is shorter than its diff:
```python
import jax
import jax.numpy as jnp
from jax import lax
from jax.experimental import pallas as pl
from jax.experimental.pallas import tpu as pltpu
from jax.sharding import PartitionSpec as P

F32 = jnp.float32
BF16 = jnp.bfloat16
EDGE = 16
LANES = 128


def dot(a, b):
    return jnp.dot(a, b, preferred_element_type=F32)


def sigmoid(value):
    return 1.0 / (1.0 + jnp.exp(-value))


def full(shape):
    zeros = (0,) * len(shape)
    return pl.BlockSpec(shape, lambda *_: zeros)


def fill_padded(scratch, before, own, after):
    rows = own.shape[0]
    scratch[0:EDGE, :] = before[...].astype(F32)
    scratch[EDGE : EDGE + rows, :] = own[...].astype(F32)
    scratch[EDGE + rows : 2 * EDGE + rows, :] = after[...].astype(F32)


def conv_forward_kernel(before, own, after, seg, weight, conv_out, act_out, scratch):
    rows, width = own.shape
    taps = weight.shape[0]
    shift = EDGE - (taps - 1) // 2
    fill_padded(scratch, before, own, after)

    def column(index, carry):
        lanes = pl.ds(pl.multiple_of(index * LANES, LANES), LANES)
        seg_own = seg[EDGE : EDGE + rows, :]
        total = jnp.zeros((rows, LANES), F32)
        for tap in range(taps):
            first = tap + shift
            same = seg[first : first + rows, :] == seg_own
            piece = jnp.where(same, scratch[first : first + rows, lanes], 0.0)
            total = total + weight[tap : tap + 1, lanes] * piece
        conv_out[:, lanes] = total
        act_out[:, lanes] = (total * sigmoid(total)).astype(BF16)
        return carry

    lax.fori_loop(0, width // LANES, column, 0)


def conv_forward(before, own, after, seg, weight):
    rows, width = own.shape
    return pl.pallas_call(
        conv_forward_kernel,
        out_shape=(
            jax.ShapeDtypeStruct((rows, width), F32),
            jax.ShapeDtypeStruct((rows, width), BF16),
        ),
        scratch_shapes=[pltpu.VMEM((rows + 2 * EDGE, width), F32)],
        compiler_params=pltpu.CompilerParams(vmem_limit_bytes=32 << 20),
        name="conv_forward",
    )(before, own, after, seg, weight)


def conv_backward_kernel(before, own, after, seg, weight, grad_mixed, out, scratch):
    rows, width = own.shape
    taps = weight.shape[0]
    shift = EDGE - (taps - 1) // 2
    fill_padded(scratch, before, own, after)

    def column(index, carry):
        lanes = pl.ds(pl.multiple_of(index * LANES, LANES), LANES)
        seg_own = seg[EDGE : EDGE + rows, :]
        total = grad_mixed[:, lanes]
        for tap in range(taps):
            first = tap + shift
            same = seg[first : first + rows, :] == seg_own
            piece = jnp.where(same, scratch[first : first + rows, lanes], 0.0)
            total = total + weight[taps - 1 - tap : taps - tap, lanes] * piece
        out[:, lanes] = total.astype(BF16)
        return carry

    lax.fori_loop(0, width // LANES, column, 0)


def conv_backward(before, own, after, seg, weight, grad_mixed):
    rows, width = own.shape
    return pl.pallas_call(
        conv_backward_kernel,
        out_shape=jax.ShapeDtypeStruct((rows, width), BF16),
        scratch_shapes=[pltpu.VMEM((rows + 2 * EDGE, width), F32)],
        compiler_params=pltpu.CompilerParams(vmem_limit_bytes=32 << 20),
        name="conv_backward",
    )(before, own, after, seg, weight, grad_mixed)


def tail_kernel(*refs):
    count = len(refs) - 11
    parts = refs[:count]
    cot, conv, point_t, before, own, after, seg, grad_mixed, grad_conv, conv_grad, scratch = refs[
        count:
    ]
    rows, width = own.shape
    taps = conv_grad.shape[0] - 1
    shift = EDGE - (taps - 1) // 2
    total = cot[...].astype(F32)
    for part in parts:
        total = total + part[...].astype(F32)
    grad_mixed[...] = total
    grad_act = dot(total.astype(BF16), point_t[...])
    value = conv[...]
    sigma = sigmoid(value)
    grad_conv[...] = (grad_act * (sigma * (1.0 + value * (1.0 - sigma)))).astype(BF16)
    fill_padded(scratch, before, own, after)
    conv_grad[taps : taps + 1, :] = jnp.zeros((1, width), F32)

    def column(index, carry):
        lanes = pl.ds(pl.multiple_of(index * LANES, LANES), LANES)
        seg_own = seg[EDGE : EDGE + rows, :]
        slope = grad_conv[:, lanes].astype(F32)
        for tap in range(taps):
            first = tap + shift
            same = seg[first : first + rows, :] == seg_own
            piece = jnp.where(same, scratch[first : first + rows, lanes], 0.0)
            conv_grad[tap : tap + 1, lanes] = jnp.sum(slope * piece, axis=0, keepdims=True)
        return carry

    lax.fori_loop(0, width // LANES, column, 0)


def tail(parts, cot, conv, point_t, before, own, after, seg, taps):
    rows, width = own.shape
    return pl.pallas_call(
        tail_kernel,
        out_shape=(
            jax.ShapeDtypeStruct((rows, width), F32),
            jax.ShapeDtypeStruct((rows, width), BF16),
            jax.ShapeDtypeStruct((taps + 1, width), F32),
        ),
        scratch_shapes=[pltpu.VMEM((rows + 2 * EDGE, width), F32)],
        compiler_params=pltpu.CompilerParams(vmem_limit_bytes=32 << 20),
        name="tail",
    )(*parts, cot, conv, point_t, before, own, after, seg)


def expert_kernel(
    rows,
    cots,
    weight_in,
    weight_out,
    weight_in_t,
    weight_out_t,
    router_cols,
    router_row,
    gated_out,
    back_out,
    hidden_out,
    grad_pre_out,
    grad_y_out,
    router_out,
):
    row = rows[...]
    width = row.shape[1]
    cot = cots[...].astype(F32)
    gate = sigmoid(dot(row, router_cols[...]))
    gate_wide = jnp.concatenate([gate] * (width // LANES), axis=1)
    grad_y = (gate_wide * cot).astype(BF16)
    grad_y_out[...] = grad_y
    pre = dot(row, weight_in[...])
    sigma = sigmoid(pre)
    hidden = (pre * sigma).astype(BF16)
    hidden_out[...] = hidden
    slope = sigma * (1.0 + pre * (1.0 - sigma))
    grad_pre = (dot(grad_y, weight_out_t[...]) * slope).astype(BF16)
    grad_pre_out[...] = grad_pre
    out = dot(hidden, weight_out[...])
    gated_out[...] = (gate_wide * out).astype(BF16)
    grad_gate = jnp.sum(cot * out, axis=1, keepdims=True)
    grad_logit = grad_gate * (gate * (1.0 - gate))[:, 0:1]
    back = dot(grad_pre, weight_in_t[...]) + grad_logit * router_row[0:1, :]
    back_out[...] = back.astype(BF16)
    partial = jnp.sum(row.astype(F32) * grad_logit, axis=0, keepdims=True)

    @pl.when(pl.program_id(0) == 0)
    def _():
        router_out[...] = jnp.zeros_like(router_out)

    router_out[0:1, :] += partial


def expert(rows, cots, weight_in, weight_out, weight_in_t, weight_out_t, router_cols, router_row):
    total, width = rows.shape
    inner = weight_in.shape[1]
    chunk = 384 if total % 384 == 0 else total

    def tall(columns):
        return pl.BlockSpec((chunk, columns), lambda i: (i, 0))

    return pl.pallas_call(
        expert_kernel,
        grid=(total // chunk,),
        in_specs=[
            tall(width),
            tall(width),
            full(weight_in.shape),
            full(weight_out.shape),
            full(weight_in_t.shape),
            full(weight_out_t.shape),
            full(router_cols.shape),
            full(router_row.shape),
        ],
        out_specs=(
            tall(width),
            tall(width),
            tall(inner),
            tall(inner),
            tall(width),
            full((8, width)),
        ),
        out_shape=(
            jax.ShapeDtypeStruct((total, width), BF16),
            jax.ShapeDtypeStruct((total, width), BF16),
            jax.ShapeDtypeStruct((total, inner), BF16),
            jax.ShapeDtypeStruct((total, inner), BF16),
            jax.ShapeDtypeStruct((total, width), BF16),
            jax.ShapeDtypeStruct((8, width), F32),
        ),
        compiler_params=pltpu.CompilerParams(
            dimension_semantics=("arbitrary",), vmem_limit_bytes=48 << 20
        ),
        name="expert",
    )(rows, cots, weight_in, weight_out, weight_in_t, weight_out_t, router_cols, router_row)


def partners(axis):
    devices = lax.axis_size(axis)
    if devices & (devices - 1):
        raise ValueError("axis size")
    return [[(i, i ^ k) for i in range(devices)] for k in range(1, devices)]


def from_all(array, axis):
    return [array] + [lax.ppermute(array, axis, pairs) for pairs in partners(axis)]


def to_all(arrays, axis):
    return [arrays[0]] + [
        lax.ppermute(part, axis, pairs) for part, pairs in zip(arrays[1:], partners(axis))
    ]


def edges(array, axis):
    devices = lax.axis_size(axis)
    up = [(i, i + 1) for i in range(devices - 1)]
    down = [(j, i) for i, j in up]
    before = lax.ppermute(array[array.shape[0] - EDGE :], axis, up)
    after = lax.ppermute(array[:EDGE], axis, down)
    return before, after


def exchange(array, axis):
    return lax.all_to_all(array, axis, split_axis=0, concat_axis=0, tiled=True)


def sum_parts(parts):
    total = parts[0].astype(F32)
    for part in parts[1:]:
        total = total + part.astype(F32)
    return total


def local(
    frames,
    segments,
    conv_weight,
    point_weight,
    router_weight,
    expert_ids,
    expert_in,
    expert_out,
    cotangent,
):
    rows_here, width = frames.shape[1:]
    taps = conv_weight.shape[0]
    experts = router_weight.shape[1]
    capacity = 3 * rows_here // experts
    packs = lax.axis_size("dp")
    places = lax.axis_size("seq")
    own_frames = frames[0]
    own_cot = cotangent[0]
    before, after = edges(own_frames, "seq")

    seg_line = jnp.pad(segments[0], (EDGE, EDGE), constant_values=-1)
    first_row = lax.axis_index("seq") * rows_here
    seg_here = lax.dynamic_slice_in_dim(seg_line, first_row, rows_here + 2 * EDGE)
    seg = jnp.broadcast_to(seg_here[:, None], (rows_here + 2 * EDGE, LANES))

    ids = jnp.stack(from_all(expert_ids[0].T, "dp"))
    cots = from_all(own_cot, "dp")
    frames_all = from_all(own_frames, "dp")
    span = packs * rows_here
    per_expert = packs * capacity

    named = (ids[:, :, None, :] == jnp.arange(experts, dtype=jnp.int32)[:, None]).astype(BF16)
    earlier = (jnp.arange(rows_here)[:, None] < jnp.arange(rows_here)[None, :]).astype(BF16)
    counts = lax.dot_general(
        named[:, 0] + named[:, 1], earlier, (((2,), (0,)), ((), ())), preferred_element_type=F32
    )
    slot = jnp.sum(named.astype(F32) * counts[:, None], axis=2).astype(jnp.int32)
    pack = jnp.arange(packs, dtype=jnp.int32)[:, None, None]
    position = ids * per_expert + pack * capacity + slot
    rows = jnp.arange(experts * per_expert, dtype=jnp.int32)[:, None]
    table = (
        (rows == position[:, 0].reshape(1, span)) | (rows == position[:, 1].reshape(1, span))
    ).astype(BF16)

    def place(array):
        placed = dot(table, array).astype(BF16)
        return placed.reshape(experts, per_expert, width)

    def collect(buffer):
        return lax.dot_general(
            table,
            buffer.reshape(-1, width),
            (((0,), (0,)), ((), ())),
            preferred_element_type=F32,
        )

    cots_arrived = exchange(place(jnp.concatenate(cots, axis=0)), "seq").reshape(-1, width)

    conv, activated = conv_forward(before, own_frames, after, seg, conv_weight)
    act_all = jnp.concatenate(from_all(activated, "dp"), axis=0)
    mixed_all = (
        jnp.concatenate(frames_all, axis=0).astype(F32) + dot(act_all, point_weight)
    ).astype(BF16)
    rows_arrived = exchange(place(mixed_all), "seq").reshape(-1, width)

    weight_in = expert_in[0]
    weight_out = expert_out[0]
    place_here = lax.axis_index("seq")
    router_col = lax.dynamic_slice_in_dim(router_weight, place_here, 1, axis=1)
    router_cols = jnp.broadcast_to(router_col, (width, LANES))
    router_row = jnp.broadcast_to(router_col.astype(F32).reshape(1, width), (8, width))
    gated, back, hidden, grad_pre, grad_y, router_part = expert(
        rows_arrived,
        cots_arrived,
        weight_in,
        weight_out,
        weight_in.T,
        weight_out.T,
        router_cols,
        router_row,
    )

    back_home = exchange(back.reshape(experts, per_expert, width), "seq")
    gated_home = exchange(gated.reshape(experts, per_expert, width), "seq")
    contract = (((0,), (0,)), ((), ()))
    grad_wout = lax.dot_general(hidden, grad_y, contract, preferred_element_type=F32)[None]
    grad_win = lax.dot_general(rows_arrived, grad_pre, contract, preferred_element_type=F32)[None]

    back_part = collect(back_home)
    back_low = back_part.astype(BF16).reshape(packs, rows_here, width)
    back_parts = to_all([back_low[k] for k in range(packs)], "dp")
    with_cot = jnp.concatenate(
        [(back_part[:rows_here] + own_cot.astype(F32)).astype(BF16)]
        + [back_low[k] for k in range(1, packs)],
        axis=0,
    )
    point_part = lax.dot_general(act_all, with_cot, contract, preferred_element_type=F32)

    spot = (jnp.arange(experts, dtype=jnp.int32) == place_here)[:, None]
    router_rows = jnp.where(spot, router_part[0:1, :], 0.0)
    used = width + experts
    step = EDGE * places
    padding = -used % step
    shared = jnp.concatenate(
        [point_part.astype(BF16), router_rows.astype(BF16), jnp.zeros((padding, width), BF16)],
        axis=0,
    ).reshape(places, (used + padding) // places, width)
    share = jnp.sum(exchange(shared, "seq").astype(F32), axis=0)
    share = sum_parts(from_all(share.astype(BF16), "dp")).astype(BF16)
    spread = exchange(jnp.broadcast_to(share[None], (places,) + share.shape), "seq")
    spread = spread.reshape(-1, width).astype(F32)
    point_grad = spread[:width]
    router_grad = spread[width:used].T

    grad_mixed, grad_conv, conv_part = tail(
        back_parts, own_cot, conv, point_weight.T, before, own_frames, after, seg, taps
    )
    grad_before, grad_after = edges(grad_conv, "seq")
    frames_grad = conv_backward(grad_before, grad_conv, grad_after, seg, conv_weight, grad_mixed)

    conv_seq = exchange(
        jnp.broadcast_to(conv_part.astype(BF16)[None], (places,) + conv_part.shape), "seq"
    )
    conv_sum = jnp.sum(conv_seq.astype(F32), axis=0).astype(BF16)
    conv_grad = sum_parts(from_all(conv_sum, "dp"))[:taps]

    gated_part = collect(gated_home).astype(BF16).reshape(packs, rows_here, width)
    gated_parts = to_all([gated_part[k] for k in range(packs)], "dp")
    block_out = (mixed_all[:rows_here].astype(F32) + sum_parts(gated_parts)).astype(BF16)
    return (
        block_out[None],
        frames_grad[None],
        conv_grad,
        router_grad,
        point_grad,
        grad_win,
        grad_wout,
    )


def solution(mesh):
    placed = (
        P("dp", "seq", None),
        P("dp", None),
        P(),
        P(),
        P(),
        P("dp", "seq", None),
        P("seq", None, "dp"),
        P("seq", "dp", None),
        P("dp", "seq", None),
    )
    return jax.shard_map(
        local,
        mesh=mesh,
        in_specs=placed,
        out_specs=(
            P("dp", "seq", None),
            P("dp", "seq", None),
            P(),
            P(),
            P(),
            P("seq", None, "dp"),
            P("seq", "dp", None),
        ),
        check_vma=False,
    )
```

time: 501 us -> 309 us (0.62)
  waiting for transfers between devices: 307 us -> 107 us
  starting transfers between devices: 15.9 us -> 106 us
  blocking collectives: 72.2 us -> 21.3 us
  other arithmetic: 27 us -> 5.22 us
  Pallas kernels: 0 us -> 21 us
  between operations: 15.4 us -> 1.18 us
  matrix products: 39.9 us -> 26.6 us
    reduce_scatter x2 -> x0, waiting for transfers between devices: 149 us -> none  [the longest x1 75.1 us: local(): lax.psum_scatter(jnp.dot(piece, weight_in.T, preferred_element_type=jnp.f...]
    psum x1 -> x0, waiting for transfers between devices: 83.3 us -> none  [local(): lax.psum((part_conv, part_router, part_point), ('dp', 'seq'))]
    all_gather x2 -> x0, waiting for transfers between devices: 70.9 us -> none  [the longest x1 39.6 us: local(): grads_all = lax.all_gather(grad_arrived, 'dp', axis=0, tiled=True)]
    all_to_all x2 -> x6, starting transfers between devices: 7.31 us -> 59.1 us  [exchange(): return lax.all_to_all(array, axis, split_axis=0, concat_axis=0, tiled=True)]
    all_to_all x2 -> x6, waiting for transfers between devices: 3.65 us -> 55.3 us  [exchange(): return lax.all_to_all(array, axis, split_axis=0, concat_axis=0, tiled=True)]
    ppermute x4 -> x28, waiting for transfers between devices: 0.01 us -> 51.4 us  [the longest x18 27.9 us: from_all(): lax.ppermute(array, axis, pairs)]
    psum x1 -> x0, blocking collectives: 41.2 us -> none  [local(): lax.psum((part_conv, part_router, part_point), ('dp', 'seq'))]
    ppermute x4 -> x28, starting transfers between devices: 7.97 us -> 46.9 us  [the longest x18 29 us: from_all(): lax.ppermute(array, axis, pairs)]
  transfers between devices with their start and end apart: 11 -> 34, of which waited for: 6 -> 12; matrix products, arithmetic and copies ran while one was open for 11% -> 11% of each run, Pallas kernels for 0% -> 3%
where the time goes in v1:
time: 309 us; the launch traced here: 306 us
  waiting for transfers between devices  107 us (35%)
  starting transfers between devices  106 us (34%)
  matrix products  26.6 us (9%)
  blocking collectives  21.3 us (7%)
  Pallas kernels  21 us (7%)
  local copies, waits for them, and re-layouts  17.7 us (6%)
  other arithmetic  5.22 us (2%)
    all_to_all x6, starting transfers between devices, exchange(): return lax.all_to_all(array, axis, split_axis=0, concat_axis=0, tiled=True)  59.1 us
    all_to_all x6, waiting for transfers between devices, exchange(): return lax.all_to_all(array, axis, split_axis=0, concat_axis=0, tiled=True)  55.3 us
    ppermute x18, starting transfers between devices, from_all(): lax.ppermute(array, axis, pairs)  29 us
    ppermute x18, waiting for transfers between devices, from_all(): lax.ppermute(array, axis, pairs)  27.9 us
    all_to_all x1, blocking collectives, exchange(): return lax.all_to_all(array, axis, split_axis=0, concat_axis=0, tiled=True)  21.3 us
    ppermute x6, waiting for transfers between devices, to_all(): lax.ppermute(part, axis, pairs)  20.7 us
    pallas_call x1, Pallas kernels, expert(): pl.pallas_call(expert_kernel, grid=(total // chunk,), in_specs=[tall(widt...  12.9 us
    ppermute x6, starting transfers between devices, to_all(): lax.ppermute(part, axis, pairs)  11.1 us
  transfers between devices with their start and end apart: 34, of which 12 were waited for; matrix products, arithmetic and copies ran while one was open for 11% of the time, Pallas kernels for 3%

profile of v1, /device:TPU:0, one launch (start us, length us, event | category | flops | bytes accessed | tf_op | source)
XLA Modules:
  0.0 305.7 jit_solution(13099737578541985277)
XLA Ops:
  0.6 3.1 %collective-permute-start.8 = (s32[2,128]{1,0:T(2,128)}, s32[2,128]{1,0:T(2,128)S(1)}, u32[]{:S(2)}, u32[]{:S(2)}) collective-permute-start(s32[2,128]{1,0:T(2,128)} %bitcast.97), channel_id=1, source_target_pairs={{0,8},{8,0},{16,24},{24,16},{1,9},{9,1},{17,25},{25,17},{2,10},{10... | collective-permute-start | bytes 3080 | tf_op jit(solution)/shard_map/ppermute | solution.py:248
  7.2 3.5 %collective-permute-start.12 = (bf16[128,768]{1,0:T(8,128)(2,1)}, bf16[128,768]{1,0:T(8,128)(2,1)S(1)}, u32[]{:S(2)}, u32[]{:S(2)}) collective-permute-start(bf16[128,768]{1,0:T(8,128)(2,1)} %bitcast.84), channel_id=1, source_target_pairs={{0,16},{8,24},{16,0},{24,8},{1,17},{9,25},{17,1},{25,9},{2,18},{10... | collective-permute-start | bytes 589832 | tf_op jit(solution)/shard_map/ppermute | solution.py:248
  15.5 9.7 %collective-permute-done.12 = bf16[128,768]{1,0:T(8,128)(2,1)S(1)} collective-permute-done((bf16[128,768]{1,0:T(8,128)(2,1)}, bf16[128,768]{1,0:T(8,128)(2,1)S(1)}, u32[]{:S(2)}, u32[]{:S(2)}) %collective-permute-start.12) | collective-permute-done | bytes 196640 | tf_op jit(solution)/shard_map/ppermute | solution.py:248
  25.2 3.9 %convolution_convert_fusion = bf16[1536,768]{1,0:T(8,128)(2,1)} fusion(s32[512]{0:T(512)S(1)} %get-tuple-element.41, s32[512]{0:T(512)S(1)} %get-tuple-element.40, bf16[128,768]{1,0:T(8,128)(2,1)S(1)} %collective-permute-done.13, bf16[128,768]{1,0:T(8,128)(2,1)S(1)} %collective-permute-done.12, bf16[128,768]{1,0:T(8,128)(2,1)S(1)} %collective-permute-done.11, ...), kind=kOutput, calls=%fused_computation | convolution fusion | flops 1214644224 | bytes 3149824 | tf_op jit(solution)/shard_map/dot_general | solution.py:15
  29.1 3.9 %all-to-all-start.1 = ((bf16[8,192,768]{2,1,0:T(8,128)(2,1)}), bf16[8,192,768]{2,1,0:T(8,128)(2,1)S(1)}, u32[]{:S(2)}, u32[]{:S(2)}) async-start(bf16[8,192,768]{2,1,0:T(8,128)(2,1)} %bitcast.91), calls=%async_computation.1 | async-start | bytes 4718592 | tf_op jit(solution)/shard_map/all_to_all | solution.py:267
  51.6 12.5 %collective-permute-done.6 = bf16[128,768]{1,0:T(8,128)(2,1)S(1)} collective-permute-done((bf16[128,768]{1,0:T(8,128)(2,1)S(1)}, bf16[128,768]{1,0:T(8,128)(2,1)S(1)}, u32[]{:S(2)}, u32[]{:S(2)}) %collective-permute-start.6) | collective-permute-done | bytes 196640 | tf_op jit(solution)/shard_map/ppermute | solution.py:248
  72.5 39.6 %all-to-all-start = ((bf16[8,192,768]{2,1,0:T(8,128)(2,1)}), bf16[8,192,768]{2,1,0:T(8,128)(2,1)}, u32[]{:S(2)}, u32[]{:S(2)}) async-start(bf16[8,192,768]{2,1,0:T(8,128)(2,1)} %bitcast.94), calls=%async_computation | async-start | bytes 4718592 | tf_op jit(solution)/shard_map/all_to_all | solution.py:267
  114.8 26.8 %all-to-all-done = bf16[8,192,768]{2,1,0:T(8,128)(2,1)} async-done(((bf16[8,192,768]{2,1,0:T(8,128)(2,1)}), bf16[8,192,768]{2,1,0:T(8,128)(2,1)}, u32[]{:S(2)}, u32[]{:S(2)}) %all-to-all-start) | async-done | bytes 2359328 | tf_op jit(solution)/shard_map/all_to_all | solution.py:267
  143.1 12.9 %expert.1 = (bf16[1536,768]{1,0:T(8,128)(2,1)}, bf16[1536,768]{1,0:T(8,128)(2,1)}, bf16[1536,768]{1,0:T(8,128)(2,1)}, bf16[1536,768]{1,0:T(8,128)(2,1)}, bf16[15...) custom-call(bf16[1536,768]{1,0:T(8,128)(2,1)} %bitcast.19.rows, bf16[1536,768]{1,0:T(8,128)(2,1)} %bitcast.88, ...), custom_call_target="tpu_custom_call" | custom-call | tf_op jit(solution)/shard_map/expert/pallas_call | solution.py:204
  156.6 3.7 %all-to-all-start.3 = ((bf16[8,192,768]{2,1,0:T(8,128)(2,1)}), bf16[8,192,768]{2,1,0:T(8,128)(2,1)S(1)}, u32[]{:S(2)}, u32[]{:S(2)}) async-start(bf16[8,192,768]{2,1,0:T(8,128)(2,1)} %bitcast.92), calls=%async_computation.3 | async-start | bytes 4718592 | tf_op jit(solution)/shard_map/all_to_all | solution.py:267
  161.3 28.5 %all-to-all-done.3 = bf16[8,192,768]{2,1,0:T(8,128)(2,1)S(1)} async-done(((bf16[8,192,768]{2,1,0:T(8,128)(2,1)}), bf16[8,192,768]{2,1,0:T(8,128)(2,1)S(1)}, u32[]{:S(2)}, u32[]{:S(2)}) %all-to-all-start.3) | async-done | bytes 2359328 | tf_op jit(solution)/shard_map/all_to_all | solution.py:267
  193.4 21.3 %all_to_all.35 = bf16[8,112,768]{2,1,0:T(8,128)(2,1)S(1)} all-to-all(bf16[8,112,768]{2,1,0:T(8,128)(2,1)S(1)} %bitcast.89), channel_id=1, replica_groups=mesh['dp'=4,'seq'=8] {'seq'}, dimensions={0} | all-to-all | bytes 2752512 | tf_op jit(solution)/shard_map/all_to_all | solution.py:267
  214.7 4.4 %all-to-all-start.2 = ((bf16[8,192,768]{2,1,0:T(8,128)(2,1)}), bf16[8,192,768]{2,1,0:T(8,128)(2,1)}, u32[]{:S(2)}, u32[]{:S(2)}) async-start(bf16[8,192,768]{2,1,0:T(8,128)(2,1)} %bitcast.90), calls=%async_computation.2 | async-start | bytes 4718592 | tf_op jit(solution)/shard_map/all_to_all | solution.py:267
  221.9 3.9 %collective-permute-start.17 = (bf16[128,768]{1,0:T(8,128)(2,1)S(1)}, bf16[128,768]{1,0:T(8,128)(2,1)S(1)}, u32[]{:S(2)}, u32[]{:S(2)}) collective-permute-start(bf16[128,768]{1,0:T(8,128)(2,1)S(1)} %get-tuple-element.31), channel_id=1, source_target_pairs={{0,8},{8,0},{16,24},{24,16},{1,9},{9,1},{17,25},{25,17},{2,10},{10... | collective-permute-start | bytes 589832 | tf_op jit(solution)/shard_map/ppermute | solution.py:253
  228.3 5.9 %convolution_bitcast_fusion.1 = f32[1,768,768]{2,1,0:T(8,128)} fusion(bf16[1536,768]{1,0:T(8,128)(2,1)} %bitcast.19.rows, bf16[1536,768]{1,0:T(8,128)(2,1)} %get-tuple-element.26), kind=kOutput, calls=%fused_computation.6 | convolution fusion | flops 1811939328 | bytes 7077888 | tf_op jit(solution)/shard_map/dot_general | solution.py:364
  235.0 8.0 %collective-permute-done.18.refs_2_ = bf16[128,768]{1,0:T(8,128)(2,1)S(1)} collective-permute-done((bf16[128,768]{1,0:T(8,128)(2,1)S(1)}, bf16[128,768]{1,0:T(8,128)(2,1)S(1)}, u32[]{:S(2)}, u32[]{:S(2)}) %collective-permute-start.18) | collective-permute-done | bytes 196640 | tf_op jit(solution)/shard_map/ppermute | solution.py:253
  243.0 3.2 %tail.1 = (f32[128,768]{1,0:T(8,128)S(1)}, bf16[128,768]{1,0:T(8,128)(2,1)S(1)}, f32[32,768]{1,0:T(8,128)S(1)}) custom-call(bf16[128,768]{1,0:T(8,128)(2,1)S(1)} %get-tuple-element.32.refs_0_, bf16[128,768]{1,0:T(8,128)(2,1)S(1)} %collective-permute-done.17.refs_1_, bf16[128,768]{1,0:T(8,128)(2,1)S(1)} %collective-permute-done.18.refs_2_, ...), custom_call_target="tpu_custom_call" | custom-call | tf_op jit(solution)/shard_map/tail/pallas_call | solution.py:138
  246.4 4.0 %collective-permute-start.25 = (bf16[112,768]{1,0:T(8,128)(2,1)S(1)}, bf16[112,768]{1,0:T(8,128)(2,1)S(1)}, u32[]{:S(2)}, u32[]{:S(2)}) collective-permute-start(bf16[112,768]{1,0:T(8,128)(2,1)S(1)} %reduce_sum.35), channel_id=1, source_target_pairs={{0,8},{8,0},{16,24},{24,16},{1,9},{9,1},{17,25},{25,17},{2,10},{10... | collective-permute-start | bytes 516104 | tf_op jit(solution)/shard_map/ppermute | solution.py:248
  253.6 3.9 %all-to-all-start.4 = ((bf16[8,32,768]{2,1,0:T(8,128)(2,1)}), bf16[8,32,768]{2,1,0:T(8,128)(2,1)S(1)}, u32[]{:S(2)}, u32[]{:S(2)}) async-start(bf16[8,32,768]{2,1,0:T(8,128)(2,1)} %broadcast_in_dim.84), calls=%async_computation.4 | async-start | bytes 786432 | tf_op jit(solution)/shard_map/all_to_all | solution.py:267
  257.5 5.8 %convolution_bitcast_fusion = f32[1,768,768]{2,1,0:T(8,128)} fusion(bf16[1536,768]{1,0:T(8,128)(2,1)} %get-tuple-element.27, bf16[1536,768]{1,0:T(8,128)(2,1)} %get-tuple-element.28), kind=kOutput, calls=%fused_computation.5 | convolution fusion | flops 1811939328 | bytes 7077888 | tf_op jit(solution)/shard_map/dot_general | solution.py:363
  267.2 3.7 %all-to-all-start.6 = ((bf16[8,112,768]{2,1,0:T(8,128)(2,1)}), bf16[8,112,768]{2,1,0:T(8,128)(2,1)S(1)}, u32[]{:S(2)}, u32[]{:S(2)}) async-start(bf16[8,112,768]{2,1,0:T(8,128)(2,1)} %broadcast_in_dim.90), calls=%async_computation.6 | async-start | bytes 2752512 | tf_op jit(solution)/shard_map/all_to_all | solution.py:267
  270.9 3.3 %convolution_convert_fusion.3 = bf16[512,768]{1,0:T(8,128)(2,1)S(1)} fusion(bf16[1536,768]{1,0:T(8,128)(2,1)} %bitcast.30, s32[512]{0:T(512)S(1)} %copy-done.27, s32[512]{0:T(512)S(1)} %copy-done.25), kind=kOutput, calls=%fused_computation.9 | convolution fusion | flops 1210712064 | bytes 3149824 | tf_op jit(solution)/shard_map/dot_general | solution.py:327
  283.0 4.0 %collective-permute-done.14 = bf16[128,768]{1,0:T(8,128)(2,1)} collective-permute-done((bf16[128,768]{1,0:T(8,128)(2,1)}, bf16[128,768]{1,0:T(8,128)(2,1)}, u32[]{:S(2)}, u32[]{:S(2)}) %collective-permute-start.14) | collective-permute-done | bytes 196640 | tf_op jit(solution)/shard_map/ppermute | solution.py:253
  287.0 7.8 %collective-permute-done.15 = bf16[128,768]{1,0:T(8,128)(2,1)} collective-permute-done((bf16[128,768]{1,0:T(8,128)(2,1)}, bf16[128,768]{1,0:T(8,128)(2,1)}, u32[]{:S(2)}, u32[]{:S(2)}) %collective-permute-start.15) | collective-permute-done | bytes 196640 | tf_op jit(solution)/shard_map/ppermute | solution.py:253
  (155 shorter events, 77.4 us)
Async XLA Ops:
  7.2 18.0 %collective-permute-start.12 = (bf16[128,768]{1,0:T(8,128)(2,1)}, bf16[128,768]{1,0:T(8,128)(2,1)S(1)}, u32[]{:S(2)}, u32[]{:S(2)}) collective-permute-start(bf16[128,768]{1,0:T(8,128)(2,1)} %bitcast.84), channel_id=1, source_target_pairs={{0,16},{8,24},{16,0},{24,8},{1,17},{9,25},{17,1},{25,9},{2,18},{10... | collective-permute-start | bytes 589832 | tf_op jit(solution)/shard_map/ppermute | solution.py:248
  10.7 14.5 %collective-permute-start.13 = (bf16[128,768]{1,0:T(8,128)(2,1)}, bf16[128,768]{1,0:T(8,128)(2,1)S(1)}, u32[]{:S(2)}, u32[]{:S(2)}) collective-permute-start(bf16[128,768]{1,0:T(8,128)(2,1)} %bitcast.85), channel_id=1, source_target_pairs={{0,24},{8,16},{16,8},{24,0},{1,25},{9,17},{17,9},{25,1},{2,26},{10... | collective-permute-start | bytes 589832 | tf_op jit(solution)/shard_map/ppermute | solution.py:248
  29.1 42.0 %all-to-all-start.1 = ((bf16[8,192,768]{2,1,0:T(8,128)(2,1)}), bf16[8,192,768]{2,1,0:T(8,128)(2,1)S(1)}, u32[]{:S(2)}, u32[]{:S(2)}) async-start(bf16[8,192,768]{2,1,0:T(8,128)(2,1)} %bitcast.91), calls=%async_computation.1 | async-start | bytes 4718592 | tf_op jit(solution)/shard_map/all_to_all | solution.py:267
  44.8 19.4 %collective-permute-start = (bf16[128,768]{1,0:T(8,128)(2,1)S(1)}, bf16[128,768]{1,0:T(8,128)(2,1)S(1)}, u32[]{:S(2)}, u32[]{:S(2)}) collective-permute-start(bf16[128,768]{1,0:T(8,128)(2,1)S(1)} %bitcast.78), channel_id=1, source_target_pairs={{0,8},{8,0},{16,24},{24,16},{1,9},{9,1},{17,25},{25,17},{2,10},{10... | collective-permute-start | bytes 589832 | tf_op jit(solution)/shard_map/ppermute | solution.py:248
  44.8 19.3 %collective-permute-start.1 = (bf16[128,768]{1,0:T(8,128)(2,1)S(1)}, bf16[128,768]{1,0:T(8,128)(2,1)S(1)}, u32[]{:S(2)}, u32[]{:S(2)}) collective-permute-start(bf16[128,768]{1,0:T(8,128)(2,1)S(1)} %bitcast.79), channel_id=1, source_target_pairs={{0,16},{8,24},{16,0},{24,8},{1,17},{9,25},{17,1},{25,9},{2,18},{10... | collective-permute-start | bytes 589832 | tf_op jit(solution)/shard_map/ppermute | solution.py:248
  47.7 16.5 %collective-permute-start.2 = (bf16[128,768]{1,0:T(8,128)(2,1)S(1)}, bf16[128,768]{1,0:T(8,128)(2,1)S(1)}, u32[]{:S(2)}, u32[]{:S(2)}) collective-permute-start(bf16[128,768]{1,0:T(8,128)(2,1)S(1)} %bitcast.80), channel_id=1, source_target_pairs={{0,24},{8,16},{16,8},{24,0},{1,25},{9,17},{17,9},{25,1},{2,26},{10... | collective-permute-start | bytes 589832 | tf_op jit(solution)/shard_map/ppermute | solution.py:248
  49.2 14.9 %collective-permute-start.6 = (bf16[128,768]{1,0:T(8,128)(2,1)S(1)}, bf16[128,768]{1,0:T(8,128)(2,1)S(1)}, u32[]{:S(2)}, u32[]{:S(2)}) collective-permute-start(bf16[128,768]{1,0:T(8,128)(2,1)S(1)} %get-tuple-element.18), channel_id=1, source_target_pairs={{0,16},{8,24},{16,0},{24,8},{1,17},{9,25},{17,1},{25,9},{2,18},{10... | collective-permute-start | bytes 589832 | tf_op jit(solution)/shard_map/ppermute | solution.py:248
  49.3 14.9 %collective-permute-start.7 = (bf16[128,768]{1,0:T(8,128)(2,1)S(1)}, bf16[128,768]{1,0:T(8,128)(2,1)S(1)}, u32[]{:S(2)}, u32[]{:S(2)}) collective-permute-start(bf16[128,768]{1,0:T(8,128)(2,1)S(1)} %get-tuple-element.18), channel_id=1, source_target_pairs={{0,24},{8,16},{16,8},{24,0},{1,25},{9,17},{17,9},{25,1},{2,26},{10... | collective-permute-start | bytes 589832 | tf_op jit(solution)/shard_map/ppermute | solution.py:248
  72.5 69.1 %all-to-all-start = ((bf16[8,192,768]{2,1,0:T(8,128)(2,1)}), bf16[8,192,768]{2,1,0:T(8,128)(2,1)}, u32[]{:S(2)}, u32[]{:S(2)}) async-start(bf16[8,192,768]{2,1,0:T(8,128)(2,1)} %bitcast.94), calls=%async_computation | async-start | bytes 4718592 | tf_op jit(solution)/shard_map/all_to_all | solution.py:267
  156.6 33.1 %all-to-all-start.3 = ((bf16[8,192,768]{2,1,0:T(8,128)(2,1)}), bf16[8,192,768]{2,1,0:T(8,128)(2,1)S(1)}, u32[]{:S(2)}, u32[]{:S(2)}) async-start(bf16[8,192,768]{2,1,0:T(8,128)(2,1)} %bitcast.92), calls=%async_computation.3 | async-start | bytes 4718592 | tf_op jit(solution)/shard_map/all_to_all | solution.py:267
  214.7 38.2 %all-to-all-start.2 = ((bf16[8,192,768]{2,1,0:T(8,128)(2,1)}), bf16[8,192,768]{2,1,0:T(8,128)(2,1)}, u32[]{:S(2)}, u32[]{:S(2)}) async-start(bf16[8,192,768]{2,1,0:T(8,128)(2,1)} %bitcast.90), calls=%async_computation.2 | async-start | bytes 4718592 | tf_op jit(solution)/shard_map/all_to_all | solution.py:267
  221.9 13.0 %collective-permute-start.17 = (bf16[128,768]{1,0:T(8,128)(2,1)S(1)}, bf16[128,768]{1,0:T(8,128)(2,1)S(1)}, u32[]{:S(2)}, u32[]{:S(2)}) collective-permute-start(bf16[128,768]{1,0:T(8,128)(2,1)S(1)} %get-tuple-element.31), channel_id=1, source_target_pairs={{0,8},{8,0},{16,24},{24,16},{1,9},{9,1},{17,25},{25,17},{2,10},{10... | collective-permute-start | bytes 589832 | tf_op jit(solution)/shard_map/ppermute | solution.py:253
  225.9 17.1 %collective-permute-start.18 = (bf16[128,768]{1,0:T(8,128)(2,1)S(1)}, bf16[128,768]{1,0:T(8,128)(2,1)S(1)}, u32[]{:S(2)}, u32[]{:S(2)}) collective-permute-start(bf16[128,768]{1,0:T(8,128)(2,1)S(1)} %get-tuple-element.30), channel_id=1, source_target_pairs={{0,16},{8,24},{16,0},{24,8},{1,17},{9,25},{17,1},{25,9},{2,18},{10... | collective-permute-start | bytes 589832 | tf_op jit(solution)/shard_map/ppermute | solution.py:253
  226.9 16.1 %collective-permute-start.19 = (bf16[128,768]{1,0:T(8,128)(2,1)S(1)}, bf16[128,768]{1,0:T(8,128)(2,1)S(1)}, u32[]{:S(2)}, u32[]{:S(2)}) collective-permute-start(bf16[128,768]{1,0:T(8,128)(2,1)S(1)} %get-tuple-element.29), channel_id=1, source_target_pairs={{0,24},{8,16},{16,8},{24,0},{1,25},{9,17},{17,9},{25,1},{2,26},{10... | collective-permute-start | bytes 589832 | tf_op jit(solution)/shard_map/ppermute | solution.py:253
  246.4 16.9 %collective-permute-start.25 = (bf16[112,768]{1,0:T(8,128)(2,1)S(1)}, bf16[112,768]{1,0:T(8,128)(2,1)S(1)}, u32[]{:S(2)}, u32[]{:S(2)}) collective-permute-start(bf16[112,768]{1,0:T(8,128)(2,1)S(1)} %reduce_sum.35), channel_id=1, source_target_pairs={{0,8},{8,0},{16,24},{24,16},{1,9},{9,1},{17,25},{25,17},{2,10},{10... | collective-permute-start | bytes 516104 | tf_op jit(solution)/shard_map/ppermute | solution.py:248
  250.4 15.5 %collective-permute-start.26 = (bf16[112,768]{1,0:T(8,128)(2,1)S(1)}, bf16[112,768]{1,0:T(8,128)(2,1)S(1)}, u32[]{:S(2)}, u32[]{:S(2)}) collective-permute-start(bf16[112,768]{1,0:T(8,128)(2,1)S(1)} %reduce_sum.35), channel_id=1, source_target_pairs={{0,16},{8,24},{16,0},{24,8},{1,17},{9,25},{17,1},{25,9},{2,18},{10... | collective-permute-start | bytes 516104 | tf_op jit(solution)/shard_map/ppermute | solution.py:248
  251.4 14.5 %collective-permute-start.27 = (bf16[112,768]{1,0:T(8,128)(2,1)S(1)}, bf16[112,768]{1,0:T(8,128)(2,1)S(1)}, u32[]{:S(2)}, u32[]{:S(2)}) collective-permute-start(bf16[112,768]{1,0:T(8,128)(2,1)S(1)} %reduce_sum.35), channel_id=1, source_target_pairs={{0,24},{8,16},{16,8},{24,0},{1,25},{9,17},{17,9},{25,1},{2,26},{10... | collective-permute-start | bytes 516104 | tf_op jit(solution)/shard_map/ppermute | solution.py:248
  253.6 12.4 %all-to-all-start.4 = ((bf16[8,32,768]{2,1,0:T(8,128)(2,1)}), bf16[8,32,768]{2,1,0:T(8,128)(2,1)S(1)}, u32[]{:S(2)}, u32[]{:S(2)}) async-start(bf16[8,32,768]{2,1,0:T(8,128)(2,1)} %broadcast_in_dim.84), calls=%async_computation.4 | async-start | bytes 786432 | tf_op jit(solution)/shard_map/all_to_all | solution.py:267
  267.2 36.1 %all-to-all-start.6 = ((bf16[8,112,768]{2,1,0:T(8,128)(2,1)}), bf16[8,112,768]{2,1,0:T(8,128)(2,1)S(1)}, u32[]{:S(2)}, u32[]{:S(2)}) async-start(bf16[8,112,768]{2,1,0:T(8,128)(2,1)} %broadcast_in_dim.90), calls=%async_computation.6 | async-start | bytes 2752512 | tf_op jit(solution)/shard_map/all_to_all | solution.py:267
  277.4 17.5 %collective-permute-start.15 = (bf16[128,768]{1,0:T(8,128)(2,1)}, bf16[128,768]{1,0:T(8,128)(2,1)}, u32[]{:S(2)}, u32[]{:S(2)}) collective-permute-start(bf16[128,768]{1,0:T(8,128)(2,1)} %get-tuple-element.35), channel_id=1, source_target_pairs={{0,16},{8,24},{16,0},{24,8},{1,17},{9,25},{17,1},{25,9},{2,18},{10... | collective-permute-start | bytes 589832 | tf_op jit(solution)/shard_map/ppermute | solution.py:253
  278.3 16.6 %collective-permute-start.16 = (bf16[128,768]{1,0:T(8,128)(2,1)}, bf16[128,768]{1,0:T(8,128)(2,1)}, u32[]{:S(2)}, u32[]{:S(2)}) collective-permute-start(bf16[128,768]{1,0:T(8,128)(2,1)} %get-tuple-element.34), channel_id=1, source_target_pairs={{0,24},{8,16},{16,8},{24,0},{1,25},{9,17},{17,9},{25,1},{2,26},{10... | collective-permute-start | bytes 589832 | tf_op jit(solution)/shard_map/ppermute | solution.py:253
  279.8 20.0 %collective-permute-start.20 = (bf16[16,768]{1,0:T(8,128)(2,1)S(1)}, bf16[16,768]{1,0:T(8,128)(2,1)S(1)}, u32[]{:S(2)}, u32[]{:S(2)}) collective-permute-start(bf16[16,768]{1,0:T(8,128)(2,1)S(1)} %get-tuple-element.37), channel_id=1, source_target_pairs={{0,1},{1,2},{2,3},{3,4},{4,5},{5,6},{6,7},{8,9},{9,10},{10,11},{11... | collective-permute-start | bytes 73736 | tf_op jit(solution)/shard_map/ppermute | solution.py:261
  281.6 18.2 %collective-permute-start.21 = (bf16[16,768]{1,0:T(8,128)(2,1)S(1)}, bf16[16,768]{1,0:T(8,128)(2,1)S(1)}, u32[]{:S(2)}, u32[]{:S(2)}) collective-permute-start(bf16[16,768]{1,0:T(8,128)(2,1)S(1)} %get-tuple-element.36), channel_id=1, source_target_pairs={{1,0},{2,1},{3,2},{4,3},{5,4},{6,5},{7,6},{9,8},{10,9},{11,10},{12... | collective-permute-start | bytes 73736 | tf_op jit(solution)/shard_map/ppermute | solution.py:262
  287.0 15.5 %collective-permute-start.22 = (bf16[32,768]{1,0:T(8,128)(2,1)S(1)}, bf16[32,768]{1,0:T(8,128)(2,1)S(1)}, u32[]{:S(2)}, u32[]{:S(2)}) collective-permute-start(bf16[32,768]{1,0:T(8,128)(2,1)S(1)} %reduce_sum.34), channel_id=1, source_target_pairs={{0,8},{8,0},{16,24},{24,16},{1,9},{9,1},{17,25},{25,17},{2,10},{10... | collective-permute-start | bytes 147464 | tf_op jit(solution)/shard_map/ppermute | solution.py:248
  (38 other events, 644.9 us)

commit v2 on v1

v2 whole, which is shorter than its diff:
```python
import jax
import jax.numpy as jnp
from jax import lax
from jax.experimental import pallas as pl
from jax.experimental.pallas import tpu as pltpu
from jax.sharding import PartitionSpec as P

F32 = jnp.float32
BF16 = jnp.bfloat16
EDGE = 16
LANES = 128
SUB = 384
PARAMS = pltpu.CompilerParams(vmem_limit_bytes=56 << 20)


def shape(dims, dtype):
    return jax.ShapeDtypeStruct(dims, dtype)


def dot(a, b):
    return jnp.dot(a, b, preferred_element_type=F32)


def dot_rows(a, b):
    return lax.dot_general(a, b, (((0,), (0,)), ((), ())), preferred_element_type=F32)


def sigmoid(value):
    return 1.0 / (1.0 + jnp.exp(-value))


def fill_padded(scratch, before, own, after):
    rows = own.shape[0]
    scratch[0:EDGE, :] = before[...].astype(F32)
    scratch[EDGE : EDGE + rows, :] = own[...].astype(F32)
    scratch[EDGE + rows : 2 * EDGE + rows, :] = after[...].astype(F32)


def conv_forward_kernel(
    before, own, after, seg, weight, point, ids, conv_out, act_out, packet, scratch
):
    rows, width = own.shape
    taps = weight.shape[0]
    shift = EDGE - (taps - 1) // 2
    fill_padded(scratch, before, own, after)

    def column(index, carry):
        lanes = pl.ds(pl.multiple_of(index * LANES, LANES), LANES)
        seg_own = seg[EDGE : EDGE + rows, :]
        total = jnp.zeros((rows, LANES), F32)
        for tap in range(taps):
            first = tap + shift
            same = seg[first : first + rows, :] == seg_own
            piece = jnp.where(same, scratch[first : first + rows, lanes], 0.0)
            total = total + weight[tap : tap + 1, lanes] * piece
        conv_out[:, lanes] = total
        act_out[:, lanes] = (total * sigmoid(total)).astype(BF16)
        return carry

    lax.fori_loop(0, width // LANES, column, 0)
    packet[:rows, :] = (own[...].astype(F32) + dot(act_out[...], point[...])).astype(BF16)
    packet[rows:, :] = ids[...]


def conv_forward(before, own, after, seg, weight, point, ids):
    rows, width = own.shape
    return pl.pallas_call(
        conv_forward_kernel,
        out_shape=(
            shape((rows, width), F32),
            shape((rows, width), BF16),
            shape((rows + EDGE, width), BF16),
        ),
        scratch_shapes=[pltpu.VMEM((rows + 2 * EDGE, width), F32)],
        compiler_params=PARAMS,
        name="conv_forward",
    )(before, own, after, seg, weight, point, ids)


def conv_backward_kernel(before, own, after, seg, weight, grad_mixed, out, scratch):
    rows, width = own.shape
    taps = weight.shape[0]
    shift = EDGE - (taps - 1) // 2
    fill_padded(scratch, before, own, after)

    def column(index, carry):
        lanes = pl.ds(pl.multiple_of(index * LANES, LANES), LANES)
        seg_own = seg[EDGE : EDGE + rows, :]
        total = grad_mixed[:, lanes]
        for tap in range(taps):
            first = tap + shift
            same = seg[first : first + rows, :] == seg_own
            piece = jnp.where(same, scratch[first : first + rows, lanes], 0.0)
            total = total + weight[taps - 1 - tap : taps - tap, lanes] * piece
        out[:, lanes] = total.astype(BF16)
        return carry

    lax.fori_loop(0, width // LANES, column, 0)


def conv_backward(before, own, after, seg, weight, grad_mixed):
    rows, width = own.shape
    return pl.pallas_call(
        conv_backward_kernel,
        out_shape=shape((rows, width), BF16),
        scratch_shapes=[pltpu.VMEM((rows + 2 * EDGE, width), F32)],
        compiler_params=PARAMS,
        name="conv_backward",
    )(before, own, after, seg, weight, grad_mixed)


def tail(
    parts, cot, conv, act, point_t, before, own, after, seg, spot, router_part, core, places, taps
):
    rows, width = own.shape
    experts = spot.shape[0]
    shift = EDGE - (taps - 1) // 2
    groups = places // 2
    used = width // places
    lead = -(-used // EDGE) * EDGE
    extra = -(-(taps + 1 + experts) // EDGE)
    count = len(parts)
    pieces = (groups, lead + EDGE, width)

    def kernel(core, *refs):
        parts = refs[:count]
        cot, conv, act, point_t, before, own, after, seg, spot, router_part = refs[
            count : count + 10
        ]
        grad_mixed, grad_conv, mine, theirs, scratch, shared = refs[count + 10 :]
        total = cot[...].astype(F32)
        for part in parts:
            total = total + part[...].astype(F32)
        grad_mixed[...] = total
        low = total.astype(BF16)
        grad_act = dot(low, point_t[...])
        value = conv[...]
        sigma = sigmoid(value)
        grad_conv[...] = (grad_act * (sigma * (1.0 + value * (1.0 - sigma)))).astype(BF16)
        fill_padded(scratch, before, own, after)
        point = dot_rows(act[...], low).astype(BF16)
        for index in range(places):
            side, group = divmod(index, groups)
            shared[side, group] = jnp.zeros(pieces[1:], BF16)
            shared[side, group, 0:used, :] = point[index * used : (index + 1) * used]

        def column(index, carry):
            lanes = pl.ds(pl.multiple_of(index * LANES, LANES), LANES)
            seg_own = seg[EDGE : EDGE + rows, :]
            slope = grad_conv[:, lanes].astype(F32)
            sums = []
            for tap in range(taps):
                first = tap + shift
                same = seg[first : first + rows, :] == seg_own
                piece = jnp.where(same, scratch[first : first + rows, lanes], 0.0)
                sums.append(jnp.sum(slope * piece, axis=0, keepdims=True))
            sums.append(jnp.zeros((1, LANES), F32))
            sums.append(spot[...] * router_part[0:1, lanes])
            missing = extra * EDGE - (taps + 1 + experts)
            if missing:
                sums.append(jnp.zeros((missing, LANES), F32))
            small = jnp.concatenate(sums, axis=0).astype(BF16)
            for index in range(extra):
                side, group = divmod(index, groups)
                shared[side, group, lead : lead + EDGE, lanes] = small[
                    index * EDGE : (index + 1) * EDGE
                ]
            return carry

        lax.fori_loop(0, width // LANES, column, 0)
        mine[...] = shared[core[0]]
        theirs[...] = shared[1 - core[0]]

    return pl.pallas_call(
        kernel,
        in_specs=[pl.BlockSpec(memory_space=pltpu.SMEM)]
        + [pl.BlockSpec(memory_space=pltpu.VMEM)] * (count + 10),
        out_shape=(
            shape((rows, width), F32),
            shape((rows, width), BF16),
            shape(pieces, BF16),
            shape(pieces, BF16),
        ),
        scratch_shapes=[
            pltpu.VMEM((rows + 2 * EDGE, width), F32),
            pltpu.VMEM((2,) + pieces, BF16),
        ],
        compiler_params=PARAMS,
        name="tail",
    )(core, *parts, cot, conv, act, point_t, before, own, after, seg, spot, router_part)


def table_of(ids, experts, capacity):
    rows = ids.shape[1]
    ids = ids[0:2, :].astype(F32)
    expert = lax.broadcasted_iota(jnp.int32, (experts, rows), 0).astype(F32)
    named = [jnp.where(expert == ids[j : j + 1, :], 1.0, 0.0) for j in range(2)]
    earlier = lax.broadcasted_iota(jnp.int32, (rows, rows), 0)
    earlier = earlier < lax.broadcasted_iota(jnp.int32, (rows, rows), 1)
    counts = dot((named[0] + named[1]).astype(BF16), jnp.where(earlier, 1.0, 0.0).astype(BF16))
    row = lax.broadcasted_iota(jnp.int32, (experts * capacity, rows), 0).astype(F32)
    table = jnp.zeros((experts * capacity, rows), F32)
    for j in range(2):
        slot = jnp.sum(named[j] * counts, axis=0, keepdims=True)
        table = jnp.where(row == ids[j : j + 1, :] * capacity + slot, 1.0, table)
    return table.astype(BF16)


def place_all(packets, experts, capacity, pack_here):
    count = len(packets)
    rows, width = packets[0].shape[0] - EDGE, packets[0].shape[1]
    per_expert = count * capacity

    def kernel(pack_here, *refs):
        packets, out, tables = refs[:count], refs[count], refs[count + 1]
        for k, packet in enumerate(packets):
            table = table_of(packet[rows:, :rows], experts, capacity)
            tables[k] = table
            placed = dot(table, packet[:rows, :]).astype(BF16)
            first = (pack_here[0] ^ k) * capacity
            for expert in range(experts):
                start = pl.multiple_of(expert * per_expert + first, EDGE)
                piece = placed[expert * capacity : (expert + 1) * capacity]
                out[pl.ds(start, capacity), :] = piece

    return pl.pallas_call(
        kernel,
        in_specs=[pl.BlockSpec(memory_space=pltpu.SMEM)]
        + [pl.BlockSpec(memory_space=pltpu.VMEM)] * count,
        out_shape=(
            shape((experts * per_expert, width), BF16),
            shape((count, experts * capacity, rows), BF16),
        ),
        compiler_params=PARAMS,
        name="place_all",
    )(pack_here, *packets)


def place_more(tables, arrays, experts, capacity, pack_here):
    count, _, rows = tables.shape
    width = arrays[0].shape[1]
    per_expert = count * capacity

    def kernel(pack_here, tables, *refs):
        out = refs[count]
        for k, array in enumerate(refs[:count]):
            placed = dot(tables[k], array[...]).astype(BF16)
            first = (pack_here[0] ^ k) * capacity
            for expert in range(experts):
                start = pl.multiple_of(expert * per_expert + first, EDGE)
                piece = placed[expert * capacity : (expert + 1) * capacity]
                out[pl.ds(start, capacity), :] = piece

    return pl.pallas_call(
        kernel,
        in_specs=[pl.BlockSpec(memory_space=pltpu.SMEM)]
        + [pl.BlockSpec(memory_space=pltpu.VMEM)] * (count + 1),
        out_shape=shape((experts * per_expert, width), BF16),
        compiler_params=PARAMS,
        name="place_more",
    )(pack_here, tables, *arrays)


def finish(tables, buffer, packet):
    rows = tables.shape[2]
    width = buffer.shape[1]

    def kernel(tables, buffer, packet, out):
        summed = dot_rows(tables[0], buffer[...])
        out[...] = (packet[:rows, :].astype(F32) + summed).astype(BF16)

    return pl.pallas_call(
        kernel,
        out_shape=shape((rows, width), BF16),
        compiler_params=PARAMS,
        name="finish",
    )(tables, buffer, packet)


def collect(tables, buffer, experts, capacity, pack_here):
    count, _, rows = tables.shape
    width = buffer.shape[1]
    per_expert = count * capacity

    def kernel(pack_here, tables, buffer, *outs):
        for k, out in enumerate(outs):
            first = (pack_here[0] ^ k) * capacity
            starts = [
                pl.multiple_of(expert * per_expert + first, EDGE) for expert in range(experts)
            ]
            pieces = [buffer[pl.ds(start, capacity), :] for start in starts]
            out[...] = dot_rows(tables[k], jnp.concatenate(pieces, axis=0)).astype(BF16)

    return pl.pallas_call(
        kernel,
        in_specs=[pl.BlockSpec(memory_space=pltpu.SMEM)]
        + [pl.BlockSpec(memory_space=pltpu.VMEM)] * 2,
        out_shape=[shape((rows, width), BF16)] * count,
        compiler_params=PARAMS,
        name="collect",
    )(pack_here, tables, buffer)


def expert_specs(rows, inner):
    places, packs, capacity, width = rows.shape
    group = max(1, SUB // (packs * capacity))
    chunk = group * packs * capacity
    by_place = pl.BlockSpec((group, packs, capacity, width), lambda i: (i, 0, 0, 0))
    by_pack = pl.BlockSpec((packs, group, capacity, width), lambda i: (0, i, 0, 0))

    def flat(columns):
        return pl.BlockSpec((chunk, columns), lambda i: (i, 0))

    def full(dims):
        return pl.BlockSpec(dims, lambda i: (0,) * len(dims))

    return group, chunk, by_place, by_pack, flat, full


def expert_forward(rows, weight_in, weight_out, router_cols):
    places, packs, capacity, width = rows.shape
    inner = weight_in.shape[1]
    total = places * packs * capacity
    group, chunk, by_place, by_pack, flat, full = expert_specs(rows, inner)
    cells = [(place, pack) for place in range(group) for pack in range(packs)]

    def kernel(rows, w_in, w_out, r_cols, gated_out, hidden_out, slope_out, gate_out):
        row = rows[...].reshape(chunk, width)
        gate = sigmoid(dot(row, r_cols[...]))
        gate_out[...] = gate
        pre = dot(row, w_in[...])
        sigma = sigmoid(pre)
        hidden = (pre * sigma).astype(BF16)
        hidden_out[...] = hidden
        slope_out[...] = (sigma * (1.0 + pre * (1.0 - sigma))).astype(BF16)
        gate_wide = jnp.concatenate([gate] * (width // LANES), axis=1)
        gated = (gate_wide * dot(hidden, w_out[...])).astype(BF16)
        for index, (place, pack) in enumerate(cells):
            gated_out[pack, place] = gated[index * capacity : (index + 1) * capacity]

    return pl.pallas_call(
        kernel,
        grid=(places // group,),
        in_specs=[by_place, full(weight_in.shape), full(weight_out.shape)]
        + [full(router_cols.shape)],
        out_specs=(by_pack, flat(inner), flat(inner), flat(LANES)),
        out_shape=(
            shape((packs, places, capacity, width), BF16),
            shape((total, inner), BF16),
            shape((total, inner), BF16),
            shape((total, LANES), F32),
        ),
        compiler_params=PARAMS,
        name="expert_forward",
    )(rows, weight_in, weight_out, router_cols)


def expert_backward(rows, cots, gated, slope, gate, weight_in_t, weight_out_t, router_row):
    places, packs, capacity, width = rows.shape
    inner = weight_in_t.shape[0]
    total = places * packs * capacity
    group, chunk, by_place, by_pack, flat, full = expert_specs(rows, inner)
    cells = [(place, pack) for place in range(group) for pack in range(packs)]

    def kernel(
        rows,
        cots,
        gated,
        slope,
        gate,
        w_in_t,
        w_out_t,
        r_row,
        back_out,
        grad_pre_out,
        grad_y_out,
        router_out,
    ):
        row = rows[...].reshape(chunk, width)
        cot = cots[...].reshape(chunk, width).astype(F32)
        gates = gate[...]
        gate_wide = jnp.concatenate([gates] * (width // LANES), axis=1)
        grad_y = (gate_wide * cot).astype(BF16)
        grad_y_out[...] = grad_y
        grad_pre = (dot(grad_y, w_out_t[...]) * slope[...].astype(F32)).astype(BF16)
        grad_pre_out[...] = grad_pre
        out = jnp.concatenate([gated[pack, place] for place, pack in cells], axis=0)
        grad_gate = jnp.sum(cot * out.astype(F32), axis=1, keepdims=True)
        grad_logit = grad_gate * (1.0 - gates)[:, 0:1]
        back = dot(grad_pre, w_in_t[...]) + grad_logit * r_row[0:1, :]
        back_out[...] = back.astype(BF16).reshape(rows.shape)
        partial = jnp.sum(row.astype(F32) * grad_logit, axis=0, keepdims=True)

        @pl.when(pl.program_id(0) == 0)
        def _():
            router_out[...] = jnp.zeros_like(router_out)

        router_out[0:1, :] += partial

    return pl.pallas_call(
        kernel,
        grid=(places // group,),
        in_specs=[by_place, by_place, by_pack, flat(inner), flat(LANES)]
        + [full(weight_in_t.shape), full(weight_out_t.shape), full(router_row.shape)],
        out_specs=(by_place, flat(inner), flat(width), full((8, width))),
        out_shape=(
            shape(rows.shape, BF16),
            shape((total, inner), BF16),
            shape((total, width), BF16),
            shape((8, width), F32),
        ),
        compiler_params=PARAMS,
        name="expert_backward",
    )(rows, cots, gated, slope, gate, weight_in_t, weight_out_t, router_row)


def add_pieces(mine, theirs, group):
    groups, size, width = mine.shape

    def kernel(group, mine, theirs, *outs):
        for index, out in enumerate(outs):
            here = group[0] ^ index
            out[...] = (mine[here].astype(F32) + theirs[here].astype(F32)).astype(BF16)

    return pl.pallas_call(
        kernel,
        in_specs=[pl.BlockSpec(memory_space=pltpu.SMEM)]
        + [pl.BlockSpec(memory_space=pltpu.VMEM)] * 2,
        out_shape=[shape((size, width), BF16)] * groups,
        compiler_params=PARAMS,
        name="add_pieces",
    )(group, mine, theirs)


def spread(own, other, group, core, used):
    count = len(own)
    size, width = own[0].shape

    def kernel(where, *refs):
        point, small = refs[2 * count :]
        for index in range(2 * count):
            side = where[1] if index < count else 1 - where[1]
            place = side * count + (where[0] ^ (index % count))
            piece = refs[index][...].astype(F32)
            point[place] = piece[:used]
            small[place] = piece[size - EDGE :]

    return pl.pallas_call(
        kernel,
        in_specs=[pl.BlockSpec(memory_space=pltpu.SMEM)]
        + [pl.BlockSpec(memory_space=pltpu.VMEM)] * (2 * count),
        out_shape=(
            shape((2 * count, used, width), F32),
            shape((2 * count, EDGE, width), F32),
        ),
        compiler_params=PARAMS,
        name="spread",
    )(jnp.stack([group, core]), *own, *other)


def swap(array, axis, k):
    devices = lax.axis_size(axis)
    return lax.ppermute(array, axis, [(i, i ^ k) for i in range(devices)])


def from_all(array, axis):
    return [array] + [swap(array, axis, k) for k in range(1, lax.axis_size(axis))]


def to_all(arrays, axis):
    return [part if k == 0 else swap(part, axis, k) for k, part in enumerate(arrays)]


def exchange(array, axis):
    return lax.all_to_all(array, axis, split_axis=0, concat_axis=0, tiled=True)


def after_all(array, others):
    return lax.optimization_barrier((array, tuple(others)))[0]


def edges(array, axis):
    devices = lax.axis_size(axis)
    up = [(i, i + 1) for i in range(devices - 1)]
    down = [(j, i) for i, j in up]
    before = lax.ppermute(array[array.shape[0] - EDGE :], axis, up)
    after = lax.ppermute(array[:EDGE], axis, down)
    return before, after


def sum_parts(parts):
    total = parts[0].astype(F32)
    for part in parts[1:]:
        total = total + part.astype(F32)
    return total


def local(
    frames,
    segments,
    conv_weight,
    point_weight,
    router_weight,
    expert_ids,
    expert_in,
    expert_out,
    cotangent,
):
    rows_here, width = frames.shape[1:]
    taps = conv_weight.shape[0]
    experts = router_weight.shape[1]
    capacity = -(-3 * rows_here // experts // EDGE) * EDGE
    packs = lax.axis_size("dp")
    places = lax.axis_size("seq")
    place_here = lax.axis_index("seq")
    pack_here = lax.axis_index("dp")[None]
    own_frames = frames[0]
    own_cot = cotangent[0]
    before, after = edges(own_frames, "seq")

    seg_line = jnp.pad(segments[0], (EDGE, EDGE), constant_values=-1)
    seg_here = lax.dynamic_slice_in_dim(seg_line, place_here * rows_here, rows_here + 2 * EDGE)
    seg = jnp.broadcast_to(seg_here[:, None], (rows_here + 2 * EDGE, LANES))

    ids = jnp.pad(expert_ids[0].T.astype(BF16), ((0, EDGE - 2), (0, width - rows_here)))
    conv, activated, packet = conv_forward(
        before, own_frames, after, seg, conv_weight, point_weight, ids
    )
    packets = from_all(packet, "dp")
    placed, tables = place_all(packets, experts, capacity, pack_here)
    rows = exchange(placed.reshape(places, packs * capacity, width), "seq")
    cots = from_all(after_all(own_cot, packets), "dp")
    cots_placed = place_more(tables, cots, experts, capacity, pack_here)
    cots_placed, rows = lax.optimization_barrier((cots_placed, rows))
    cot_rows = exchange(cots_placed.reshape(places, packs * capacity, width), "seq")

    weight_in = expert_in[0]
    weight_out = expert_out[0]
    router_col = lax.dynamic_slice_in_dim(router_weight, place_here, 1, axis=1)
    router_cols = jnp.broadcast_to(router_col, (width, LANES))
    router_row = jnp.broadcast_to(router_col.astype(F32).reshape(1, width), (8, width))
    rows = rows.reshape(places, packs, capacity, width)
    gated, hidden, slope, gate = expert_forward(rows, weight_in, weight_out, router_cols)
    gated_sum = lax.psum_scatter(
        gated.reshape(packs * places, capacity, width), "dp", scatter_dimension=0, tiled=True
    )
    back, grad_pre, grad_y, router_part = expert_backward(
        rows,
        cot_rows.reshape(rows.shape),
        gated,
        slope,
        gate,
        weight_in.T,
        weight_out.T,
        router_row,
    )
    back_home = exchange(back.reshape(places, packs * capacity, width), "seq")
    grad_wout = dot_rows(hidden, grad_y)
    grad_win = dot_rows(rows.reshape(-1, width), grad_pre)
    back_home, (grad_wout, grad_win) = lax.optimization_barrier(
        (back_home, (grad_wout, grad_win))
    )
    back_parts = collect(tables, back_home.reshape(-1, width), experts, capacity, pack_here)
    back_own = to_all(back_parts, "dp")
    gated_home = exchange(after_all(gated_sum, (back_home,)), "seq").reshape(-1, width)
    block_out = finish(tables, gated_home, packet)

    core = place_here % 2
    group = place_here // 2
    groups = places // 2
    spot = jnp.broadcast_to(
        (jnp.arange(experts, dtype=jnp.int32) == place_here).astype(F32)[:, None],
        (experts, LANES),
    )
    grad_mixed, grad_conv, mine, theirs = tail(
        back_own,
        own_cot,
        conv,
        activated,
        point_weight.T,
        before,
        own_frames,
        after,
        seg,
        spot,
        router_part,
        core[None],
        places,
        taps,
    )
    pieces = add_pieces(mine, swap(theirs, "seq", 1), group[None])
    pieces = [pieces[0]] + [swap(pieces[m], "seq", 2 * m) for m in range(1, groups)]
    share = sum_parts(pieces).astype(BF16)
    grad_before, grad_after = edges(grad_conv, "seq")
    frames_grad = conv_backward(grad_before, grad_conv, grad_after, seg, conv_weight, grad_mixed)
    share, frames_grad, block_out = lax.optimization_barrier((share, frames_grad, block_out))
    share = sum_parts(from_all(share, "dp")).astype(BF16)
    own_half = [share] + [swap(share, "seq", 2 * m) for m in range(1, groups)]
    other_half = [swap(part, "seq", 1) for part in own_half]
    point_grad, small = spread(own_half, other_half, group, core, width // places)
    point_grad = point_grad.reshape(width, width)
    small = small.reshape(-1, width)
    conv_grad = small[:taps]
    router_grad = small[taps + 1 : taps + 1 + experts].T

    return (
        block_out[None],
        frames_grad[None],
        conv_grad,
        router_grad,
        point_grad,
        grad_win[None],
        grad_wout[None],
    )


def solution(mesh):
    placed = (
        P("dp", "seq", None),
        P("dp", None),
        P(),
        P(),
        P(),
        P("dp", "seq", None),
        P("seq", None, "dp"),
        P("seq", "dp", None),
        P("dp", "seq", None),
    )
    return jax.shard_map(
        local,
        mesh=mesh,
        in_specs=placed,
        out_specs=(
            P("dp", "seq", None),
            P("dp", "seq", None),
            P(),
            P(),
            P(),
            P("seq", None, "dp"),
            P("seq", "dp", None),
        ),
        check_vma=False,
    )
```

time: 309 us -> 264 us (0.85)
  starting transfers between devices: 106 us -> 63.8 us
  Pallas kernels: 21 us -> 52.3 us
  blocking collectives: 21.3 us -> 0 us
  matrix products: 26.6 us -> 8.83 us
  between operations: 1.18 us -> 14.3 us
  waiting for transfers between devices: 107 us -> 99.4 us
    all_to_all x6 -> x4, starting transfers between devices: 59.1 us -> 21.7 us  [exchange(): return lax.all_to_all(array, axis, split_axis=0, concat_axis=0, tiled=True)]
    pallas_call x4 -> x11, Pallas kernels: 21 us -> 52.3 us  [the longest x1 10.2 us: expert_backward(): pl.pallas_call(kernel, grid=(places // group,), in_specs=[by_place, by_pl...]
    all_to_all x1 -> x0, blocking collectives: 21.3 us -> none  [exchange(): return lax.all_to_all(array, axis, split_axis=0, concat_axis=0, tiled=True)]
    dot_general x9 -> x2, matrix products: 26.6 us -> 8.83 us  [dot_rows(): lax.dot_general(a, b, (((0,), (0,)), ((), ())), preferred_element_type=F32)]
    all_to_all x6 -> x4, waiting for transfers between devices: 55.3 us -> 39.1 us  [exchange(): return lax.all_to_all(array, axis, split_axis=0, concat_axis=0, tiled=True)]
    ppermute x24 -> x23, waiting for transfers between devices: 48.6 us -> 54.9 us  [swap(): return lax.ppermute(array, axis, [(i, i ^ k) for i in range(devices)])]
    ppermute x24 -> x23, starting transfers between devices: 40.1 us -> 35.3 us  [swap(): return lax.ppermute(array, axis, [(i, i ^ k) for i in range(devices)])]
    unnamed x62 -> x67, local copies, waits for them, and re-layouts: 10.2 us -> 11.8 us
  transfers between devices with their start and end apart: 34 -> 32, of which waited for: 12 -> 20; matrix products, arithmetic and copies ran while one was open for 11% -> 8% of each run, Pallas kernels for 3% -> 15%
where the time goes in v2:
time: 264 us; the launch traced here: 262 us
  waiting for transfers between devices  99.4 us (38%)
  starting transfers between devices  63.8 us (24%)
  Pallas kernels  52.3 us (20%)
  local copies, waits for them, and re-layouts  20.5 us (8%)
  between operations  14.3 us (5%)
  matrix products  8.83 us (3%)
    ppermute x23, waiting for transfers between devices, swap(): return lax.ppermute(array, axis, [(i, i ^ k) for i in range(devices)])  54.9 us
    all_to_all x4, waiting for transfers between devices, exchange(): return lax.all_to_all(array, axis, split_axis=0, concat_axis=0, tiled=True)  39.1 us
    ppermute x23, starting transfers between devices, swap(): return lax.ppermute(array, axis, [(i, i ^ k) for i in range(devices)])  35.3 us
    all_to_all x4, starting transfers between devices, exchange(): return lax.all_to_all(array, axis, split_axis=0, concat_axis=0, tiled=True)  21.7 us
    unnamed x67, local copies, waits for them, and re-layouts  11.8 us
    pallas_call x1, Pallas kernels, expert_backward(): pl.pallas_call(kernel, grid=(places // group,), in_specs=[by_place, by_pl...  10.2 us
    pallas_call x1, Pallas kernels, expert_forward(): pl.pallas_call(kernel, grid=(places // group,), in_specs=[by_place, full(...  9.58 us
    dot_general x2, matrix products, dot_rows(): lax.dot_general(a, b, (((0,), (0,)), ((), ())), preferred_element_type=F32)  8.83 us
  transfers between devices with their start and end apart: 32, of which 20 were waited for; matrix products, arithmetic and copies ran while one was open for 8% of the time, Pallas kernels for 15%

profile of v2, /device:TPU:0, one launch (start us, length us, event | category | flops | bytes accessed | tf_op | source)
XLA Modules:
  0.0 261.5 jit_solution(5388019034372878128)
XLA Ops:
  16.2 4.6 %conv_forward.1 = (f32[128,768]{1,0:T(8,128)}, bf16[128,768]{1,0:T(8,128)(2,1)}, bf16[144,768]{1,0:T(8,128)(2,1)}) custom-call(bf16[16,768]{1,0:T(8,128)(2,1)} %copy-done.28, bf16[128,768]{1,0:T(8,128)(2,1)} %bitcast.59, bf16[16,768]{1,0:T(8,128)(2,1)} %copy-done.29, s32[160,128]{1,0:T(8,128)} %broadcast_in_dim.51.seg.refs_11_, f32[31,768]{1,0:T(8,128)} %weight.3, ...), custom_call_target="tpu_custom_call" | custom-call | tf_op jit(solution)/shard_map/conv_forward/pallas_call | solution.py:67
  25.2 5.6 %collective-permute-done.2.refs_1_ = bf16[144,768]{1,0:T(8,128)(2,1)S(1)} collective-permute-done((bf16[144,768]{1,0:T(8,128)(2,1)}, bf16[144,768]{1,0:T(8,128)(2,1)S(1)}, u32[]{:S(2)}, u32[]{:S(2)}) %collective-permute-start.2) | collective-permute-done | bytes 221216 | tf_op jit(solution)/shard_map/ppermute | solution.py:463
  31.7 7.6 %collective-permute-done.4.refs_3_ = bf16[144,768]{1,0:T(8,128)(2,1)S(1)} collective-permute-done((bf16[144,768]{1,0:T(8,128)(2,1)}, bf16[144,768]{1,0:T(8,128)(2,1)S(1)}, u32[]{:S(2)}, u32[]{:S(2)}) %collective-permute-start.4) | collective-permute-done | bytes 221216 | tf_op jit(solution)/shard_map/ppermute | solution.py:463
  40.0 3.9 %place_all.1 = (bf16[1536,768]{1,0:T(8,128)(2,1)}, bf16[4,384,128]{2,1,0:T(8,128)(2,1)}) custom-call(s32[1]{0:T(128)} %bitcast.2.pack_here, bf16[144,768]{1,0:T(8,128)(2,1)} %get-tuple-element.44.refs_0_.packet, bf16[144,768]{1,0:T(8,128)(2,1)} %copy-done.12, bf16[144,768]{1,0:T(8,128)(2,1)} %copy-done.13, bf16[144,768]{1,0:T(8,128)(2,1)} %copy-done.14), custom_call_target="tpu_custom_call" | custom-call | tf_op jit(solution)/shard_map/place_all/pallas_call | solution.py:226
  43.9 7.5 %all-to-all-start = ((bf16[8,192,768]{2,1,0:T(8,128)(2,1)}), bf16[8,192,768]{2,1,0:T(8,128)(2,1)S(1)}, u32[]{:S(2)}, u32[]{:S(2)}) async-start(bf16[8,192,768]{2,1,0:T(8,128)(2,1)} %bitcast.56), calls=%async_computation | async-start | bytes 4718592 | tf_op jit(solution)/shard_map/all_to_all | solution.py:475
  51.4 4.2 %collective-permute-start.5 = (bf16[128,768]{1,0:T(8,128)(2,1)S(1)}, bf16[128,768]{1,0:T(8,128)(2,1)S(1)}, u32[]{:S(2)}, u32[]{:S(2)}) collective-permute-start(bf16[128,768]{1,0:T(8,128)(2,1)S(1)} %bitcast.63), channel_id=1, source_target_pairs={{0,8},{8,0},{16,24},{24,16},{1,9},{9,1},{17,25},{25,17},{2,10},{10... | collective-permute-start | bytes 589832 | tf_op jit(solution)/shard_map/ppermute | solution.py:463
  58.0 6.8 %collective-permute-done.5.refs_1_ = bf16[128,768]{1,0:T(8,128)(2,1)S(1)} collective-permute-done((bf16[128,768]{1,0:T(8,128)(2,1)S(1)}, bf16[128,768]{1,0:T(8,128)(2,1)S(1)}, u32[]{:S(2)}, u32[]{:S(2)}) %collective-permute-start.5) | collective-permute-done | bytes 196640 | tf_op jit(solution)/shard_map/ppermute | solution.py:463
  64.8 7.9 %collective-permute-done.6.refs_2_ = bf16[128,768]{1,0:T(8,128)(2,1)S(1)} collective-permute-done((bf16[128,768]{1,0:T(8,128)(2,1)S(1)}, bf16[128,768]{1,0:T(8,128)(2,1)S(1)}, u32[]{:S(2)}, u32[]{:S(2)}) %collective-permute-start.6) | collective-permute-done | bytes 196640 | tf_op jit(solution)/shard_map/ppermute | solution.py:463
  76.9 3.9 %all-to-all-done = bf16[8,192,768]{2,1,0:T(8,128)(2,1)S(1)} async-done(((bf16[8,192,768]{2,1,0:T(8,128)(2,1)}), bf16[8,192,768]{2,1,0:T(8,128)(2,1)S(1)}, u32[]{:S(2)}, u32[]{:S(2)}) %all-to-all-start) | async-done | bytes 2359328 | tf_op jit(solution)/shard_map/all_to_all | solution.py:475
  82.2 4.4 %all-to-all-start.1 = ((bf16[8,192,768]{2,1,0:T(8,128)(2,1)}), bf16[8,192,768]{2,1,0:T(8,128)(2,1)}, u32[]{:S(2)}, u32[]{:S(2)}) async-start(bf16[8,192,768]{2,1,0:T(8,128)(2,1)} %bitcast.47), calls=%async_computation.1 | async-start | bytes 4718592 | tf_op jit(solution)/shard_map/all_to_all | solution.py:475
  87.6 9.6 %expert_forward.1 = (bf16[4,8,48,768]{3,2,1,0:T(8,128)(2,1)}, bf16[1536,768]{1,0:T(8,128)(2,1)}, bf16[1536,768]{1,0:T(8,128)(2,1)}, f32[1536,128]{1,0:T(8,128)}) custom-call(bf16[8,4,48,768]{3,2,1,0:T(8,128)(2,1)} %bitcast.44, bf16[768,768]{1,0:T(8,128)(2,1)} %bitcast.50, bf16[768,768]{1,0:T(8,128)(2,1)} %bitcast.51, bf16[768,128]{1,0:T(8,128)(2,1)} %broadcast_in_dim.53.r_cols), custom_call_target="tpu_custom_call" | custom-call | tf_op jit(solution)/shard_map/expert_forward/pallas_call | solution.py:341
  101.3 14.8 %all-to-all-done.1 = bf16[8,192,768]{2,1,0:T(8,128)(2,1)} async-done(((bf16[8,192,768]{2,1,0:T(8,128)(2,1)}), bf16[8,192,768]{2,1,0:T(8,128)(2,1)}, u32[]{:S(2)}, u32[]{:S(2)}) %all-to-all-start.1) | async-done | bytes 2359328 | tf_op jit(solution)/shard_map/all_to_all | solution.py:475
  116.7 10.2 %expert_backward.1 = (bf16[8,4,48,768]{3,2,1,0:T(8,128)(2,1)}, bf16[1536,768]{1,0:T(8,128)(2,1)}, bf16[1536,768]{1,0:T(8,128)(2,1)}, f32[8,768]{1,0:T(8,128)}) custom-call(bf16[8,4,48,768]{3,2,1,0:T(8,128)(2,1)} %bitcast.45, bf16[8,4,48,768]{3,2,1,0:T(8,128)(2,1)} %bitcast.13.cots, bf16[4,8,48,768]{3,2,1,0:T(8,128)(2,1)} %get-tuple-element.50.gated, ...), custom_call_target="tpu_custom_call" | custom-call | tf_op jit(solution)/shard_map/expert_backward/pallas_call | solution.py:400
  126.9 4.7 %all-to-all-start.2 = ((bf16[8,192,768]{2,1,0:T(8,128)(2,1)}), bf16[8,192,768]{2,1,0:T(8,128)(2,1)}, u32[]{:S(2)}, u32[]{:S(2)}) async-start(bf16[8,192,768]{2,1,0:T(8,128)(2,1)} %bitcast.57), calls=%async_computation.2 | async-start | bytes 4718592 | tf_op jit(solution)/shard_map/all_to_all | solution.py:475
  131.6 5.3 %fusion.2 = f32[768,768]{1,0:T(8,128)} fusion(bf16[1536,768]{1,0:T(8,128)(2,1)S(1)} %bitcast.46, bf16[1536,768]{1,0:T(8,128)(2,1)} %get-tuple-element.56), kind=kOutput, calls=%fused_computation.12 | convolution fusion | flops 1811939328 | bytes 7077888 | tf_op jit(solution)/shard_map/dot_general | solution.py:25
  140.5 20.4 %all-to-all-done.2 = bf16[8,192,768]{2,1,0:T(8,128)(2,1)} async-done(((bf16[8,192,768]{2,1,0:T(8,128)(2,1)}), bf16[8,192,768]{2,1,0:T(8,128)(2,1)}, u32[]{:S(2)}, u32[]{:S(2)}) %all-to-all-start.2) | async-done | bytes 2359328 | tf_op jit(solution)/shard_map/all_to_all | solution.py:475
  175.1 7.2 %collective-permute-done.9.refs_2_ = bf16[128,768]{1,0:T(8,128)(2,1)S(1)} collective-permute-done((bf16[128,768]{1,0:T(8,128)(2,1)}, bf16[128,768]{1,0:T(8,128)(2,1)S(1)}, u32[]{:S(2)}, u32[]{:S(2)}) %collective-permute-start.9) | collective-permute-done | bytes 196640 | tf_op jit(solution)/shard_map/ppermute | solution.py:463
  182.9 5.9 %tail.1 = (f32[128,768]{1,0:T(8,128)}, bf16[128,768]{1,0:T(8,128)(2,1)}, bf16[4,112,768]{2,1,0:T(8,128)(2,1)}, bf16[4,112,768]{2,1,0:T(8,128)(2,1)}) custom-call(s32[1]{0:T(128)} %bitcast.1.core, bf16[128,768]{1,0:T(8,128)(2,1)} %get-tuple-element.58.refs_0_, bf16[128,768]{1,0:T(8,128)(2,1)} %copy-done.16, bf16[128,768]{1,0:T(8,128)(2,1)} %copy-done.17, ...), custom_call_target="tpu_custom_call" | custom-call | tf_op jit(solution)/shard_map/tail/pallas_call | solution.py:174
  188.8 5.2 %all-to-all-start.3 = ((bf16[8,48,768]{2,1,0:T(8,128)(2,1)}), bf16[8,48,768]{2,1,0:T(8,128)(2,1)S(1)}, u32[]{:S(2)}, u32[]{:S(2)}) async-start(bf16[8,48,768]{2,1,0:T(8,128)(2,1)} %reduce-scatter.2.cloned.1.call-done), calls=%async_computation.4 | async-start | bytes 1179648 | tf_op jit(solution)/shard_map/all_to_all | solution.py:475
  204.6 3.5 %collective-permute-done.16.after = bf16[16,768]{1,0:T(8,128)(2,1)S(1)} collective-permute-done((bf16[16,768]{1,0:T(8,128)(2,1)S(1)}, bf16[16,768]{1,0:T(8,128)(2,1)S(1)}, u32[]{:S(2)}, u32[]{:S(2)}) %collective-permute-start.16) | collective-permute-done | bytes 24608 | tf_op jit(solution)/shard_map/ppermute | solution.py:487
  208.7 4.0 %conv_backward.1 = bf16[128,768]{1,0:T(8,128)(2,1)} custom-call(bf16[16,768]{1,0:T(8,128)(2,1)} %copy-done.30, bf16[128,768]{1,0:T(8,128)(2,1)} %get-tuple-element.71.own, bf16[16,768]{1,0:T(8,128)(2,1)} %copy-done.31, s32[160,128]{1,0:T(8,128)} %broadcast_in_dim.51.seg.refs_11_, f32[31,768]{1,0:T(8,128)} %weight.3, f32[128,768]{1,0:T(8,128)} %get-tuple-element.72.grad_mixed), custom_call_target="tpu_custom_call" | custom-call | tf_op jit(solution)/shard_map/conv_backward/pallas_call | solution.py:103
  225.4 3.5 %collective-permute-done.19 = bf16[112,768]{1,0:T(8,128)(2,1)S(1)} collective-permute-done((bf16[112,768]{1,0:T(8,128)(2,1)S(1)}, bf16[112,768]{1,0:T(8,128)(2,1)S(1)}, u32[]{:S(2)}, u32[]{:S(2)}) %collective-permute-start.19) | collective-permute-done | bytes 172064 | tf_op jit(solution)/shard_map/ppermute | solution.py:463
  229.1 6.7 %collective-permute-start.20 = (bf16[112,768]{1,0:T(8,128)(2,1)S(1)}, bf16[112,768]{1,0:T(8,128)(2,1)S(1)}, u32[]{:S(2)}, u32[]{:S(2)}) collective-permute-start(bf16[112,768]{1,0:T(8,128)(2,1)S(1)} %add_convert_fusion.refs_0_), channel_id=1, source_target_pairs={{0,2},{1,3},{2,0},{3,1},{4,6},{5,7},{6,4},{7,5},{8,10},{9,11},{10,... | collective-permute-start | bytes 516104 | tf_op jit(solution)/shard_map/ppermute | solution.py:463
  241.0 4.9 %collective-permute-done.21.refs_2_ = bf16[112,768]{1,0:T(8,128)(2,1)S(1)} collective-permute-done((bf16[112,768]{1,0:T(8,128)(2,1)S(1)}, bf16[112,768]{1,0:T(8,128)(2,1)S(1)}, u32[]{:S(2)}, u32[]{:S(2)}) %collective-permute-start.21) | collective-permute-done | bytes 172064 | tf_op jit(solution)/shard_map/ppermute | solution.py:463
  (137 shorter events, 85.0 us)
Async XLA Ops:
  20.8 10.0 %collective-permute-start.2 = (bf16[144,768]{1,0:T(8,128)(2,1)}, bf16[144,768]{1,0:T(8,128)(2,1)S(1)}, u32[]{:S(2)}, u32[]{:S(2)}) collective-permute-start(bf16[144,768]{1,0:T(8,128)(2,1)} %get-tuple-element.44.refs_0_.packet), channel_id=1, source_target_pairs={{0,8},{8,0},{16,24},{24,16},{1,9},{9,1},{17,25},{25,17},{2,10},{10... | collective-permute-start | bytes 663560 | tf_op jit(solution)/shard_map/ppermute | solution.py:463
  22.4 9.3 %collective-permute-start.3 = (bf16[144,768]{1,0:T(8,128)(2,1)}, bf16[144,768]{1,0:T(8,128)(2,1)S(1)}, u32[]{:S(2)}, u32[]{:S(2)}) collective-permute-start(bf16[144,768]{1,0:T(8,128)(2,1)} %get-tuple-element.44.refs_0_.packet), channel_id=1, source_target_pairs={{0,16},{8,24},{16,0},{24,8},{1,17},{9,25},{17,1},{25,9},{2,18},{10... | collective-permute-start | bytes 663560 | tf_op jit(solution)/shard_map/ppermute | solution.py:463
  25.0 14.3 %collective-permute-start.4 = (bf16[144,768]{1,0:T(8,128)(2,1)}, bf16[144,768]{1,0:T(8,128)(2,1)S(1)}, u32[]{:S(2)}, u32[]{:S(2)}) collective-permute-start(bf16[144,768]{1,0:T(8,128)(2,1)} %get-tuple-element.44.refs_0_.packet), channel_id=1, source_target_pairs={{0,24},{8,16},{16,8},{24,0},{1,25},{9,17},{17,9},{25,1},{2,26},{10... | collective-permute-start | bytes 663560 | tf_op jit(solution)/shard_map/ppermute | solution.py:463
  43.9 36.9 %all-to-all-start = ((bf16[8,192,768]{2,1,0:T(8,128)(2,1)}), bf16[8,192,768]{2,1,0:T(8,128)(2,1)S(1)}, u32[]{:S(2)}, u32[]{:S(2)}) async-start(bf16[8,192,768]{2,1,0:T(8,128)(2,1)} %bitcast.56), calls=%async_computation | async-start | bytes 4718592 | tf_op jit(solution)/shard_map/all_to_all | solution.py:475
  51.4 13.5 %collective-permute-start.5 = (bf16[128,768]{1,0:T(8,128)(2,1)S(1)}, bf16[128,768]{1,0:T(8,128)(2,1)S(1)}, u32[]{:S(2)}, u32[]{:S(2)}) collective-permute-start(bf16[128,768]{1,0:T(8,128)(2,1)S(1)} %bitcast.63), channel_id=1, source_target_pairs={{0,8},{8,0},{16,24},{24,16},{1,9},{9,1},{17,25},{25,17},{2,10},{10... | collective-permute-start | bytes 589832 | tf_op jit(solution)/shard_map/ppermute | solution.py:463
  55.6 17.1 %collective-permute-start.6 = (bf16[128,768]{1,0:T(8,128)(2,1)S(1)}, bf16[128,768]{1,0:T(8,128)(2,1)S(1)}, u32[]{:S(2)}, u32[]{:S(2)}) collective-permute-start(bf16[128,768]{1,0:T(8,128)(2,1)S(1)} %bitcast.64), channel_id=1, source_target_pairs={{0,16},{8,24},{16,0},{24,8},{1,17},{9,25},{17,1},{25,9},{2,18},{10... | collective-permute-start | bytes 589832 | tf_op jit(solution)/shard_map/ppermute | solution.py:463
  56.7 16.1 %collective-permute-start.7 = (bf16[128,768]{1,0:T(8,128)(2,1)S(1)}, bf16[128,768]{1,0:T(8,128)(2,1)S(1)}, u32[]{:S(2)}, u32[]{:S(2)}) collective-permute-start(bf16[128,768]{1,0:T(8,128)(2,1)S(1)} %bitcast.65), channel_id=1, source_target_pairs={{0,24},{8,16},{16,8},{24,0},{1,25},{9,17},{17,9},{25,1},{2,26},{10... | collective-permute-start | bytes 589832 | tf_op jit(solution)/shard_map/ppermute | solution.py:463
  82.2 33.9 %all-to-all-start.1 = ((bf16[8,192,768]{2,1,0:T(8,128)(2,1)}), bf16[8,192,768]{2,1,0:T(8,128)(2,1)}, u32[]{:S(2)}, u32[]{:S(2)}) async-start(bf16[8,192,768]{2,1,0:T(8,128)(2,1)} %bitcast.47), calls=%async_computation.1 | async-start | bytes 4718592 | tf_op jit(solution)/shard_map/all_to_all | solution.py:475
  86.6 102.2 %reduce-scatter.2.cloned.1.call-start = ((), (), s32[]{:S(2)}) async-start(), calls=%async_computation.5 | async-start | bytes 2949120 | tf_op jit(solution)/shard_map/reduce_scatter | solution.py:544
  126.9 34.0 %all-to-all-start.2 = ((bf16[8,192,768]{2,1,0:T(8,128)(2,1)}), bf16[8,192,768]{2,1,0:T(8,128)(2,1)}, u32[]{:S(2)}, u32[]{:S(2)}) async-start(bf16[8,192,768]{2,1,0:T(8,128)(2,1)} %bitcast.57), calls=%async_computation.2 | async-start | bytes 4718592 | tf_op jit(solution)/shard_map/all_to_all | solution.py:475
  164.0 9.9 %collective-permute-start.10 = (bf16[128,768]{1,0:T(8,128)(2,1)}, bf16[128,768]{1,0:T(8,128)(2,1)S(1)}, u32[]{:S(2)}, u32[]{:S(2)}) collective-permute-start(bf16[128,768]{1,0:T(8,128)(2,1)} %get-tuple-element.61), channel_id=1, source_target_pairs={{0,24},{8,16},{16,8},{24,0},{1,25},{9,17},{17,9},{25,1},{2,26},{10... | collective-permute-start | bytes 589832 | tf_op jit(solution)/shard_map/ppermute | solution.py:463
  166.4 8.6 %collective-permute-start.8 = (bf16[128,768]{1,0:T(8,128)(2,1)}, bf16[128,768]{1,0:T(8,128)(2,1)S(1)}, u32[]{:S(2)}, u32[]{:S(2)}) collective-permute-start(bf16[128,768]{1,0:T(8,128)(2,1)} %get-tuple-element.59), channel_id=1, source_target_pairs={{0,8},{8,0},{16,24},{24,16},{1,9},{9,1},{17,25},{25,17},{2,10},{10... | collective-permute-start | bytes 589832 | tf_op jit(solution)/shard_map/ppermute | solution.py:463
  169.7 12.5 %collective-permute-start.9 = (bf16[128,768]{1,0:T(8,128)(2,1)}, bf16[128,768]{1,0:T(8,128)(2,1)S(1)}, u32[]{:S(2)}, u32[]{:S(2)}) collective-permute-start(bf16[128,768]{1,0:T(8,128)(2,1)} %get-tuple-element.60), channel_id=1, source_target_pairs={{0,16},{8,24},{16,0},{24,8},{1,17},{9,25},{17,1},{25,9},{2,18},{10... | collective-permute-start | bytes 589832 | tf_op jit(solution)/shard_map/ppermute | solution.py:463
  188.8 24.9 %all-to-all-start.3 = ((bf16[8,48,768]{2,1,0:T(8,128)(2,1)}), bf16[8,48,768]{2,1,0:T(8,128)(2,1)S(1)}, u32[]{:S(2)}, u32[]{:S(2)}) async-start(bf16[8,48,768]{2,1,0:T(8,128)(2,1)} %reduce-scatter.2.cloned.1.call-done), calls=%async_computation.4 | async-start | bytes 1179648 | tf_op jit(solution)/shard_map/all_to_all | solution.py:475
  197.1 15.6 %collective-permute-start.12 = (bf16[112,768]{1,0:T(8,128)(2,1)}, bf16[112,768]{1,0:T(8,128)(2,1)S(1)}, u32[]{:S(2)}, u32[]{:S(2)}) collective-permute-start(bf16[112,768]{1,0:T(8,128)(2,1)} %get-tuple-element.68), channel_id=1, source_target_pairs={{0,2},{1,3},{2,0},{3,1},{4,6},{5,7},{6,4},{7,5},{8,10},{9,11},{10,... | collective-permute-start | bytes 516104 | tf_op jit(solution)/shard_map/ppermute | solution.py:463
  199.2 13.5 %collective-permute-start.13 = (bf16[112,768]{1,0:T(8,128)(2,1)}, bf16[112,768]{1,0:T(8,128)(2,1)S(1)}, u32[]{:S(2)}, u32[]{:S(2)}) collective-permute-start(bf16[112,768]{1,0:T(8,128)(2,1)} %get-tuple-element.69), channel_id=1, source_target_pairs={{0,4},{1,5},{2,6},{3,7},{4,0},{5,1},{6,2},{7,3},{8,12},{9,13},{10,... | collective-permute-start | bytes 516104 | tf_op jit(solution)/shard_map/ppermute | solution.py:463
  200.5 12.1 %collective-permute-start.14 = (bf16[112,768]{1,0:T(8,128)(2,1)}, bf16[112,768]{1,0:T(8,128)(2,1)S(1)}, u32[]{:S(2)}, u32[]{:S(2)}) collective-permute-start(bf16[112,768]{1,0:T(8,128)(2,1)} %get-tuple-element.70), channel_id=1, source_target_pairs={{0,6},{1,7},{2,4},{3,5},{4,2},{5,3},{6,0},{7,1},{8,14},{9,15},{10,... | collective-permute-start | bytes 516104 | tf_op jit(solution)/shard_map/ppermute | solution.py:463
  216.8 7.2 %collective-permute-start.17 = (bf16[112,768]{1,0:T(8,128)(2,1)S(1)}, bf16[112,768]{1,0:T(8,128)(2,1)S(1)}, u32[]{:S(2)}, u32[]{:S(2)}) collective-permute-start(bf16[112,768]{1,0:T(8,128)(2,1)S(1)} %add_convert_fusion.1), channel_id=1, source_target_pairs={{0,8},{8,0},{16,24},{24,16},{1,9},{9,1},{17,25},{25,17},{2,10},{10... | collective-permute-start | bytes 516104 | tf_op jit(solution)/shard_map/ppermute | solution.py:463
  216.8 8.7 %collective-permute-start.18 = (bf16[112,768]{1,0:T(8,128)(2,1)S(1)}, bf16[112,768]{1,0:T(8,128)(2,1)S(1)}, u32[]{:S(2)}, u32[]{:S(2)}) collective-permute-start(bf16[112,768]{1,0:T(8,128)(2,1)S(1)} %add_convert_fusion.1), channel_id=1, source_target_pairs={{0,16},{8,24},{16,0},{24,8},{1,17},{9,25},{17,1},{25,9},{2,18},{10... | collective-permute-start | bytes 516104 | tf_op jit(solution)/shard_map/ppermute | solution.py:463
  219.8 9.2 %collective-permute-start.19 = (bf16[112,768]{1,0:T(8,128)(2,1)S(1)}, bf16[112,768]{1,0:T(8,128)(2,1)S(1)}, u32[]{:S(2)}, u32[]{:S(2)}) collective-permute-start(bf16[112,768]{1,0:T(8,128)(2,1)S(1)} %add_convert_fusion.1), channel_id=1, source_target_pairs={{0,24},{8,16},{16,8},{24,0},{1,25},{9,17},{17,9},{25,1},{2,26},{10... | collective-permute-start | bytes 516104 | tf_op jit(solution)/shard_map/ppermute | solution.py:463
  229.1 11.9 %collective-permute-start.20 = (bf16[112,768]{1,0:T(8,128)(2,1)S(1)}, bf16[112,768]{1,0:T(8,128)(2,1)S(1)}, u32[]{:S(2)}, u32[]{:S(2)}) collective-permute-start(bf16[112,768]{1,0:T(8,128)(2,1)S(1)} %add_convert_fusion.refs_0_), channel_id=1, source_target_pairs={{0,2},{1,3},{2,0},{3,1},{4,6},{5,7},{6,4},{7,5},{8,10},{9,11},{10,... | collective-permute-start | bytes 516104 | tf_op jit(solution)/shard_map/ppermute | solution.py:463
  235.7 10.2 %collective-permute-start.21 = (bf16[112,768]{1,0:T(8,128)(2,1)S(1)}, bf16[112,768]{1,0:T(8,128)(2,1)S(1)}, u32[]{:S(2)}, u32[]{:S(2)}) collective-permute-start(bf16[112,768]{1,0:T(8,128)(2,1)S(1)} %add_convert_fusion.refs_0_), channel_id=1, source_target_pairs={{0,4},{1,5},{2,6},{3,7},{4,0},{5,1},{6,2},{7,3},{8,12},{9,13},{10,... | collective-permute-start | bytes 516104 | tf_op jit(solution)/shard_map/ppermute | solution.py:463
  237.7 8.2 %collective-permute-start.22 = (bf16[112,768]{1,0:T(8,128)(2,1)S(1)}, bf16[112,768]{1,0:T(8,128)(2,1)S(1)}, u32[]{:S(2)}, u32[]{:S(2)}) collective-permute-start(bf16[112,768]{1,0:T(8,128)(2,1)S(1)} %add_convert_fusion.refs_0_), channel_id=1, source_target_pairs={{0,6},{1,7},{2,4},{3,5},{4,2},{5,3},{6,0},{7,1},{8,14},{9,15},{10,... | collective-permute-start | bytes 516104 | tf_op jit(solution)/shard_map/ppermute | solution.py:463
  239.1 7.9 %collective-permute-start.23 = (bf16[112,768]{1,0:T(8,128)(2,1)S(1)}, bf16[112,768]{1,0:T(8,128)(2,1)S(1)}, u32[]{:S(2)}, u32[]{:S(2)}) collective-permute-start(bf16[112,768]{1,0:T(8,128)(2,1)S(1)} %add_convert_fusion.refs_0_), channel_id=1, source_target_pairs={{0,1},{1,0},{2,3},{3,2},{4,5},{5,4},{6,7},{7,6},{8,9},{9,8},{10,11... | collective-permute-start | bytes 516104 | tf_op jit(solution)/shard_map/ppermute | solution.py:463
  (40 other events, 254.0 us)
Sparse Core Ops, SparseCore 0:
  97.3 51.1 reduce-scatter.1

commit v3 on v2

v3 whole, which is shorter than its diff:
```python
import jax
import jax.numpy as jnp
from jax import lax
from jax.experimental import pallas as pl
from jax.experimental.pallas import tpu as pltpu
from jax.sharding import PartitionSpec as P

F32 = jnp.float32
BF16 = jnp.bfloat16
EDGE = 16
LANES = 128
SUB = 384
PARAMS = pltpu.CompilerParams(vmem_limit_bytes=56 << 20)


def shape(dims, dtype):
    return jax.ShapeDtypeStruct(dims, dtype)


def dot(a, b):
    return jnp.dot(a, b, preferred_element_type=F32)


def dot_rows(a, b):
    return lax.dot_general(a, b, (((0,), (0,)), ((), ())), preferred_element_type=F32)


def dot_last(a, b):
    return lax.dot_general(a, b, (((1,), (1,)), ((), ())), preferred_element_type=F32)


def sigmoid(value):
    return 0.5 + 0.5 * jnp.tanh(0.5 * value)


def fill_padded(scratch, before, own, after):
    rows = own.shape[0]
    scratch[0:EDGE, :] = before[...].astype(F32)
    scratch[EDGE : EDGE + rows, :] = own[...].astype(F32)
    scratch[EDGE + rows : 2 * EDGE + rows, :] = after[...].astype(F32)


def conv_forward(before, own, after, segments, ids, weight, point, place):
    rows, width = own.shape
    length = segments.shape[1]
    taps = weight.shape[0]
    shift = EDGE - (taps - 1) // 2
    tall = rows + 2 * EDGE

    def kernel(
        place,
        before,
        own,
        after,
        segments,
        ids,
        weight,
        point,
        conv_out,
        act_out,
        packet,
        seg,
        scratch,
    ):
        fill_padded(scratch, before, own, after)
        frame = lax.broadcasted_iota(jnp.int32, (tall, length), 0) + (place[0] * rows - EDGE)
        chosen = frame == lax.broadcasted_iota(jnp.int32, (tall, length), 1)
        chosen = jnp.where(chosen, 1.0, 0.0).astype(BF16)
        numbers = jnp.broadcast_to(segments[...].astype(F32) + 1.0, (LANES, length))
        seg[...] = dot_last(chosen, numbers.astype(BF16)) - 1.0
        low = jnp.concatenate([ids[...].astype(F32), jnp.zeros((EDGE - 2, rows), F32)], axis=0)
        packet[rows:, :] = jnp.zeros((EDGE, width), BF16)
        packet[rows:, 0:rows] = low.astype(BF16)

        def column(index, carry):
            lanes = pl.ds(pl.multiple_of(index * LANES, LANES), LANES)
            seg_own = seg[EDGE : EDGE + rows, :]
            total = jnp.zeros((rows, LANES), F32)
            for tap in range(taps):
                first = tap + shift
                same = seg[first : first + rows, :] == seg_own
                piece = jnp.where(same, scratch[first : first + rows, lanes], 0.0)
                total = total + weight[tap : tap + 1, lanes] * piece
            conv_out[:, lanes] = total
            act_out[:, lanes] = (total * sigmoid(total)).astype(BF16)
            return carry

        lax.fori_loop(0, width // LANES, column, 0)
        packet[:rows, :] = (own[...].astype(F32) + dot(act_out[...], point[...])).astype(BF16)

    return pl.pallas_call(
        kernel,
        in_specs=[pl.BlockSpec(memory_space=pltpu.SMEM)]
        + [pl.BlockSpec(memory_space=pltpu.VMEM)] * 7,
        out_shape=(
            shape((rows, width), F32),
            shape((rows, width), BF16),
            shape((rows + EDGE, width), BF16),
            shape((tall, LANES), F32),
        ),
        scratch_shapes=[pltpu.VMEM((tall, width), F32)],
        compiler_params=PARAMS,
        name="conv_forward",
    )(place, before, own, after, segments, ids, weight, point)


def conv_backward_kernel(before, own, after, seg, weight, grad_mixed, out, scratch):
    rows, width = own.shape
    taps = weight.shape[0]
    shift = EDGE - (taps - 1) // 2
    fill_padded(scratch, before, own, after)

    def column(index, carry):
        lanes = pl.ds(pl.multiple_of(index * LANES, LANES), LANES)
        seg_own = seg[EDGE : EDGE + rows, :]
        total = grad_mixed[:, lanes]
        for tap in range(taps):
            first = tap + shift
            same = seg[first : first + rows, :] == seg_own
            piece = jnp.where(same, scratch[first : first + rows, lanes], 0.0)
            total = total + weight[taps - 1 - tap : taps - tap, lanes] * piece
        out[:, lanes] = total.astype(BF16)
        return carry

    lax.fori_loop(0, width // LANES, column, 0)


def conv_backward(before, own, after, seg, weight, grad_mixed):
    rows, width = own.shape
    return pl.pallas_call(
        conv_backward_kernel,
        out_shape=shape((rows, width), BF16),
        scratch_shapes=[pltpu.VMEM((rows + 2 * EDGE, width), F32)],
        compiler_params=PARAMS,
        name="conv_backward",
    )(before, own, after, seg, weight, grad_mixed)


def tail(
    where, parts, cot, conv, act, point_t, before, own, after, seg, router_part, places, taps, experts
):
    rows, width = own.shape
    shift = EDGE - (taps - 1) // 2
    groups = places // 2
    used = width // places
    lead = -(-used // EDGE) * EDGE
    extra = -(-(taps + 1 + experts) // EDGE)
    count = len(parts)
    pieces = (groups, lead + EDGE, width)

    def kernel(where, *refs):
        parts = refs[:count]
        cot, conv, act, point_t, before, own, after, seg, router_part = refs[count : count + 9]
        grad_mixed, grad_conv, mine, theirs, scratch, shared = refs[count + 9 :]
        core = where[0] % 2
        total = cot[...].astype(F32)
        for part in parts:
            total = total + part[...].astype(F32)
        grad_mixed[...] = total
        low = total.astype(BF16)
        grad_act = dot(low, point_t[...])
        value = conv[...]
        sigma = sigmoid(value)
        grad_conv[...] = (grad_act * (sigma * (1.0 + value * (1.0 - sigma)))).astype(BF16)
        fill_padded(scratch, before, own, after)
        point = dot_rows(act[...], low).astype(BF16)
        for index in range(places):
            side, group = divmod(index, groups)
            shared[side, group] = jnp.zeros(pieces[1:], BF16)
            shared[side, group, 0:used, :] = point[index * used : (index + 1) * used]

        def column(index, carry):
            lanes = pl.ds(pl.multiple_of(index * LANES, LANES), LANES)
            seg_own = seg[EDGE : EDGE + rows, :]
            slope = grad_conv[:, lanes].astype(F32)
            sums = []
            for tap in range(taps):
                first = tap + shift
                same = seg[first : first + rows, :] == seg_own
                piece = jnp.where(same, scratch[first : first + rows, lanes], 0.0)
                sums.append(jnp.sum(slope * piece, axis=0, keepdims=True))
            sums.append(jnp.zeros((1, LANES), F32))
            spot = lax.broadcasted_iota(jnp.int32, (experts, LANES), 0) == where[0]
            sums.append(jnp.where(spot, router_part[0:1, lanes], 0.0))
            missing = extra * EDGE - (taps + 1 + experts)
            if missing:
                sums.append(jnp.zeros((missing, LANES), F32))
            small = jnp.concatenate(sums, axis=0).astype(BF16)
            for index in range(extra):
                side, group = divmod(index, groups)
                shared[side, group, lead : lead + EDGE, lanes] = small[
                    index * EDGE : (index + 1) * EDGE
                ]
            return carry

        lax.fori_loop(0, width // LANES, column, 0)
        mine[...] = shared[core]
        theirs[...] = shared[1 - core]

    return pl.pallas_call(
        kernel,
        in_specs=[pl.BlockSpec(memory_space=pltpu.SMEM)]
        + [pl.BlockSpec(memory_space=pltpu.VMEM)] * (count + 9),
        out_shape=(
            shape((rows, width), F32),
            shape((rows, width), BF16),
            shape(pieces, BF16),
            shape(pieces, BF16),
        ),
        scratch_shapes=[
            pltpu.VMEM((rows + 2 * EDGE, width), F32),
            pltpu.VMEM((2,) + pieces, BF16),
        ],
        compiler_params=PARAMS,
        name="tail",
    )(where, *parts, cot, conv, act, point_t, before, own, after, seg, router_part)


def table_of(ids, experts, capacity):
    rows = ids.shape[1]
    ids = ids[0:2, :].astype(F32)
    expert = lax.broadcasted_iota(jnp.int32, (experts, rows), 0).astype(F32)
    named = [jnp.where(expert == ids[j : j + 1, :], 1.0, 0.0) for j in range(2)]
    earlier = lax.broadcasted_iota(jnp.int32, (rows, rows), 0)
    earlier = earlier < lax.broadcasted_iota(jnp.int32, (rows, rows), 1)
    counts = dot((named[0] + named[1]).astype(BF16), jnp.where(earlier, 1.0, 0.0).astype(BF16))
    row = lax.broadcasted_iota(jnp.int32, (experts * capacity, rows), 0).astype(F32)
    table = jnp.zeros((experts * capacity, rows), F32)
    for j in range(2):
        slot = jnp.sum(named[j] * counts, axis=0, keepdims=True)
        table = jnp.where(row == ids[j : j + 1, :] * capacity + slot, 1.0, table)
    return table.astype(BF16)


def place_own(packet, cot, experts, capacity):
    rows, width = cot.shape

    def kernel(packet, cot, out, table_out):
        table = table_of(packet[rows:, :rows], experts, capacity)
        table_out[...] = table
        for index, array in enumerate((packet[:rows, :], cot[...])):
            placed = dot(table, array).astype(BF16)
            for expert in range(experts):
                start = (2 * expert + index) * capacity
                piece = placed[expert * capacity : (expert + 1) * capacity]
                out[start : start + capacity, :] = piece

    return pl.pallas_call(
        kernel,
        out_shape=(
            shape((2 * experts * capacity, width), BF16),
            shape((experts * capacity, rows), BF16),
        ),
        compiler_params=PARAMS,
        name="place_own",
    )(packet, cot)


def place_rest(packets, experts, capacity):
    count = len(packets)
    rows, width = packets[0].shape[0] - EDGE, packets[0].shape[1]
    per_expert = count * capacity

    def kernel(*refs):
        out, tables = refs[count:]
        for k, packet in enumerate(refs[:count]):
            table = table_of(packet[rows:, :rows], experts, capacity)
            tables[k] = table
            placed = dot(table, packet[:rows, :]).astype(BF16)
            for expert in range(experts):
                start = expert * per_expert + k * capacity
                piece = placed[expert * capacity : (expert + 1) * capacity]
                out[start : start + capacity, :] = piece

    return pl.pallas_call(
        kernel,
        out_shape=(
            shape((experts * per_expert, width), BF16),
            shape((count, experts * capacity, rows), BF16),
        ),
        compiler_params=PARAMS,
        name="place_rest",
    )(*packets)


def place_more(tables, arrays, experts, capacity):
    count, _, rows = tables.shape
    width = arrays[0].shape[1]
    per_expert = count * capacity

    def kernel(tables, *refs):
        out = refs[count]
        for k, array in enumerate(refs[:count]):
            placed = dot(tables[k], array[...]).astype(BF16)
            for expert in range(experts):
                start = expert * per_expert + k * capacity
                piece = placed[expert * capacity : (expert + 1) * capacity]
                out[start : start + capacity, :] = piece

    return pl.pallas_call(
        kernel,
        out_shape=shape((experts * per_expert, width), BF16),
        compiler_params=PARAMS,
        name="place_more",
    )(tables, *arrays)


def collect(table, tables, buffer, experts, capacity):
    rest, _, rows = tables.shape
    count = rest + 1
    width = buffer.shape[1]
    per_expert = count * capacity

    def kernel(table, tables, buffer, *outs):
        for k, out in enumerate(outs):
            starts = [expert * per_expert + k * capacity for expert in range(experts)]
            pieces = [buffer[start : start + capacity, :] for start in starts]
            here = tables[k - 1] if k else table[...]
            out[...] = dot_rows(here, jnp.concatenate(pieces, axis=0)).astype(BF16)

    return pl.pallas_call(
        kernel,
        out_shape=[shape((rows, width), BF16)] * count,
        compiler_params=PARAMS,
        name="collect",
    )(table, tables, buffer)


def expert_specs(own, rest):
    places, _, capacity, width = own.shape
    packs = rest.shape[1] + 1
    group = max(1, SUB // (packs * capacity))
    chunk = group * packs * capacity

    def by_place(*dims):
        zeros = (0,) * len(dims)
        return pl.BlockSpec((group,) + dims, lambda i: (i,) + zeros)

    def flat(columns):
        return pl.BlockSpec((chunk, columns), lambda i: (i, 0))

    def full(dims):
        return pl.BlockSpec(dims, lambda i: (0,) * len(dims))

    return packs, group, chunk, by_place, flat, full


def by_cell(own, rest, which, group):
    pieces = []
    for place in range(group):
        pieces.append(own[place, which])
        pieces += [rest[place, k] for k in range(rest.shape[1])]
    return jnp.concatenate(pieces, axis=0)


def chosen_expert(where, rows, columns, axis):
    index = lax.broadcasted_iota(jnp.int32, (rows, columns), axis)
    return jnp.where(index == where[0], 1.0, 0.0).astype(BF16)


def expert_forward(where, own, rest, weight_in, weight_out, router_weight):
    places, _, capacity, width = own.shape
    inner = weight_in.shape[1]
    packs, group, chunk, by_place, flat, full = expert_specs(own, rest)
    total = places * packs * capacity

    experts = router_weight.shape[0]

    def kernel(where, own, rest, w_in, w_out, router, *outs):
        gated_out, rows_out, hidden_out, slope_out, gate_out = outs
        row = by_cell(own, rest, 0, group)
        rows_out[...] = row
        router_rows = dot(chosen_expert(where, LANES, experts, 1), router[...]).astype(BF16)
        gate = sigmoid(dot_last(row, router_rows))
        gate_out[...] = gate
        pre = dot(row, w_in[...])
        sigma = sigmoid(pre)
        hidden = (pre * sigma).astype(BF16)
        hidden_out[...] = hidden
        slope_out[...] = (sigma * (1.0 + pre * (1.0 - sigma))).astype(BF16)
        gate_wide = jnp.concatenate([gate] * (width // LANES), axis=1)
        gated = (gate_wide * dot(hidden, w_out[...])).astype(BF16)
        gated_out[...] = gated.reshape(gated_out.shape)

    return pl.pallas_call(
        kernel,
        grid=(places // group,),
        in_specs=[
            pl.BlockSpec(memory_space=pltpu.SMEM),
            by_place(2, capacity, width),
            by_place(packs - 1, capacity, width),
            full(weight_in.shape),
            full(weight_out.shape),
            full(router_weight.shape),
        ],
        out_specs=[by_place(packs * capacity, width)]
        + [flat(width), flat(inner), flat(inner), flat(LANES)],
        out_shape=[
            shape((places, packs * capacity, width), BF16),
            shape((total, width), BF16),
            shape((total, inner), BF16),
            shape((total, inner), BF16),
            shape((total, LANES), F32),
        ],
        compiler_params=PARAMS,
        name="expert_forward",
    )(where, own, rest, weight_in, weight_out, router_weight)


def expert_backward(
    where, rows, own, rest, gated, slope, gate, weight_in_t, weight_out_t, router_weight
):
    places, _, capacity, width = own.shape
    inner = weight_in_t.shape[0]
    packs, group, chunk, by_place, flat, full = expert_specs(own, rest)
    total = places * packs * capacity

    experts = router_weight.shape[0]

    def kernel(where, rows, own, rest, gated, slope, gate, w_in_t, w_out_t, router, *outs):
        back_out, grad_pre_out, grad_y_out, router_out = outs
        cot = by_cell(own, rest, 1, group).astype(F32)
        gates = gate[...]
        gate_wide = jnp.concatenate([gates] * (width // LANES), axis=1)
        grad_y = (gate_wide * cot).astype(BF16)
        grad_y_out[...] = grad_y
        grad_pre = (dot(grad_y, w_out_t[...]) * slope[...].astype(F32)).astype(BF16)
        grad_pre_out[...] = grad_pre
        out = gated[...].reshape(chunk, width).astype(F32)
        grad_gate = jnp.sum(cot * out, axis=1, keepdims=True)
        grad_logit = grad_gate * (1.0 - gates)[:, 0:1]
        router_row = dot(chosen_expert(where, 8, experts, 1), router[...])[0:1, :]
        back = dot(grad_pre, w_in_t[...]) + grad_logit * router_row
        back_out[...] = back.astype(BF16).reshape(back_out.shape)
        partial = jnp.sum(rows[...].astype(F32) * grad_logit, axis=0, keepdims=True)

        @pl.when(pl.program_id(0) == 0)
        def _():
            router_out[...] = jnp.zeros_like(router_out)

        router_out[0:1, :] += partial

    return pl.pallas_call(
        kernel,
        grid=(places // group,),
        in_specs=[
            pl.BlockSpec(memory_space=pltpu.SMEM),
            flat(width),
            by_place(2, capacity, width),
            by_place(packs - 1, capacity, width),
            by_place(packs * capacity, width),
            flat(inner),
            flat(LANES),
            full(weight_in_t.shape),
            full(weight_out_t.shape),
            full(router_weight.shape),
        ],
        out_specs=(
            by_place(packs * capacity, width),
            flat(inner),
            flat(width),
            full((8, width)),
        ),
        out_shape=(
            shape((places, packs * capacity, width), BF16),
            shape((total, inner), BF16),
            shape((total, width), BF16),
            shape((8, width), F32),
        ),
        compiler_params=PARAMS,
        name="expert_backward",
    )(where, rows, own, rest, gated, slope, gate, weight_in_t, weight_out_t, router_weight)


def add_pieces(mine, theirs, group):
    groups, size, width = mine.shape

    def kernel(group, mine, theirs, *outs):
        for index, out in enumerate(outs):
            here = group[0] ^ index
            out[...] = (mine[here].astype(F32) + theirs[here].astype(F32)).astype(BF16)

    return pl.pallas_call(
        kernel,
        in_specs=[pl.BlockSpec(memory_space=pltpu.SMEM)]
        + [pl.BlockSpec(memory_space=pltpu.VMEM)] * 2,
        out_shape=[shape((size, width), BF16)] * groups,
        compiler_params=PARAMS,
        name="add_pieces",
    )(group, mine, theirs)


def spread(own, other, group, core, used, taps, experts):
    count = len(own)
    size, width = own[0].shape

    def kernel(where, *refs):
        point, conv, router, small = refs[2 * count :]
        for index in range(2 * count):
            side = where[1] if index < count else 1 - where[1]
            place = side * count + (where[0] ^ (index % count))
            piece = refs[index][...].astype(F32)
            point[pl.ds(pl.multiple_of(place * used, 8), used), :] = piece[:used]
            small[place] = piece[size - EDGE :]
        last = -(-(taps + 1 + experts) // EDGE)
        rows = jnp.concatenate([small[place] for place in range(last)], axis=0)
        conv[...] = rows[:taps]
        router[...] = rows[taps + 1 : taps + 1 + experts]

    return pl.pallas_call(
        kernel,
        in_specs=[pl.BlockSpec(memory_space=pltpu.SMEM)]
        + [pl.BlockSpec(memory_space=pltpu.VMEM)] * (2 * count),
        out_shape=(
            shape((2 * count * used, width), F32),
            shape((taps, width), F32),
            shape((experts, width), F32),
        ),
        scratch_shapes=[pltpu.VMEM((2 * count, EDGE, width), F32)],
        compiler_params=PARAMS,
        name="spread",
    )(jnp.stack([group, core]), *own, *other)


def swap(array, axis, k):
    devices = lax.axis_size(axis)
    return lax.ppermute(array, axis, [(i, i ^ k) for i in range(devices)])


def from_all(array, axis):
    return [array] + [swap(array, axis, k) for k in range(1, lax.axis_size(axis))]


def to_all(arrays, axis):
    return [part if k == 0 else swap(part, axis, k) for k, part in enumerate(arrays)]


def exchange(array, axis):
    return lax.all_to_all(array, axis, split_axis=0, concat_axis=0, tiled=True)


def after_all(array, others):
    return lax.optimization_barrier((array, tuple(others)))[0]


def edges(array, axis):
    devices = lax.axis_size(axis)
    up = [(i, i + 1) for i in range(devices - 1)]
    down = [(j, i) for i, j in up]
    before = lax.ppermute(array[array.shape[0] - EDGE :], axis, up)
    after = lax.ppermute(array[:EDGE], axis, down)
    return before, after


def sum_parts(parts):
    parts = [part.astype(F32) for part in parts]
    while len(parts) > 1:
        parts = [a + b for a, b in zip(parts[::2], parts[1::2])]
    return parts[0]


def local(
    frames,
    segments,
    conv_weight,
    point_weight,
    router_weight,
    expert_ids,
    expert_in,
    expert_out,
    cotangent,
):
    rows_here, width = frames.shape[1:]
    taps = conv_weight.shape[0]
    experts = router_weight.shape[1]
    capacity = -(-3 * rows_here // experts // EDGE) * EDGE
    packs = lax.axis_size("dp")
    places = lax.axis_size("seq")
    place_here = lax.axis_index("seq")
    own_frames = frames[0]
    own_cot = cotangent[0]
    before, after = edges(own_frames, "seq")

    where = place_here[None]
    conv, activated, packet, seg = conv_forward(
        before, own_frames, after, segments, expert_ids[0].T, conv_weight, point_weight, where
    )
    packets = from_all(packet, "dp")
    cell = (places, -1, capacity, width)

    own_placed, table = place_own(packet, own_cot, experts, capacity)
    own_rows = exchange(own_placed.reshape(places, -1, width), "seq").reshape(cell)
    rest_placed, tables = place_rest(packets[1:], experts, capacity)
    cots = from_all(after_all(own_cot, packets), "dp")
    rest_placed, own_rows, cots[1] = lax.optimization_barrier((rest_placed, own_rows, cots[1]))
    rest_rows = exchange(rest_placed.reshape(places, -1, width), "seq")
    cots_placed = place_more(tables, cots[1:], experts, capacity)
    cots_placed, rest_rows = lax.optimization_barrier((cots_placed, rest_rows))
    rest_cots = exchange(cots_placed.reshape(places, -1, width), "seq").reshape(cell)
    rest_rows = rest_rows.reshape(cell)

    weight_in = expert_in[0]
    weight_out = expert_out[0]
    gated, rows, hidden, slope, gate = expert_forward(
        where, own_rows, rest_rows, weight_in, weight_out, router_weight.T
    )
    weight_in, weight_out, gated = lax.optimization_barrier((weight_in, weight_out, gated))
    back, grad_pre, grad_y, router_part = expert_backward(
        where,
        rows,
        own_rows,
        rest_cots,
        gated,
        slope,
        gate,
        weight_in.T,
        weight_out.T,
        router_weight.T,
    )
    back_home = exchange(back, "seq")
    grad_wout = dot_rows(hidden, grad_y)
    grad_win = dot_rows(rows, grad_pre)
    point_t = after_all(point_weight, (back,)).T
    back_home, grad_wout, grad_win, point_t = lax.optimization_barrier(
        (back_home, grad_wout, grad_win, point_t)
    )
    back_parts = collect(table, tables, back_home.reshape(-1, width), experts, capacity)
    gated_home = exchange(after_all(gated, back_parts), "seq")
    back_own = to_all(back_parts, "dp")

    core = place_here % 2
    group = place_here // 2
    groups = places // 2
    grad_mixed, grad_conv, mine, theirs = tail(
        where,
        back_own,
        own_cot,
        conv,
        activated,
        point_t,
        before,
        own_frames,
        after,
        seg,
        router_part,
        places,
        taps,
        experts,
    )
    pieces = add_pieces(mine, swap(theirs, "seq", 1), group[None])
    pieces = [pieces[0]] + [swap(pieces[m], "seq", 2 * m) for m in range(1, groups)]
    gated_parts = collect(table, tables, gated_home.reshape(-1, width), experts, capacity)
    pieces, gated_parts = lax.optimization_barrier((pieces, gated_parts))
    share = sum_parts(pieces).astype(BF16)
    grad_before, grad_after = edges(grad_conv, "seq")
    frames_grad = conv_backward(grad_before, grad_conv, grad_after, seg, conv_weight, grad_mixed)
    share = sum_parts(from_all(share, "dp")).astype(BF16)
    share, frames_grad, gated_parts = lax.optimization_barrier((share, frames_grad, gated_parts))
    gated_own = to_all(gated_parts, "dp")
    block_out = (packet[:rows_here].astype(F32) + sum_parts(gated_own)).astype(BF16)
    own_half = [share] + [swap(share, "seq", 2 * m) for m in range(1, groups)]
    other_half = [swap(part, "seq", 1) for part in own_half]
    point_grad, conv_grad, router_rows = spread(
        own_half, other_half, group, core, width // places, taps, experts
    )
    router_grad = router_rows.T
    return (
        block_out[None],
        frames_grad[None],
        conv_grad,
        router_grad,
        point_grad,
        grad_win[None],
        grad_wout[None],
    )


def solution(mesh):
    placed = (
        P("dp", "seq", None),
        P("dp", None),
        P(),
        P(),
        P(),
        P("dp", "seq", None),
        P("seq", None, "dp"),
        P("seq", "dp", None),
        P("dp", "seq", None),
    )
    return jax.shard_map(
        local,
        mesh=mesh,
        in_specs=placed,
        out_specs=(
            P("dp", "seq", None),
            P("dp", "seq", None),
            P(),
            P(),
            P(),
            P("seq", None, "dp"),
            P("seq", "dp", None),
        ),
        check_vma=False,
    )
```

time: 264 us -> 249 us (0.943)
  between operations: 14.3 us -> 0.96 us
  local copies, waits for them, and re-layouts: 20.5 us -> 13.8 us
  Pallas kernels: 52.3 us -> 55.5 us
    all_to_all x4 -> x5, waiting for transfers between devices: 39.1 us -> 30.8 us  [exchange(): return lax.all_to_all(array, axis, split_axis=0, concat_axis=0, tiled=True)]
    ppermute x23 -> x26, waiting for transfers between devices: 54.9 us -> 61.7 us  [swap(): return lax.ppermute(array, axis, [(i, i ^ k) for i in range(devices)])]
    pallas_call x7 -> x8, Pallas kernels: 37 us -> 40.3 us  [the longest x1 10.7 us: expert_backward(): pl.pallas_call(kernel, grid=(places // group,), in_specs=[pl.BlockSpec(me...]
    broadcast_in_dim x4 -> x0, local copies, waits for them, and re-layouts: 2.86 us -> none  [the longest x1 0.85 us: local(): router_cols = jnp.broadcast_to(router_col, (width, LANES))]
    ppermute x23 -> x26, starting transfers between devices: 35.3 us -> 37.4 us  [swap(): return lax.ppermute(array, axis, [(i, i ^ k) for i in range(devices)])]
    unnamed x67 -> x84, local copies, waits for them, and re-layouts: 11.8 us -> 10.7 us
    all_to_all x4 -> x5, starting transfers between devices: 21.7 us -> 22.7 us  [exchange(): return lax.all_to_all(array, axis, split_axis=0, concat_axis=0, tiled=True)]
  transfers between devices with their start and end apart: 32 -> 35, of which waited for: 20 -> 17; matrix products, arithmetic and copies ran while one was open for 8% -> 7% of each run, Pallas kernels for 15% -> 13%
where the time goes in v3:
time: 249 us; the launch traced here: 246 us
  waiting for transfers between devices  99.5 us (40%)
  starting transfers between devices  66.3 us (27%)
  Pallas kernels  55.5 us (22%)
  local copies, waits for them, and re-layouts  13.8 us (6%)
  matrix products  8.76 us (4%)
    ppermute x26, waiting for transfers between devices, swap(): return lax.ppermute(array, axis, [(i, i ^ k) for i in range(devices)])  61.7 us
    ppermute x26, starting transfers between devices, swap(): return lax.ppermute(array, axis, [(i, i ^ k) for i in range(devices)])  37.4 us
    all_to_all x5, waiting for transfers between devices, exchange(): return lax.all_to_all(array, axis, split_axis=0, concat_axis=0, tiled=True)  30.8 us
    all_to_all x5, starting transfers between devices, exchange(): return lax.all_to_all(array, axis, split_axis=0, concat_axis=0, tiled=True)  22.7 us
    unnamed x84, local copies, waits for them, and re-layouts  10.7 us
    pallas_call x1, Pallas kernels, expert_backward(): pl.pallas_call(kernel, grid=(places // group,), in_specs=[pl.BlockSpec(me...  10.7 us
    pallas_call x1, Pallas kernels, expert_forward(): pl.pallas_call(kernel, grid=(places // group,), in_specs=[pl.BlockSpec(me...  9.23 us
    dot_general x2, matrix products, dot_rows(): lax.dot_general(a, b, (((0,), (0,)), ((), ())), preferred_element_type=F32)  8.76 us
  transfers between devices with their start and end apart: 35, of which 17 were waited for; matrix products, arithmetic and copies ran while one was open for 7% of the time, Pallas kernels for 13%

profile of v3, /device:TPU:0, one launch (start us, length us, event | category | flops | bytes accessed | tf_op | source)
XLA Modules:
  0.0 246.4 jit_solution(3192611456109614616)
XLA Ops:
  5.1 3.9 %collective-permute-done.1.after.refs_10_ = bf16[16,768]{1,0:T(8,128)(2,1)S(1)} collective-permute-done((bf16[16,768]{1,0:T(8,128)(2,1)S(1)}, bf16[16,768]{1,0:T(8,128)(2,1)S(1)}, u32[]{:S(2)}, u32[]{:S(2)}) %collective-permute-start.1) | collective-permute-done | bytes 24608 | tf_op jit(solution)/shard_map/ppermute | solution.py:551
  9.6 5.0 %conv_forward.1 = (f32[128,768]{1,0:T(8,128)}, bf16[128,768]{1,0:T(8,128)(2,1)}, bf16[144,768]{1,0:T(8,128)(2,1)}, f32[160,128]{1,0:T(8,128)}) custom-call(s32[1]{0:T(128)} %bitcast.place.where, bf16[16,768]{1,0:T(8,128)(2,1)} %copy-done.31, bf16[128,768]{1,0:T(8,128)(2,1)} %bitcast.52, bf16[16,768]{1,0:T(8,128)(2,1)} %copy-done.32, s32[1,1024]{1,0:T(1,128)} %segments.1, ...), custom_call_target="tpu_custom_call" | custom-call | tf_op jit(solution)/shard_map/conv_forward/pallas_call | solution.py:91
  17.3 5.8 %all-to-all-start = ((bf16[8,96,768]{2,1,0:T(8,128)(2,1)}), bf16[8,96,768]{2,1,0:T(8,128)(2,1)S(1)}, u32[]{:S(2)}, u32[]{:S(2)}) async-start(bf16[8,96,768]{2,1,0:T(8,128)(2,1)} %bitcast.51), calls=%async_computation | async-start | bytes 2359296 | tf_op jit(solution)/shard_map/all_to_all | solution.py:539
  27.6 7.7 %collective-permute-done.2.refs_0_ = bf16[144,768]{1,0:T(8,128)(2,1)S(1)} collective-permute-done((bf16[144,768]{1,0:T(8,128)(2,1)S(1)}, bf16[144,768]{1,0:T(8,128)(2,1)S(1)}, u32[]{:S(2)}, u32[]{:S(2)}) %collective-permute-start.2) | collective-permute-done | bytes 221216 | tf_op jit(solution)/shard_map/ppermute | solution.py:527
  35.3 8.2 %collective-permute-done.3.refs_1_ = bf16[144,768]{1,0:T(8,128)(2,1)S(1)} collective-permute-done((bf16[144,768]{1,0:T(8,128)(2,1)S(1)}, bf16[144,768]{1,0:T(8,128)(2,1)S(1)}, u32[]{:S(2)}, u32[]{:S(2)}) %collective-permute-start.3) | collective-permute-done | bytes 221216 | tf_op jit(solution)/shard_map/ppermute | solution.py:527
  43.5 4.5 %collective-permute-start.5 = (bf16[128,768]{1,0:T(8,128)(2,1)S(1)}, bf16[128,768]{1,0:T(8,128)(2,1)S(1)}, u32[]{:S(2)}, u32[]{:S(2)}) collective-permute-start(bf16[128,768]{1,0:T(8,128)(2,1)S(1)} %bitcast.56), channel_id=1, source_target_pairs={{0,8},{8,0},{16,24},{24,16},{1,9},{9,1},{17,25},{25,17},{2,10},{10... | collective-permute-start | bytes 589832 | tf_op jit(solution)/shard_map/ppermute | solution.py:527
  52.4 3.8 %all-to-all-start.1 = ((bf16[8,144,768]{2,1,0:T(8,128)(2,1)}), bf16[8,144,768]{2,1,0:T(8,128)(2,1)S(1)}, u32[]{:S(2)}, u32[]{:S(2)}) async-start(bf16[8,144,768]{2,1,0:T(8,128)(2,1)} %bitcast.50), calls=%async_computation.1 | async-start | bytes 3538944 | tf_op jit(solution)/shard_map/all_to_all | solution.py:539
  60.3 12.9 %collective-permute-done.6.refs_1_ = bf16[128,768]{1,0:T(8,128)(2,1)S(1)} collective-permute-done((bf16[128,768]{1,0:T(8,128)(2,1)S(1)}, bf16[128,768]{1,0:T(8,128)(2,1)S(1)}, u32[]{:S(2)}, u32[]{:S(2)}) %collective-permute-start.6) | collective-permute-done | bytes 196640 | tf_op jit(solution)/shard_map/ppermute | solution.py:527
  79.4 4.6 %all-to-all-start.2 = ((bf16[8,144,768]{2,1,0:T(8,128)(2,1)}), bf16[8,144,768]{2,1,0:T(8,128)(2,1)}, u32[]{:S(2)}, u32[]{:S(2)}) async-start(bf16[8,144,768]{2,1,0:T(8,128)(2,1)} %bitcast.42), calls=%async_computation.2 | async-start | bytes 3538944 | tf_op jit(solution)/shard_map/all_to_all | solution.py:539
  87.8 9.2 %expert_forward.1 = (bf16[8,192,768]{2,1,0:T(8,128)(2,1)}, bf16[1536,768]{1,0:T(8,128)(2,1)}, bf16[1536,768]{1,0:T(8,128)(2,1)}, bf16[1536,768]{1,0:T(8,128)(2,1)}, f32[1536,128]{1,0:T(8,128)}) custom-call(s32[1]{0:T(128)} %bitcast.place.where, bf16[8,2,48,768]{3,2,1,0:T(8,128)(2,1)} %bitcast.38, bf16[8,3,48,768]{3,2,1,0:T(8,128)(2,1)} %bitcast.41, ...), custom_call_target="tpu_custom_call" | custom-call | tf_op jit(solution)/shard_map/expert_forward/pallas_call | solution.py:385
  97.0 10.0 %all-to-all-done.2 = bf16[8,144,768]{2,1,0:T(8,128)(2,1)} async-done(((bf16[8,144,768]{2,1,0:T(8,128)(2,1)}), bf16[8,144,768]{2,1,0:T(8,128)(2,1)}, u32[]{:S(2)}, u32[]{:S(2)}) %all-to-all-start.2) | async-done | bytes 1769504 | tf_op jit(solution)/shard_map/all_to_all | solution.py:539
  107.1 10.7 %expert_backward.1 = (bf16[8,192,768]{2,1,0:T(8,128)(2,1)}, bf16[1536,768]{1,0:T(8,128)(2,1)}, bf16[1536,768]{1,0:T(8,128)(2,1)}, f32[8,768]{1,0:T(8,128)}) custom-call(s32[1]{0:T(128)} %bitcast.place.where, bf16[1536,768]{1,0:T(8,128)(2,1)} %get-tuple-element.82.rows, bf16[8,2,48,768]{3,2,1,0:T(8,128)(2,1)} %bitcast.39, ...), custom_call_target="tpu_custom_call" | custom-call | tf_op jit(solution)/shard_map/expert_backward/pallas_call | solution.py:443
  117.8 4.7 %all-to-all-start.3 = ((bf16[8,192,768]{2,1,0:T(8,128)(2,1)}), bf16[8,192,768]{2,1,0:T(8,128)(2,1)}, u32[]{:S(2)}, u32[]{:S(2)}) async-start(bf16[8,192,768]{2,1,0:T(8,128)(2,1)} %get-tuple-element.90), calls=%async_computation.3 | async-start | bytes 4718592 | tf_op jit(solution)/shard_map/all_to_all | solution.py:539
  124.6 5.3 %fusion.3 = f32[768,768]{1,0:T(8,128)} fusion(bf16[1536,768]{1,0:T(8,128)(2,1)S(1)} %copy-done.2, bf16[1536,768]{1,0:T(8,128)(2,1)} %get-tuple-element.93), kind=kOutput, calls=%fused_computation.9 | convolution fusion | flops 1811939328 | bytes 7077888 | tf_op jit(solution)/shard_map/dot_general | solution.py:25
  129.9 3.5 %fusion.2 = f32[768,768]{1,0:T(8,128)} fusion(bf16[1536,768]{1,0:T(8,128)(2,1)S(1)} %copy-done.6, bf16[1536,768]{1,0:T(8,128)(2,1)S(1)} %copy-done.7), kind=kOutput, calls=%fused_computation.8 | convolution fusion | flops 1811939328 | bytes 7077888 | tf_op jit(solution)/shard_map/dot_general | solution.py:25
  133.4 18.4 %all-to-all-done.3 = bf16[8,192,768]{2,1,0:T(8,128)(2,1)} async-done(((bf16[8,192,768]{2,1,0:T(8,128)(2,1)}), bf16[8,192,768]{2,1,0:T(8,128)(2,1)}, u32[]{:S(2)}, u32[]{:S(2)}) %all-to-all-start.3) | async-done | bytes 2359328 | tf_op jit(solution)/shard_map/all_to_all | solution.py:539
  154.9 3.8 %all-to-all-start.4 = ((bf16[8,192,768]{2,1,0:T(8,128)(2,1)}), bf16[8,192,768]{2,1,0:T(8,128)(2,1)S(1)}, u32[]{:S(2)}, u32[]{:S(2)}) async-start(bf16[8,192,768]{2,1,0:T(8,128)(2,1)} %get-tuple-element.111.gated), calls=%async_computation.4 | async-start | bytes 4718592 | tf_op jit(solution)/shard_map/all_to_all | solution.py:539
  163.2 5.2 %collective-permute-done.10.refs_3_ = bf16[128,768]{1,0:T(8,128)(2,1)S(1)} collective-permute-done((bf16[128,768]{1,0:T(8,128)(2,1)S(1)}, bf16[128,768]{1,0:T(8,128)(2,1)S(1)}, u32[]{:S(2)}, u32[]{:S(2)}) %collective-permute-start.10) | collective-permute-done | bytes 196640 | tf_op jit(solution)/shard_map/ppermute | solution.py:527
  168.4 3.8 %collective-permute-done.8.refs_1_ = bf16[128,768]{1,0:T(8,128)(2,1)S(1)} collective-permute-done((bf16[128,768]{1,0:T(8,128)(2,1)S(1)}, bf16[128,768]{1,0:T(8,128)(2,1)S(1)}, u32[]{:S(2)}, u32[]{:S(2)}) %collective-permute-start.8) | collective-permute-done | bytes 196640 | tf_op jit(solution)/shard_map/ppermute | solution.py:527
  172.2 8.0 %collective-permute-done.9.refs_2_ = bf16[128,768]{1,0:T(8,128)(2,1)S(1)} collective-permute-done((bf16[128,768]{1,0:T(8,128)(2,1)S(1)}, bf16[128,768]{1,0:T(8,128)(2,1)S(1)}, u32[]{:S(2)}, u32[]{:S(2)}) %collective-permute-start.9) | collective-permute-done | bytes 196640 | tf_op jit(solution)/shard_map/ppermute | solution.py:527
  180.9 5.9 %tail.1 = (f32[128,768]{1,0:T(8,128)}, bf16[128,768]{1,0:T(8,128)(2,1)}, bf16[4,112,768]{2,1,0:T(8,128)(2,1)}, bf16[4,112,768]{2,1,0:T(8,128)(2,1)}) custom-call(s32[1]{0:T(128)} %bitcast.place.where, bf16[128,768]{1,0:T(8,128)(2,1)} %get-tuple-element.96.refs_0_, bf16[128,768]{1,0:T(8,128)(2,1)} %copy-done.18, bf16[128,768]{1,0:T(8,128)(2,1)} %copy-done.19, ...), custom_call_target="tpu_custom_call" | custom-call | tf_op jit(solution)/shard_map/tail/pallas_call | solution.py:200
  200.3 3.6 %collective-permute-done.13 = bf16[112,768]{1,0:T(8,128)(2,1)S(1)} collective-permute-done((bf16[112,768]{1,0:T(8,128)(2,1)}, bf16[112,768]{1,0:T(8,128)(2,1)S(1)}, u32[]{:S(2)}, u32[]{:S(2)}) %collective-permute-start.13) | collective-permute-done | bytes 172064 | tf_op jit(solution)/shard_map/ppermute | solution.py:527
  215.7 4.0 %conv_backward.1 = bf16[128,768]{1,0:T(8,128)(2,1)} custom-call(bf16[16,768]{1,0:T(8,128)(2,1)} %copy-done.33, bf16[128,768]{1,0:T(8,128)(2,1)} %get-tuple-element.120.own, bf16[16,768]{1,0:T(8,128)(2,1)} %copy-done.34, f32[160,128]{1,0:T(8,128)} %get-tuple-element.103.refs_11_.seg, f32[31,768]{1,0:T(8,128)} %weight.3, f32[128,768]{1,0:T(8,128)} %get-tuple-element.121.grad_mixed), custom_call_target="tpu_custom_call" | custom-call | tf_op jit(solution)/shard_map/conv_backward/pallas_call | solution.py:130
  230.2 6.5 %collective-permute-done.24.refs_2_ = bf16[112,768]{1,0:T(8,128)(2,1)S(1)} collective-permute-done((bf16[112,768]{1,0:T(8,128)(2,1)S(1)}, bf16[112,768]{1,0:T(8,128)(2,1)S(1)}, u32[]{:S(2)}, u32[]{:S(2)}) %collective-permute-start.24) | collective-permute-done | bytes 172064 | tf_op jit(solution)/shard_map/ppermute | solution.py:527
  (151 shorter events, 86.4 us)
Async XLA Ops:
  17.3 35.1 %all-to-all-start = ((bf16[8,96,768]{2,1,0:T(8,128)(2,1)}), bf16[8,96,768]{2,1,0:T(8,128)(2,1)S(1)}, u32[]{:S(2)}, u32[]{:S(2)}) async-start(bf16[8,96,768]{2,1,0:T(8,128)(2,1)} %bitcast.51), calls=%async_computation | async-start | bytes 2359296 | tf_op jit(solution)/shard_map/all_to_all | solution.py:539
  23.1 12.1 %collective-permute-start.2 = (bf16[144,768]{1,0:T(8,128)(2,1)S(1)}, bf16[144,768]{1,0:T(8,128)(2,1)S(1)}, u32[]{:S(2)}, u32[]{:S(2)}) collective-permute-start(bf16[144,768]{1,0:T(8,128)(2,1)S(1)} %copy-done.8), channel_id=1, source_target_pairs={{0,8},{8,0},{16,24},{24,16},{1,9},{9,1},{17,25},{25,17},{2,10},{10... | collective-permute-start | bytes 663560 | tf_op jit(solution)/shard_map/ppermute | solution.py:527
  24.8 18.7 %collective-permute-start.3 = (bf16[144,768]{1,0:T(8,128)(2,1)S(1)}, bf16[144,768]{1,0:T(8,128)(2,1)S(1)}, u32[]{:S(2)}, u32[]{:S(2)}) collective-permute-start(bf16[144,768]{1,0:T(8,128)(2,1)S(1)} %copy-done.8), channel_id=1, source_target_pairs={{0,16},{8,24},{16,0},{24,8},{1,17},{9,25},{17,1},{25,9},{2,18},{10... | collective-permute-start | bytes 663560 | tf_op jit(solution)/shard_map/ppermute | solution.py:527
  27.4 16.1 %collective-permute-start.4 = (bf16[144,768]{1,0:T(8,128)(2,1)S(1)}, bf16[144,768]{1,0:T(8,128)(2,1)S(1)}, u32[]{:S(2)}, u32[]{:S(2)}) collective-permute-start(bf16[144,768]{1,0:T(8,128)(2,1)S(1)} %copy-done.8), channel_id=1, source_target_pairs={{0,24},{8,16},{16,8},{24,0},{1,25},{9,17},{17,9},{25,1},{2,26},{10... | collective-permute-start | bytes 663560 | tf_op jit(solution)/shard_map/ppermute | solution.py:527
  43.5 8.9 %collective-permute-start.5 = (bf16[128,768]{1,0:T(8,128)(2,1)S(1)}, bf16[128,768]{1,0:T(8,128)(2,1)S(1)}, u32[]{:S(2)}, u32[]{:S(2)}) collective-permute-start(bf16[128,768]{1,0:T(8,128)(2,1)S(1)} %bitcast.56), channel_id=1, source_target_pairs={{0,8},{8,0},{16,24},{24,16},{1,9},{9,1},{17,25},{25,17},{2,10},{10... | collective-permute-start | bytes 589832 | tf_op jit(solution)/shard_map/ppermute | solution.py:527
  52.4 27.0 %all-to-all-start.1 = ((bf16[8,144,768]{2,1,0:T(8,128)(2,1)}), bf16[8,144,768]{2,1,0:T(8,128)(2,1)S(1)}, u32[]{:S(2)}, u32[]{:S(2)}) async-start(bf16[8,144,768]{2,1,0:T(8,128)(2,1)} %bitcast.50), calls=%async_computation.1 | async-start | bytes 3538944 | tf_op jit(solution)/shard_map/all_to_all | solution.py:539
  56.2 17.0 %collective-permute-start.6 = (bf16[128,768]{1,0:T(8,128)(2,1)S(1)}, bf16[128,768]{1,0:T(8,128)(2,1)S(1)}, u32[]{:S(2)}, u32[]{:S(2)}) collective-permute-start(bf16[128,768]{1,0:T(8,128)(2,1)S(1)} %bitcast.57), channel_id=1, source_target_pairs={{0,16},{8,24},{16,0},{24,8},{1,17},{9,25},{17,1},{25,9},{2,18},{10... | collective-permute-start | bytes 589832 | tf_op jit(solution)/shard_map/ppermute | solution.py:527
  59.0 14.3 %collective-permute-start.7 = (bf16[128,768]{1,0:T(8,128)(2,1)S(1)}, bf16[128,768]{1,0:T(8,128)(2,1)S(1)}, u32[]{:S(2)}, u32[]{:S(2)}) collective-permute-start(bf16[128,768]{1,0:T(8,128)(2,1)S(1)} %bitcast.58), channel_id=1, source_target_pairs={{0,24},{8,16},{16,8},{24,0},{1,25},{9,17},{17,9},{25,1},{2,26},{10... | collective-permute-start | bytes 589832 | tf_op jit(solution)/shard_map/ppermute | solution.py:527
  79.4 27.7 %all-to-all-start.2 = ((bf16[8,144,768]{2,1,0:T(8,128)(2,1)}), bf16[8,144,768]{2,1,0:T(8,128)(2,1)}, u32[]{:S(2)}, u32[]{:S(2)}) async-start(bf16[8,144,768]{2,1,0:T(8,128)(2,1)} %bitcast.42), calls=%async_computation.2 | async-start | bytes 3538944 | tf_op jit(solution)/shard_map/all_to_all | solution.py:539
  117.8 34.0 %all-to-all-start.3 = ((bf16[8,192,768]{2,1,0:T(8,128)(2,1)}), bf16[8,192,768]{2,1,0:T(8,128)(2,1)}, u32[]{:S(2)}, u32[]{:S(2)}) async-start(bf16[8,192,768]{2,1,0:T(8,128)(2,1)} %get-tuple-element.90), calls=%async_computation.3 | async-start | bytes 4718592 | tf_op jit(solution)/shard_map/all_to_all | solution.py:539
  154.9 40.8 %all-to-all-start.4 = ((bf16[8,192,768]{2,1,0:T(8,128)(2,1)}), bf16[8,192,768]{2,1,0:T(8,128)(2,1)S(1)}, u32[]{:S(2)}, u32[]{:S(2)}) async-start(bf16[8,192,768]{2,1,0:T(8,128)(2,1)} %get-tuple-element.111.gated), calls=%async_computation.4 | async-start | bytes 4718592 | tf_op jit(solution)/shard_map/all_to_all | solution.py:539
  158.7 9.7 %collective-permute-start.10 = (bf16[128,768]{1,0:T(8,128)(2,1)S(1)}, bf16[128,768]{1,0:T(8,128)(2,1)S(1)}, u32[]{:S(2)}, u32[]{:S(2)}) collective-permute-start(bf16[128,768]{1,0:T(8,128)(2,1)S(1)} %copy-done.40), channel_id=1, source_target_pairs={{0,24},{8,16},{16,8},{24,0},{1,25},{9,17},{17,9},{25,1},{2,26},{10... | collective-permute-start | bytes 589832 | tf_op jit(solution)/shard_map/ppermute | solution.py:527
  161.2 10.9 %collective-permute-start.8 = (bf16[128,768]{1,0:T(8,128)(2,1)S(1)}, bf16[128,768]{1,0:T(8,128)(2,1)S(1)}, u32[]{:S(2)}, u32[]{:S(2)}) collective-permute-start(bf16[128,768]{1,0:T(8,128)(2,1)S(1)} %copy-done.39), channel_id=1, source_target_pairs={{0,8},{8,0},{16,24},{24,16},{1,9},{9,1},{17,25},{25,17},{2,10},{10... | collective-permute-start | bytes 589832 | tf_op jit(solution)/shard_map/ppermute | solution.py:527
  162.4 17.7 %collective-permute-start.9 = (bf16[128,768]{1,0:T(8,128)(2,1)S(1)}, bf16[128,768]{1,0:T(8,128)(2,1)S(1)}, u32[]{:S(2)}, u32[]{:S(2)}) collective-permute-start(bf16[128,768]{1,0:T(8,128)(2,1)S(1)} %copy-done.38), channel_id=1, source_target_pairs={{0,16},{8,24},{16,0},{24,8},{1,17},{9,25},{17,1},{25,9},{2,18},{10... | collective-permute-start | bytes 589832 | tf_op jit(solution)/shard_map/ppermute | solution.py:527
  193.9 10.0 %collective-permute-start.13 = (bf16[112,768]{1,0:T(8,128)(2,1)}, bf16[112,768]{1,0:T(8,128)(2,1)S(1)}, u32[]{:S(2)}, u32[]{:S(2)}) collective-permute-start(bf16[112,768]{1,0:T(8,128)(2,1)} %get-tuple-element.109), channel_id=1, source_target_pairs={{0,4},{1,5},{2,6},{3,7},{4,0},{5,1},{6,2},{7,3},{8,12},{9,13},{10,... | collective-permute-start | bytes 516104 | tf_op jit(solution)/shard_map/ppermute | solution.py:527
  195.4 8.5 %collective-permute-start.14 = (bf16[112,768]{1,0:T(8,128)(2,1)}, bf16[112,768]{1,0:T(8,128)(2,1)S(1)}, u32[]{:S(2)}, u32[]{:S(2)}) collective-permute-start(bf16[112,768]{1,0:T(8,128)(2,1)} %get-tuple-element.110), channel_id=1, source_target_pairs={{0,6},{1,7},{2,4},{3,5},{4,2},{5,3},{6,0},{7,1},{8,14},{9,15},{10,... | collective-permute-start | bytes 516104 | tf_op jit(solution)/shard_map/ppermute | solution.py:527
  204.0 15.6 %collective-permute-start.15 = (bf16[112,768]{1,0:T(8,128)(2,1)S(1)}, bf16[112,768]{1,0:T(8,128)(2,1)S(1)}, u32[]{:S(2)}, u32[]{:S(2)}) collective-permute-start(bf16[112,768]{1,0:T(8,128)(2,1)S(1)} %add_convert_fusion.2), channel_id=1, source_target_pairs={{0,8},{8,0},{16,24},{24,16},{1,9},{9,1},{17,25},{25,17},{2,10},{10... | collective-permute-start | bytes 516104 | tf_op jit(solution)/shard_map/ppermute | solution.py:527
  204.1 15.6 %collective-permute-start.16 = (bf16[112,768]{1,0:T(8,128)(2,1)S(1)}, bf16[112,768]{1,0:T(8,128)(2,1)S(1)}, u32[]{:S(2)}, u32[]{:S(2)}) collective-permute-start(bf16[112,768]{1,0:T(8,128)(2,1)S(1)} %add_convert_fusion.2), channel_id=1, source_target_pairs={{0,16},{8,24},{16,0},{24,8},{1,17},{9,25},{17,1},{25,9},{2,18},{10... | collective-permute-start | bytes 516104 | tf_op jit(solution)/shard_map/ppermute | solution.py:527
  207.0 12.7 %collective-permute-start.17 = (bf16[112,768]{1,0:T(8,128)(2,1)S(1)}, bf16[112,768]{1,0:T(8,128)(2,1)S(1)}, u32[]{:S(2)}, u32[]{:S(2)}) collective-permute-start(bf16[112,768]{1,0:T(8,128)(2,1)S(1)} %add_convert_fusion.2), channel_id=1, source_target_pairs={{0,24},{8,16},{16,8},{24,0},{1,25},{9,17},{17,9},{25,1},{2,26},{10... | collective-permute-start | bytes 516104 | tf_op jit(solution)/shard_map/ppermute | solution.py:527
  222.3 15.5 %collective-permute-start.20 = (bf16[128,768]{1,0:T(8,128)(2,1)S(1)}, bf16[128,768]{1,0:T(8,128)(2,1)S(1)}, u32[]{:S(2)}, u32[]{:S(2)}) collective-permute-start(bf16[128,768]{1,0:T(8,128)(2,1)S(1)} %copy-done.37), channel_id=1, source_target_pairs={{0,8},{8,0},{16,24},{24,16},{1,9},{9,1},{17,25},{25,17},{2,10},{10... | collective-permute-start | bytes 589832 | tf_op jit(solution)/shard_map/ppermute | solution.py:527
  223.7 16.8 %collective-permute-start.21 = (bf16[128,768]{1,0:T(8,128)(2,1)S(1)}, bf16[128,768]{1,0:T(8,128)(2,1)S(1)}, u32[]{:S(2)}, u32[]{:S(2)}) collective-permute-start(bf16[128,768]{1,0:T(8,128)(2,1)S(1)} %copy-done.36), channel_id=1, source_target_pairs={{0,16},{8,24},{16,0},{24,8},{1,17},{9,25},{17,1},{25,9},{2,18},{10... | collective-permute-start | bytes 589832 | tf_op jit(solution)/shard_map/ppermute | solution.py:527
  225.3 15.8 %collective-permute-start.22 = (bf16[128,768]{1,0:T(8,128)(2,1)S(1)}, bf16[128,768]{1,0:T(8,128)(2,1)S(1)}, u32[]{:S(2)}, u32[]{:S(2)}) collective-permute-start(bf16[128,768]{1,0:T(8,128)(2,1)S(1)} %copy-done.35), channel_id=1, source_target_pairs={{0,24},{8,16},{16,8},{24,0},{1,25},{9,17},{17,9},{25,1},{2,26},{10... | collective-permute-start | bytes 589832 | tf_op jit(solution)/shard_map/ppermute | solution.py:527
  226.7 10.0 %collective-permute-start.24 = (bf16[112,768]{1,0:T(8,128)(2,1)S(1)}, bf16[112,768]{1,0:T(8,128)(2,1)S(1)}, u32[]{:S(2)}, u32[]{:S(2)}) collective-permute-start(bf16[112,768]{1,0:T(8,128)(2,1)S(1)} %add_convert_fusion.1.refs_0_), channel_id=1, source_target_pairs={{0,4},{1,5},{2,6},{3,7},{4,0},{5,1},{6,2},{7,3},{8,12},{9,13},{10,... | collective-permute-start | bytes 516104 | tf_op jit(solution)/shard_map/ppermute | solution.py:527
  228.0 9.8 %collective-permute-start.25 = (bf16[112,768]{1,0:T(8,128)(2,1)S(1)}, bf16[112,768]{1,0:T(8,128)(2,1)S(1)}, u32[]{:S(2)}, u32[]{:S(2)}) collective-permute-start(bf16[112,768]{1,0:T(8,128)(2,1)S(1)} %add_convert_fusion.1.refs_0_), channel_id=1, source_target_pairs={{0,6},{1,7},{2,4},{3,5},{4,2},{5,3},{6,0},{7,1},{8,14},{9,15},{10,... | collective-permute-start | bytes 516104 | tf_op jit(solution)/shard_map/ppermute | solution.py:527
  (52 other events, 462.5 us)

commit v4 on v3

--- a/solution.py
+++ b/solution.py
@@ -40,7 +40,7 @@
     scratch[EDGE + rows : 2 * EDGE + rows, :] = after[...].astype(F32)
 
 
-def conv_forward(before, own, after, segments, ids, weight, point, place):
+def conv_forward(before, own, after, segments, weight, point, place):
     rows, width = own.shape
     length = segments.shape[1]
     taps = weight.shape[0]
@@ -53,12 +53,11 @@
         own,
         after,
         segments,
-        ids,
         weight,
         point,
         conv_out,
         act_out,
-        packet,
+        mixed,
         seg,
         scratch,
     ):
@@ -68,9 +67,6 @@
         chosen = jnp.where(chosen, 1.0, 0.0).astype(BF16)
         numbers = jnp.broadcast_to(segments[...].astype(F32) + 1.0, (LANES, length))
         seg[...] = dot_last(chosen, numbers.astype(BF16)) - 1.0
-        low = jnp.concatenate([ids[...].astype(F32), jnp.zeros((EDGE - 2, rows), F32)], axis=0)
-        packet[rows:, :] = jnp.zeros((EDGE, width), BF16)
-        packet[rows:, 0:rows] = low.astype(BF16)
 
         def column(index, carry):
             lanes = pl.ds(pl.multiple_of(index * LANES, LANES), LANES)
@@ -86,22 +82,22 @@
             return carry
 
         lax.fori_loop(0, width // LANES, column, 0)
-        packet[:rows, :] = (own[...].astype(F32) + dot(act_out[...], point[...])).astype(BF16)
+        mixed[...] = (own[...].astype(F32) + dot(act_out[...], point[...])).astype(BF16)
 
     return pl.pallas_call(
         kernel,
         in_specs=[pl.BlockSpec(memory_space=pltpu.SMEM)]
-        + [pl.BlockSpec(memory_space=pltpu.VMEM)] * 7,
+        + [pl.BlockSpec(memory_space=pltpu.VMEM)] * 6,
         out_shape=(
             shape((rows, width), F32),
             shape((rows, width), BF16),
-            shape((rows + EDGE, width), BF16),
+            shape((rows, width), BF16),
             shape((tall, LANES), F32),
         ),
         scratch_shapes=[pltpu.VMEM((tall, width), F32)],
         compiler_params=PARAMS,
         name="conv_forward",
-    )(place, before, own, after, segments, ids, weight, point)
+    )(place, before, own, after, segments, weight, point)
 
 
 def conv_backward_kernel(before, own, after, seg, weight, grad_mixed, out, scratch):
@@ -137,7 +133,7 @@
 
 
 def tail(
-    where, parts, cot, conv, act, point_t, before, own, after, seg, router_part, places, taps, experts
+    where, parts, cot, conv, act, point_w, before, own, after, seg, router_part, places, taps, experts
 ):
     rows, width = own.shape
     shift = EDGE - (taps - 1) // 2
@@ -150,7 +146,7 @@
 
     def kernel(where, *refs):
         parts = refs[:count]
-        cot, conv, act, point_t, before, own, after, seg, router_part = refs[count : count + 9]
+        cot, conv, act, point_w, before, own, after, seg, router_part = refs[count : count + 9]
         grad_mixed, grad_conv, mine, theirs, scratch, shared = refs[count + 9 :]
         core = where[0] % 2
         total = cot[...].astype(F32)
@@ -158,7 +154,7 @@
             total = total + part[...].astype(F32)
         grad_mixed[...] = total
         low = total.astype(BF16)
-        grad_act = dot(low, point_t[...])
+        grad_act = dot_last(low, point_w[...])
         value = conv[...]
         sigma = sigmoid(value)
         grad_conv[...] = (grad_act * (sigma * (1.0 + value * (1.0 - sigma)))).astype(BF16)
@@ -213,7 +209,7 @@
         ],
         compiler_params=PARAMS,
         name="tail",
-    )(where, *parts, cot, conv, act, point_t, before, own, after, seg, router_part)
+    )(where, *parts, cot, conv, act, point_w, before, own, after, seg, router_part)
 
 
 def table_of(ids, experts, capacity):
@@ -232,31 +228,7 @@
     return table.astype(BF16)
 
 
-def place_own(packet, cot, experts, capacity):
-    rows, width = cot.shape
-
-    def kernel(packet, cot, out, table_out):
-        table = table_of(packet[rows:, :rows], experts, capacity)
-        table_out[...] = table
-        for index, array in enumerate((packet[:rows, :], cot[...])):
-            placed = dot(table, array).astype(BF16)
-            for expert in range(experts):
-                start = (2 * expert + index) * capacity
-                piece = placed[expert * capacity : (expert + 1) * capacity]
-                out[start : start + capacity, :] = piece
-
-    return pl.pallas_call(
-        kernel,
-        out_shape=(
-            shape((2 * experts * capacity, width), BF16),
-            shape((experts * capacity, rows), BF16),
-        ),
-        compiler_params=PARAMS,
-        name="place_own",
-    )(packet, cot)
-
-
-def place_rest(packets, experts, capacity):
+def place_packets(packets, experts, capacity):
     count = len(packets)
     rows, width = packets[0].shape[0] - EDGE, packets[0].shape[1]
     per_expert = count * capacity
@@ -279,78 +251,64 @@
             shape((count, experts * capacity, rows), BF16),
         ),
         compiler_params=PARAMS,
-        name="place_rest",
+        name="place_packets",
     )(*packets)
 
 
-def place_more(tables, arrays, experts, capacity):
-    count, _, rows = tables.shape
+def split_tables(refs, counts):
+    return [ref.at[k] for ref, count in zip(refs, counts) for k in range(count)]
+
+
+def place_rows(where, tables, arrays, experts, capacity):
+    counts = [table.shape[0] for table in tables]
+    groups = len(tables)
     width = arrays[0].shape[1]
-    per_expert = count * capacity
-
-    def kernel(tables, *refs):
-        out = refs[count]
-        for k, array in enumerate(refs[:count]):
-            placed = dot(tables[k], array[...]).astype(BF16)
+    per_expert = len(arrays) * capacity
+    given = groups + len(arrays)
+
+    def kernel(where, *refs):
+        outs, scratch = refs[given:-1], refs[-1]
+        here = split_tables(refs[:groups], counts)
+        for k, (table, array) in enumerate(zip(here, refs[groups:given])):
+            placed = dot(table[...], array[...]).astype(BF16)
             for expert in range(experts):
-                start = expert * per_expert + k * capacity
                 piece = placed[expert * capacity : (expert + 1) * capacity]
-                out[start : start + capacity, :] = piece
-
-    return pl.pallas_call(
-        kernel,
-        out_shape=shape((experts * per_expert, width), BF16),
-        compiler_params=PARAMS,
-        name="place_more",
-    )(tables, *arrays)
-
-
-def collect(table, tables, buffer, experts, capacity):
-    rest, _, rows = tables.shape
-    count = rest + 1
+                scratch[expert, k * capacity : (k + 1) * capacity, :] = piece
+        for index, out in enumerate(outs):
+            out[...] = scratch[where[0] ^ index]
+
+    return pl.pallas_call(
+        kernel,
+        in_specs=[pl.BlockSpec(memory_space=pltpu.SMEM)]
+        + [pl.BlockSpec(memory_space=pltpu.VMEM)] * given,
+        out_shape=[shape((per_expert, width), BF16)] * experts,
+        scratch_shapes=[pltpu.VMEM((experts, per_expert, width), BF16)],
+        compiler_params=PARAMS,
+        name="place_rows",
+    )(where, *tables, *arrays)
+
+
+def collect(tables, buffer, experts, capacity):
+    counts = [table.shape[0] for table in tables]
+    groups = len(tables)
+    rows = tables[0].shape[2]
     width = buffer.shape[1]
-    per_expert = count * capacity
-
-    def kernel(table, tables, buffer, *outs):
-        for k, out in enumerate(outs):
+    per_expert = sum(counts) * capacity
+
+    def kernel(*refs):
+        buffer = refs[groups]
+        here = split_tables(refs[:groups], counts)
+        for k, (table, out) in enumerate(zip(here, refs[groups + 1 :])):
             starts = [expert * per_expert + k * capacity for expert in range(experts)]
             pieces = [buffer[start : start + capacity, :] for start in starts]
-            here = tables[k - 1] if k else table[...]
-            out[...] = dot_rows(here, jnp.concatenate(pieces, axis=0)).astype(BF16)
-
-    return pl.pallas_call(
-        kernel,
-        out_shape=[shape((rows, width), BF16)] * count,
+            out[...] = dot_rows(table[...], jnp.concatenate(pieces, axis=0)).astype(BF16)
+
+    return pl.pallas_call(
+        kernel,
+        out_shape=[shape((rows, width), BF16)] * sum(counts),
         compiler_params=PARAMS,
         name="collect",
-    )(table, tables, buffer)
-
-
-def expert_specs(own, rest):
-    places, _, capacity, width = own.shape
-    packs = rest.shape[1] + 1
-    group = max(1, SUB // (packs * capacity))
-    chunk = group * packs * capacity
-
-    def by_place(*dims):
-        zeros = (0,) * len(dims)
-        return pl.BlockSpec((group,) + dims, lambda i: (i,) + zeros)
-
-    def flat(columns):
-        return pl.BlockSpec((chunk, columns), lambda i: (i, 0))
-
-    def full(dims):
-        return pl.BlockSpec(dims, lambda i: (0,) * len(dims))
-
-    return packs, group, chunk, by_place, flat, full
-
-
-def by_cell(own, rest, which, group):
-    pieces = []
-    for place in range(group):
-        pieces.append(own[place, which])
-        pieces += [rest[place, k] for k in range(rest.shape[1])]
-    return jnp.concatenate(pieces, axis=0)
+    )(*tables, buffer)
 
 
 def chosen_expert(where, rows, columns, axis):
@@ -358,118 +316,125 @@
     return jnp.where(index == where[0], 1.0, 0.0).astype(BF16)
 
 
-def expert_forward(where, own, rest, weight_in, weight_out, router_weight):
-    places, _, capacity, width = own.shape
-    inner = weight_in.shape[1]
-    packs, group, chunk, by_place, flat, full = expert_specs(own, rest)
-    total = places * packs * capacity
-
+def collect_packs(pack_here, table, buffer, experts, capacity):
+    count, _, rows = table.shape
+    width = buffer.shape[1]
+    per_expert = count * capacity
+
+    def kernel(pack_here, table, buffer, out):
+        for k in range(count):
+            starts = [expert * per_expert + k * capacity for expert in range(experts)]
+            pieces = [buffer[start : start + capacity, :] for start in starts]
+            summed = dot_rows(table[k], jnp.concatenate(pieces, axis=0))
+            out[pack_here[0] ^ k] = summed.astype(BF16)
+
+    return pl.pallas_call(
+        kernel,
+        in_specs=[pl.BlockSpec(memory_space=pltpu.SMEM)]
+        + [pl.BlockSpec(memory_space=pltpu.VMEM)] * 2,
+        out_shape=shape((count, rows, width), BF16),
+        compiler_params=PARAMS,
+        name="collect_packs",
+    )(pack_here, table, buffer)
+
+
+def expert(where, rows, cots, weights, router_weight):
+    places, packs, capacity, width = cots.shape
+    inner = weights[0].shape[1]
     experts = router_weight.shape[0]
-
-    def kernel(where, own, rest, w_in, w_out, router, *outs):
-        gated_out, rows_out, hidden_out, slope_out, gate_out = outs
-        row = by_cell(own, rest, 0, group)
+    per_place = packs * capacity
+    total = places * per_place
+    group = 1
+    while 2 * group * per_place <= SUB and places % (2 * group) == 0:
+        group = 2 * group
+    chunk = group * per_place
+
+    def kernel(where, *refs):
+        rows = refs[:places]
+        cots, w_in, w_out, router = refs[places : places + 4]
+        back_out, gated_out, rows_out, hidden_out, grad_pre_out, grad_y_out, router_out = refs[
+            places + 4 : -1
+        ]
+        scratch = refs[-1]
+        step = pl.program_id(0)
+
+        @pl.when(step == 0)
+        def _():
+            router_out[...] = jnp.zeros_like(router_out)
+            for index, ref in enumerate(rows):
+                scratch[index] = ref[...]
+
+        inside = where[0] % group
+        row = jnp.concatenate([scratch[step * group + index] for index in range(group)], axis=0)
         rows_out[...] = row
-        router_rows = dot(chosen_expert(where, LANES, experts, 1), router[...]).astype(BF16)
-        gate = sigmoid(dot_last(row, router_rows))
-        gate_out[...] = gate
+        cot = jnp.concatenate(
+            [cots[inside ^ index].reshape(per_place, width) for index in range(group)], axis=0
+        ).astype(F32)
+        router_rows = dot(chosen_expert(where, LANES, experts, 1), router[...])
+        gate = sigmoid(dot_last(row, router_rows.astype(BF16)))
+        gate_wide = jnp.concatenate([gate] * (width // LANES), axis=1)
+        grad_y = (gate_wide * cot).astype(BF16)
+        grad_y_out[...] = grad_y
         pre = dot(row, w_in[...])
         sigma = sigmoid(pre)
         hidden = (pre * sigma).astype(BF16)
         hidden_out[...] = hidden
-        slope_out[...] = (sigma * (1.0 + pre * (1.0 - sigma))).astype(BF16)
-        gate_wide = jnp.concatenate([gate] * (width // LANES), axis=1)
-        gated = (gate_wide * dot(hidden, w_out[...])).astype(BF16)
-        gated_out[...] = gated.reshape(gated_out.shape)
-
-    return pl.pallas_call(
-        kernel,
-        grid=(places // group,),
-        in_specs=[
-            pl.BlockSpec(memory_space=pltpu.SMEM),
-            by_place(2, capacity, width),
-            by_place(packs - 1, capacity, width),
-            full(weight_in.shape),
-            full(weight_out.shape),
-            full(router_weight.shape),
-        ],
-        out_specs=[by_place(packs * capacity, width)]
-        + [flat(width), flat(inner), flat(inner), flat(LANES)],
+        slope = sigma * (1.0 + pre * (1.0 - sigma))
+        grad_pre = (dot_last(grad_y, w_out[...]) * slope).astype(BF16)
+        grad_pre_out[...] = grad_pre
+        gated = gate_wide * dot(hidden, w_out[...])
+        grad_gate = jnp.sum(cot * gated, axis=1, keepdims=True)
+        grad_logit = grad_gate * (1.0 - gate)[:, 0:1]
+        back = (dot_last(grad_pre, w_in[...]) + grad_logit * router_rows[0:1, :]).astype(BF16)
+        gated = gated.astype(BF16)
+        for index in range(group):
+            piece = slice(index * per_place, (index + 1) * per_place)
+            gated_out[inside ^ index] = gated[piece]
+            back_out[inside ^ index] = back[piece]
+        router_out[0:1, :] += jnp.sum(row.astype(F32) * grad_logit, axis=0, keepdims=True)
+
+    def by_place(*dims):
+        zeros = (0,) * len(dims)
+        return pl.BlockSpec((group,) + dims, lambda i, where: (i ^ (where[0] // group),) + zeros)
+
+    def flat(columns):
+        return pl.BlockSpec((chunk, columns), lambda i, where: (i, 0))
+
+    def full(dims):
+        return pl.BlockSpec(dims, lambda i, where: (0,) * len(dims))
+
+    return pl.pallas_call(
+        kernel,
+        grid_spec=pltpu.PrefetchScalarGridSpec(
+            num_scalar_prefetch=1,
+            grid=(places // group,),
+            in_specs=[full((per_place, width))] * places
+            + [by_place(packs, capacity, width)]
+            + [full(weight.shape) for weight in weights]
+            + [full(router_weight.shape)],
+            out_specs=[
+                by_place(per_place, width),
+                by_place(per_place, width),
+                flat(width),
+                flat(inner),
+                flat(inner),
+                flat(width),
+                full((8, width)),
+            ],
+            scratch_shapes=[pltpu.VMEM((places, per_place, width), BF16)],
+        ),
         out_shape=[
-            shape((places, packs * capacity, width), BF16),
+            shape((places, per_place, width), BF16),
+            shape((places, per_place, width), BF16),
             shape((total, width), BF16),
             shape((total, inner), BF16),
             shape((total, inner), BF16),
-            shape((total, LANES), F32),
-        ],
-        compiler_params=PARAMS,
-        name="expert_forward",
-    )(where, own, rest, weight_in, weight_out, router_weight)
-
-
-def expert_backward(
-    where, rows, own, rest, gated, slope, gate, weight_in_t, weight_out_t, router_weight
-):
-    places, _, capacity, width = own.shape
-    inner = weight_in_t.shape[0]
-    packs, group, chunk, by_place, flat, full = expert_specs(own, rest)
-    total = places * packs * capacity
-
-    experts = router_weight.shape[0]
-
-    def kernel(where, rows, own, rest, gated, slope, gate, w_in_t, w_out_t, router, *outs):
-        back_out, grad_pre_out, grad_y_out, router_out = outs
-        cot = by_cell(own, rest, 1, group).astype(F32)
-        gates = gate[...]
-        gate_wide = jnp.concatenate([gates] * (width // LANES), axis=1)
-        grad_y = (gate_wide * cot).astype(BF16)
-        grad_y_out[...] = grad_y
-        grad_pre = (dot(grad_y, w_out_t[...]) * slope[...].astype(F32)).astype(BF16)
-        grad_pre_out[...] = grad_pre
-        out = gated[...].reshape(chunk, width).astype(F32)
-        grad_gate = jnp.sum(cot * out, axis=1, keepdims=True)
-        grad_logit = grad_gate * (1.0 - gates)[:, 0:1]
-        router_row = dot(chosen_expert(where, 8, experts, 1), router[...])[0:1, :]
-        back = dot(grad_pre, w_in_t[...]) + grad_logit * router_row
-        back_out[...] = back.astype(BF16).reshape(back_out.shape)
-        partial = jnp.sum(rows[...].astype(F32) * grad_logit, axis=0, keepdims=True)
-
-        @pl.when(pl.program_id(0) == 0)
-        def _():
-            router_out[...] = jnp.zeros_like(router_out)
-
-        router_out[0:1, :] += partial
-
-    return pl.pallas_call(
-        kernel,
-        grid=(places // group,),
-        in_specs=[
-            pl.BlockSpec(memory_space=pltpu.SMEM),
-            flat(width),
-            by_place(2, capacity, width),
-            by_place(packs - 1, capacity, width),
-            by_place(packs * capacity, width),
-            flat(inner),
-            flat(LANES),
-            full(weight_in_t.shape),
-            full(weight_out_t.shape),
-            full(router_weight.shape),
-        ],
-        out_specs=(
-            by_place(packs * capacity, width),
-            flat(inner),
-            flat(width),
-            full((8, width)),
-        ),
-        out_shape=(
-            shape((places, packs * capacity, width), BF16),
-            shape((total, inner), BF16),
             shape((total, width), BF16),
             shape((8, width), F32),
-        ),
-        compiler_params=PARAMS,
-        name="expert_backward",
-    )(where, rows, own, rest, gated, slope, gate, weight_in_t, weight_out_t, router_weight)
+        ],
+        compiler_params=PARAMS,
+        name="expert",
+    )(where, *rows, cots, *weights, router_weight)
 
 
 def add_pieces(mine, theirs, group):
@@ -537,6 +502,15 @@
 
 def exchange(array, axis):
     return lax.all_to_all(array, axis, split_axis=0, concat_axis=0, tiled=True)
+
+
+def to_all_blocks(arrays, axis):
+    count = len(arrays)
+    if count <= 8:
+        return to_all(arrays, axis)
+    order = jnp.arange(count, dtype=jnp.int32) ^ lax.axis_index(axis)
+    moved = exchange(jnp.stack(arrays)[order], axis)[order]
+    return [moved[k] for k in range(count)]
 
 
 def after_all(array, others):
@@ -582,49 +556,35 @@
     before, after = edges(own_frames, "seq")
 
     where = place_here[None]
-    conv, activated, packet, seg = conv_forward(
-        before, own_frames, after, segments, expert_ids[0].T, conv_weight, point_weight, where
-    )
+
+    ids = jnp.pad(expert_ids[0].T.astype(BF16), ((0, EDGE - 2), (0, width - rows_here)))
+    packet = jnp.concatenate([own_cot, ids], axis=0)
     packets = from_all(packet, "dp")
+    conv, activated, mixed, seg = conv_forward(
+        before, own_frames, after, segments, conv_weight, point_weight, where
+    )
+    mixed_all = from_all(mixed, "dp")
     cell = (places, -1, capacity, width)
 
-    own_placed, table = place_own(packet, own_cot, experts, capacity)
-    own_rows = exchange(own_placed.reshape(places, -1, width), "seq").reshape(cell)
-    rest_placed, tables = place_rest(packets[1:], experts, capacity)
-    cots = from_all(after_all(own_cot, packets), "dp")
-    rest_placed, own_rows, cots[1] = lax.optimization_barrier((rest_placed, own_rows, cots[1]))
-    rest_rows = exchange(rest_placed.reshape(places, -1, width), "seq")
-    cots_placed = place_more(tables, cots[1:], experts, capacity)
-    cots_placed, rest_rows = lax.optimization_barrier((cots_placed, rest_rows))
-    rest_cots = exchange(cots_placed.reshape(places, -1, width), "seq").reshape(cell)
-    rest_rows = rest_rows.reshape(cell)
-
+    placed, table = place_packets(packets, experts, capacity)
+    placed, mixed_all[0] = lax.optimization_barrier((placed, mixed_all[0]))
+    tables = [table]
+    cots = exchange(placed.reshape(places, -1, width), "seq").reshape(cell)
+    rows = to_all_blocks(place_rows(where, tables, mixed_all, experts, capacity), "seq")
     weight_in = expert_in[0]
     weight_out = expert_out[0]
-    gated, rows, hidden, slope, gate = expert_forward(
-        where, own_rows, rest_rows, weight_in, weight_out, router_weight.T
-    )
-    weight_in, weight_out, gated = lax.optimization_barrier((weight_in, weight_out, gated))
-    back, grad_pre, grad_y, router_part = expert_backward(
+    back, gated, rows, hidden, grad_pre, grad_y, router_part = expert(
         where,
         rows,
-        own_rows,
-        rest_cots,
-        gated,
-        slope,
-        gate,
-        weight_in.T,
-        weight_out.T,
+        cots,
+        (weight_in, weight_out),
         router_weight.T,
     )
     back_home = exchange(back, "seq")
     grad_wout = dot_rows(hidden, grad_y)
     grad_win = dot_rows(rows, grad_pre)
-    point_t = after_all(point_weight, (back,)).T
-    back_home, grad_wout, grad_win, point_t = lax.optimization_barrier(
-        (back_home, grad_wout, grad_win, point_t)
-    )
-    back_parts = collect(table, tables, back_home.reshape(-1, width), experts, capacity)
+    back_home, grad_wout, grad_win = lax.optimization_barrier((back_home, grad_wout, grad_win))
+    back_parts = collect(tables, back_home.reshape(-1, width), experts, capacity)
     gated_home = exchange(after_all(gated, back_parts), "seq")
     back_own = to_all(back_parts, "dp")
 
@@ -637,7 +597,7 @@
         own_cot,
         conv,
         activated,
-        point_t,
+        point_weight,
         before,
         own_frames,
         after,
@@ -649,15 +609,19 @@
     )
     pieces = add_pieces(mine, swap(theirs, "seq", 1), group[None])
     pieces = [pieces[0]] + [swap(pieces[m], "seq", 2 * m) for m in range(1, groups)]
-    gated_parts = collect(table, tables, gated_home.reshape(-1, width), experts, capacity)
+    pack_here = lax.axis_index("dp")[None]
+    gated_parts = collect_packs(
+        pack_here, table, gated_home.reshape(-1, width), experts, capacity
+    )
     pieces, gated_parts = lax.optimization_barrier((pieces, gated_parts))
     share = sum_parts(pieces).astype(BF16)
     grad_before, grad_after = edges(grad_conv, "seq")
     frames_grad = conv_backward(grad_before, grad_conv, grad_after, seg, conv_weight, grad_mixed)
     share = sum_parts(from_all(share, "dp")).astype(BF16)
     share, frames_grad, gated_parts = lax.optimization_barrier((share, frames_grad, gated_parts))
-    gated_own = to_all(gated_parts, "dp")
-    block_out = (packet[:rows_here].astype(F32) + sum_parts(gated_own)).astype(BF16)
+    gated_own = exchange(gated_parts, "dp")
+    gated_sum = jnp.sum(gated_own.astype(F32), axis=0)
+    block_out = (mixed.astype(F32) + gated_sum).astype(BF16)
     own_half = [share] + [swap(share, "seq", 2 * m) for m in range(1, groups)]
     other_half = [swap(part, "seq", 1) for part in own_half]
     point_grad, conv_grad, router_rows = spread(

time: 249 us -> 239 us (0.960)
  waiting for transfers between devices: 99.5 us -> 89.2 us
  Pallas kernels: 55.5 us -> 48.1 us
  starting transfers between devices: 66.3 us -> 73.4 us
    ppermute x26 -> x30, starting transfers between devices: 37.4 us -> 52.2 us  [swap(): return lax.ppermute(array, axis, [(i, i ^ k) for i in range(devices)])]
    all_to_all x5 -> x4, waiting for transfers between devices: 30.8 us -> 22.6 us  [exchange(): return lax.all_to_all(array, axis, split_axis=0, concat_axis=0, tiled=True)]
    pallas_call x7 -> x5, Pallas kernels: 35.3 us -> 27.8 us  [the longest x1 14.1 us: expert(): pl.pallas_call(kernel, grid_spec=pltpu.PrefetchScalarGridSpec(num_scalar_...]
    all_to_all x5 -> x4, starting transfers between devices: 22.7 us -> 16.1 us  [exchange(): return lax.all_to_all(array, axis, split_axis=0, concat_axis=0, tiled=True)]
    ppermute x26 -> x30, waiting for transfers between devices: 61.7 us -> 59.7 us  [swap(): return lax.ppermute(array, axis, [(i, i ^ k) for i in range(devices)])]
    unnamed x84 -> x80, local copies, waits for them, and re-layouts: 10.7 us -> 11.7 us
  transfers between devices with their start and end apart: 35 -> 38, of which waited for: 17 -> 20; matrix products, arithmetic and copies ran while one was open for 7% -> 5% of each run, Pallas kernels for 13% -> 11%
where the time goes in v4:
time: 239 us; the launch traced here: 238 us
  waiting for transfers between devices  89.2 us (37%)
  starting transfers between devices  73.4 us (31%)
  Pallas kernels  48.1 us (20%)
  local copies, waits for them, and re-layouts  13.2 us (6%)
  matrix products  9.47 us (4%)
  other arithmetic  3.27 us (1%)
    ppermute x30, waiting for transfers between devices, swap(): return lax.ppermute(array, axis, [(i, i ^ k) for i in range(devices)])  59.7 us
    ppermute x30, starting transfers between devices, swap(): return lax.ppermute(array, axis, [(i, i ^ k) for i in range(devices)])  52.2 us
    all_to_all x4, waiting for transfers between devices, exchange(): return lax.all_to_all(array, axis, split_axis=0, concat_axis=0, tiled=True)  22.6 us
    all_to_all x4, starting transfers between devices, exchange(): return lax.all_to_all(array, axis, split_axis=0, concat_axis=0, tiled=True)  16.1 us
    pallas_call x1, Pallas kernels, expert(): pl.pallas_call(kernel, grid_spec=pltpu.PrefetchScalarGridSpec(num_scalar_...  14.1 us
    unnamed x80, local copies, waits for them, and re-layouts  11.7 us
    dot_general x2, matrix products, dot_rows(): lax.dot_general(a, b, (((0,), (0,)), ((), ())), preferred_element_type=F32)  9.47 us
    ppermute x2, waiting for transfers between devices, edges(): after = lax.ppermute(array[:EDGE], axis, down)  6.91 us
  transfers between devices with their start and end apart: 38, of which 20 were waited for; matrix products, arithmetic and copies ran while one was open for 5% of the time, Pallas kernels for 11%

profile of v4, /device:TPU:0, one launch (start us, length us, event | category | flops | bytes accessed | tf_op | source)
XLA Modules:
  0.0 237.6 jit_solution(14038784266475866233)
XLA Ops:
  11.3 3.7 %collective-permute-done.1.after.refs_10_ = bf16[16,768]{1,0:T(8,128)(2,1)S(1)} collective-permute-done((bf16[16,768]{1,0:T(8,128)(2,1)S(1)}, bf16[16,768]{1,0:T(8,128)(2,1)S(1)}, u32[]{:S(2)}, u32[]{:S(2)}) %collective-permute-start.1) | collective-permute-done | bytes 24608 | tf_op jit(solution)/shard_map/ppermute | solution.py:525
  15.6 5.0 %conv_forward.1 = (f32[128,768]{1,0:T(8,128)}, bf16[128,768]{1,0:T(8,128)(2,1)}, bf16[128,768]{1,0:T(8,128)(2,1)}, f32[160,128]{1,0:T(8,128)}) custom-call(s32[1]{0:T(128)} %bitcast.place.where, bf16[16,768]{1,0:T(8,128)(2,1)} %copy-done.33, bf16[128,768]{1,0:T(8,128)(2,1)} %bitcast.39, bf16[16,768]{1,0:T(8,128)(2,1)} %copy-done.34, s32[1,1024]{1,0:T(1,128)} %segments.1, ...), custom_call_target="tpu_custom_call" | custom-call | tf_op jit(solution)/shard_map/conv_forward/pallas_call | solution.py:87
  20.6 3.5 %collective-permute-done.3.refs_2_ = bf16[144,768]{1,0:T(8,128)(2,1)S(1)} collective-permute-done((bf16[144,768]{1,0:T(8,128)(2,1)S(1)}, bf16[144,768]{1,0:T(8,128)(2,1)S(1)}, u32[]{:S(2)}, u32[]{:S(2)}) %collective-permute-start.3) | collective-permute-done | bytes 221216 | tf_op jit(solution)/shard_map/ppermute | solution.py:492
  25.5 3.9 %place_packets.1 = (bf16[1536,768]{1,0:T(8,128)(2,1)}, bf16[4,384,128]{2,1,0:T(8,128)(2,1)}) custom-call(bf16[144,768]{1,0:T(8,128)(2,1)} %copy-done.5, bf16[144,768]{1,0:T(8,128)(2,1)} %copy-done.16, bf16[144,768]{1,0:T(8,128)(2,1)} %copy-done.17, bf16[144,768]{1,0:T(8,128)(2,1)} %copy-done.18), custom_call_target="tpu_custom_call" | custom-call | tf_op jit(solution)/shard_map/place_packets/pallas_call | solution.py:247
  29.4 3.9 %all-to-all-start = ((bf16[8,192,768]{2,1,0:T(8,128)(2,1)}), bf16[8,192,768]{2,1,0:T(8,128)(2,1)S(1)}, u32[]{:S(2)}, u32[]{:S(2)}) async-start(bf16[8,192,768]{2,1,0:T(8,128)(2,1)} %bitcast.36), calls=%async_computation | async-start | bytes 4718592 | tf_op jit(solution)/shard_map/all_to_all | solution.py:504
  39.0 6.8 %collective-permute-done.5.refs_2_ = bf16[128,768]{1,0:T(8,128)(2,1)S(1)} collective-permute-done((bf16[128,768]{1,0:T(8,128)(2,1)S(1)}, bf16[128,768]{1,0:T(8,128)(2,1)S(1)}, u32[]{:S(2)}, u32[]{:S(2)}) %collective-permute-start.5) | collective-permute-done | bytes 196640 | tf_op jit(solution)/shard_map/ppermute | solution.py:492
  45.8 7.9 %collective-permute-done.6.refs_3_ = bf16[128,768]{1,0:T(8,128)(2,1)S(1)} collective-permute-done((bf16[128,768]{1,0:T(8,128)(2,1)S(1)}, bf16[128,768]{1,0:T(8,128)(2,1)S(1)}, u32[]{:S(2)}, u32[]{:S(2)}) %collective-permute-start.6) | collective-permute-done | bytes 196640 | tf_op jit(solution)/shard_map/ppermute | solution.py:492
  63.4 4.2 %collective-permute-done.10.refs_3_ = bf16[192,768]{1,0:T(8,128)(2,1)S(1)} collective-permute-done((bf16[192,768]{1,0:T(8,128)(2,1)}, bf16[192,768]{1,0:T(8,128)(2,1)S(1)}, u32[]{:S(2)}, u32[]{:S(2)}) %collective-permute-start.10) | collective-permute-done | bytes 294944 | tf_op jit(solution)/shard_map/ppermute | solution.py:492
  68.9 13.7 %collective-permute-start.9 = (bf16[192,768]{1,0:T(8,128)(2,1)}, bf16[192,768]{1,0:T(8,128)(2,1)}, u32[]{:S(2)}, u32[]{:S(2)}) collective-permute-start(bf16[192,768]{1,0:T(8,128)(2,1)} %get-tuple-element.63), channel_id=1, source_target_pairs={{0,2},{1,3},{2,0},{3,1},{4,6},{5,7},{6,4},{7,5},{8,10},{9,11},{10,... | collective-permute-start | bytes 884744 | tf_op jit(solution)/shard_map/ppermute | solution.py:492
  82.6 5.3 %collective-permute-done.12.refs_5_ = bf16[192,768]{1,0:T(8,128)(2,1)S(1)} collective-permute-done((bf16[192,768]{1,0:T(8,128)(2,1)}, bf16[192,768]{1,0:T(8,128)(2,1)S(1)}, u32[]{:S(2)}, u32[]{:S(2)}) %collective-permute-start.12) | collective-permute-done | bytes 294944 | tf_op jit(solution)/shard_map/ppermute | solution.py:492
  92.2 14.1 %expert.1 = (bf16[8,192,768]{2,1,0:T(8,128)(2,1)}, bf16[8,192,768]{2,1,0:T(8,128)(2,1)}, bf16[1536,768]{1,0:T(8,128)(2,1)}, bf16[1536,768]{1,0:T(8,128)(2,1)}, b...) custom-call(s32[1]{0:T(128)} %bitcast.place.where, ...), custom_call_target="tpu_custom_call" | custom-call | tf_op jit(solution)/shard_map/expert/pallas_call | solution.py:406
  106.3 3.6 %all-to-all-start.1 = ((bf16[8,192,768]{2,1,0:T(8,128)(2,1)}), bf16[8,192,768]{2,1,0:T(8,128)(2,1)S(1)}, u32[]{:S(2)}, u32[]{:S(2)}) async-start(bf16[8,192,768]{2,1,0:T(8,128)(2,1)} %get-tuple-element.70), calls=%async_computation.1 | async-start | bytes 4718592 | tf_op jit(solution)/shard_map/all_to_all | solution.py:504
  109.9 6.0 %fusion.5 = f32[768,768]{1,0:T(8,128)} fusion(bf16[1536,768]{1,0:T(8,128)(2,1)} %get-tuple-element.73, bf16[1536,768]{1,0:T(8,128)(2,1)} %get-tuple-element.74), kind=kOutput, calls=%fused_computation.14 | convolution fusion | flops 1811939328 | bytes 7077888 | tf_op jit(solution)/shard_map/dot_general | solution.py:25
  119.4 19.9 %all-to-all-done.1 = bf16[8,192,768]{2,1,0:T(8,128)(2,1)S(1)} async-done(((bf16[8,192,768]{2,1,0:T(8,128)(2,1)}), bf16[8,192,768]{2,1,0:T(8,128)(2,1)S(1)}, u32[]{:S(2)}, u32[]{:S(2)}) %all-to-all-start.1) | async-done | bytes 2359328 | tf_op jit(solution)/shard_map/all_to_all | solution.py:504
  143.8 3.9 %all-to-all-start.2 = ((bf16[8,192,768]{2,1,0:T(8,128)(2,1)}), bf16[8,192,768]{2,1,0:T(8,128)(2,1)S(1)}, u32[]{:S(2)}, u32[]{:S(2)}) async-start(bf16[8,192,768]{2,1,0:T(8,128)(2,1)} %get-tuple-element.91), calls=%async_computation.2 | async-start | bytes 4718592 | tf_op jit(solution)/shard_map/all_to_all | solution.py:504
  147.7 3.5 %collective-permute-start.15 = (bf16[128,768]{1,0:T(8,128)(2,1)S(1)}, bf16[128,768]{1,0:T(8,128)(2,1)S(1)}, u32[]{:S(2)}, u32[]{:S(2)}) collective-permute-start(bf16[128,768]{1,0:T(8,128)(2,1)S(1)} %copy-done.39), channel_id=1, source_target_pairs={{0,8},{8,0},{16,24},{24,16},{1,9},{9,1},{17,25},{25,17},{2,10},{10... | collective-permute-start | bytes 589832 | tf_op jit(solution)/shard_map/ppermute | solution.py:492
  153.7 6.3 %collective-permute-done.15.refs_1_ = bf16[128,768]{1,0:T(8,128)(2,1)S(1)} collective-permute-done((bf16[128,768]{1,0:T(8,128)(2,1)S(1)}, bf16[128,768]{1,0:T(8,128)(2,1)S(1)}, u32[]{:S(2)}, u32[]{:S(2)}) %collective-permute-start.15) | collective-permute-done | bytes 196640 | tf_op jit(solution)/shard_map/ppermute | solution.py:492
  160.0 8.3 %collective-permute-done.16.refs_2_ = bf16[128,768]{1,0:T(8,128)(2,1)S(1)} collective-permute-done((bf16[128,768]{1,0:T(8,128)(2,1)S(1)}, bf16[128,768]{1,0:T(8,128)(2,1)S(1)}, u32[]{:S(2)}, u32[]{:S(2)}) %collective-permute-start.16) | collective-permute-done | bytes 196640 | tf_op jit(solution)/shard_map/ppermute | solution.py:492
  169.1 6.1 %tail.1 = (f32[128,768]{1,0:T(8,128)}, bf16[128,768]{1,0:T(8,128)(2,1)}, bf16[4,112,768]{2,1,0:T(8,128)(2,1)}, bf16[4,112,768]{2,1,0:T(8,128)(2,1)}) custom-call(s32[1]{0:T(128)} %bitcast.place.where, bf16[128,768]{1,0:T(8,128)(2,1)} %get-tuple-element.76.refs_0_, bf16[128,768]{1,0:T(8,128)(2,1)} %copy-done.19, bf16[128,768]{1,0:T(8,128)(2,1)} %copy-done.20, ...), custom_call_target="tpu_custom_call" | custom-call | tf_op jit(solution)/shard_map/tail/pallas_call | solution.py:196
  188.8 3.5 %collective-permute-done.20 = bf16[112,768]{1,0:T(8,128)(2,1)S(1)} collective-permute-done((bf16[112,768]{1,0:T(8,128)(2,1)}, bf16[112,768]{1,0:T(8,128)(2,1)S(1)}, u32[]{:S(2)}, u32[]{:S(2)}) %collective-permute-start.20) | collective-permute-done | bytes 172064 | tf_op jit(solution)/shard_map/ppermute | solution.py:492
  192.4 3.7 %collective-permute-start.22 = (bf16[112,768]{1,0:T(8,128)(2,1)S(1)}, bf16[112,768]{1,0:T(8,128)(2,1)S(1)}, u32[]{:S(2)}, u32[]{:S(2)}) collective-permute-start(bf16[112,768]{1,0:T(8,128)(2,1)S(1)} %add_convert_fusion.2), channel_id=1, source_target_pairs={{0,8},{8,0},{16,24},{24,16},{1,9},{9,1},{17,25},{25,17},{2,10},{10... | collective-permute-start | bytes 516104 | tf_op jit(solution)/shard_map/ppermute | solution.py:492
  205.8 4.0 %conv_backward.1 = bf16[128,768]{1,0:T(8,128)(2,1)} custom-call(bf16[16,768]{1,0:T(8,128)(2,1)} %copy-done.35, bf16[128,768]{1,0:T(8,128)(2,1)} %get-tuple-element.96.own, bf16[16,768]{1,0:T(8,128)(2,1)} %copy-done.36, f32[160,128]{1,0:T(8,128)} %get-tuple-element.82.refs_11_.seg, f32[31,768]{1,0:T(8,128)} %weight.3, f32[128,768]{1,0:T(8,128)} %get-tuple-element.97.grad_mixed), custom_call_target="tpu_custom_call" | custom-call | tf_op jit(solution)/shard_map/conv_backward/pallas_call | solution.py:126
  211.5 4.6 %all-to-all-start.3 = ((bf16[4,128,768]{2,1,0:T(8,128)(2,1)}), bf16[4,128,768]{2,1,0:T(8,128)(2,1)S(1)}, u32[]{:S(2)}, u32[]{:S(2)}) async-start(bf16[4,128,768]{2,1,0:T(8,128)(2,1)} %collect_packs.1), calls=%async_computation.3 | async-start | bytes 1572864 | tf_op jit(solution)/shard_map/all_to_all | solution.py:504
  223.6 4.7 %collective-permute-done.28.refs_2_ = bf16[112,768]{1,0:T(8,128)(2,1)S(1)} collective-permute-done((bf16[112,768]{1,0:T(8,128)(2,1)S(1)}, bf16[112,768]{1,0:T(8,128)(2,1)S(1)}, u32[]{:S(2)}, u32[]{:S(2)}) %collective-permute-start.28) | collective-permute-done | bytes 172064 | tf_op jit(solution)/shard_map/ppermute | solution.py:492
  (153 shorter events, 86.7 us)
Async XLA Ops:
  2.3 18.3 %collective-permute-start.2 = (bf16[144,768]{1,0:T(8,128)(2,1)S(1)}, bf16[144,768]{1,0:T(8,128)(2,1)S(1)}, u32[]{:S(2)}, u32[]{:S(2)}) collective-permute-start(bf16[144,768]{1,0:T(8,128)(2,1)S(1)} %fusion.1.refs_0_), channel_id=1, source_target_pairs={{0,8},{8,0},{16,24},{24,16},{1,9},{9,1},{17,25},{25,17},{2,10},{10... | collective-permute-start | bytes 663560 | tf_op jit(solution)/shard_map/ppermute | solution.py:492
  5.4 18.7 %collective-permute-start.3 = (bf16[144,768]{1,0:T(8,128)(2,1)S(1)}, bf16[144,768]{1,0:T(8,128)(2,1)S(1)}, u32[]{:S(2)}, u32[]{:S(2)}) collective-permute-start(bf16[144,768]{1,0:T(8,128)(2,1)S(1)} %fusion.1.refs_0_), channel_id=1, source_target_pairs={{0,16},{8,24},{16,0},{24,8},{1,17},{9,25},{17,1},{25,9},{2,18},{10... | collective-permute-start | bytes 663560 | tf_op jit(solution)/shard_map/ppermute | solution.py:492
  8.0 16.2 %collective-permute-start.4 = (bf16[144,768]{1,0:T(8,128)(2,1)S(1)}, bf16[144,768]{1,0:T(8,128)(2,1)S(1)}, u32[]{:S(2)}, u32[]{:S(2)}) collective-permute-start(bf16[144,768]{1,0:T(8,128)(2,1)S(1)} %fusion.1.refs_0_), channel_id=1, source_target_pairs={{0,24},{8,16},{16,8},{24,0},{1,25},{9,17},{17,9},{25,1},{2,26},{10... | collective-permute-start | bytes 663560 | tf_op jit(solution)/shard_map/ppermute | solution.py:492
  29.4 61.4 %all-to-all-start = ((bf16[8,192,768]{2,1,0:T(8,128)(2,1)}), bf16[8,192,768]{2,1,0:T(8,128)(2,1)S(1)}, u32[]{:S(2)}, u32[]{:S(2)}) async-start(bf16[8,192,768]{2,1,0:T(8,128)(2,1)} %bitcast.36), calls=%async_computation | async-start | bytes 4718592 | tf_op jit(solution)/shard_map/all_to_all | solution.py:504
  33.2 12.5 %collective-permute-start.5 = (bf16[128,768]{1,0:T(8,128)(2,1)S(1)}, bf16[128,768]{1,0:T(8,128)(2,1)S(1)}, u32[]{:S(2)}, u32[]{:S(2)}) collective-permute-start(bf16[128,768]{1,0:T(8,128)(2,1)S(1)} %copy-done.6), channel_id=1, source_target_pairs={{0,8},{8,0},{16,24},{24,16},{1,9},{9,1},{17,25},{25,17},{2,10},{10... | collective-permute-start | bytes 589832 | tf_op jit(solution)/shard_map/ppermute | solution.py:492
  36.5 17.1 %collective-permute-start.6 = (bf16[128,768]{1,0:T(8,128)(2,1)S(1)}, bf16[128,768]{1,0:T(8,128)(2,1)S(1)}, u32[]{:S(2)}, u32[]{:S(2)}) collective-permute-start(bf16[128,768]{1,0:T(8,128)(2,1)S(1)} %copy-done.6), channel_id=1, source_target_pairs={{0,16},{8,24},{16,0},{24,8},{1,17},{9,25},{17,1},{25,9},{2,18},{10... | collective-permute-start | bytes 589832 | tf_op jit(solution)/shard_map/ppermute | solution.py:492
  37.6 16.0 %collective-permute-start.7 = (bf16[128,768]{1,0:T(8,128)(2,1)S(1)}, bf16[128,768]{1,0:T(8,128)(2,1)S(1)}, u32[]{:S(2)}, u32[]{:S(2)}) collective-permute-start(bf16[128,768]{1,0:T(8,128)(2,1)S(1)} %copy-done.6), channel_id=1, source_target_pairs={{0,24},{8,16},{16,8},{24,0},{1,25},{9,17},{17,9},{25,1},{2,26},{10... | collective-permute-start | bytes 589832 | tf_op jit(solution)/shard_map/ppermute | solution.py:492
  57.9 11.1 %collective-permute-start.11 = (bf16[192,768]{1,0:T(8,128)(2,1)}, bf16[192,768]{1,0:T(8,128)(2,1)S(1)}, u32[]{:S(2)}, u32[]{:S(2)}) collective-permute-start(bf16[192,768]{1,0:T(8,128)(2,1)} %get-tuple-element.65), channel_id=1, source_target_pairs={{0,4},{1,5},{2,6},{3,7},{4,0},{5,1},{6,2},{7,3},{8,12},{9,13},{10,... | collective-permute-start | bytes 884744 | tf_op jit(solution)/shard_map/ppermute | solution.py:492
  59.8 28.1 %collective-permute-start.12 = (bf16[192,768]{1,0:T(8,128)(2,1)}, bf16[192,768]{1,0:T(8,128)(2,1)S(1)}, u32[]{:S(2)}, u32[]{:S(2)}) collective-permute-start(bf16[192,768]{1,0:T(8,128)(2,1)} %get-tuple-element.66), channel_id=1, source_target_pairs={{0,5},{1,4},{2,7},{3,6},{4,1},{5,0},{6,3},{7,2},{8,13},{9,12},{10,... | collective-permute-start | bytes 884744 | tf_op jit(solution)/shard_map/ppermute | solution.py:492
  61.3 26.7 %collective-permute-start.13 = (bf16[192,768]{1,0:T(8,128)(2,1)}, bf16[192,768]{1,0:T(8,128)(2,1)S(1)}, u32[]{:S(2)}, u32[]{:S(2)}) collective-permute-start(bf16[192,768]{1,0:T(8,128)(2,1)} %get-tuple-element.67), channel_id=1, source_target_pairs={{0,6},{1,7},{2,4},{3,5},{4,2},{5,3},{6,0},{7,1},{8,14},{9,15},{10,... | collective-permute-start | bytes 884744 | tf_op jit(solution)/shard_map/ppermute | solution.py:492
  62.7 25.2 %collective-permute-start.14 = (bf16[192,768]{1,0:T(8,128)(2,1)}, bf16[192,768]{1,0:T(8,128)(2,1)S(1)}, u32[]{:S(2)}, u32[]{:S(2)}) collective-permute-start(bf16[192,768]{1,0:T(8,128)(2,1)} %get-tuple-element.68), channel_id=1, source_target_pairs={{0,7},{1,6},{2,5},{3,4},{4,3},{5,2},{6,1},{7,0},{8,15},{9,14},{10,... | collective-permute-start | bytes 884744 | tf_op jit(solution)/shard_map/ppermute | solution.py:492
  67.6 20.4 %collective-permute-start.8 = (bf16[192,768]{1,0:T(8,128)(2,1)}, bf16[192,768]{1,0:T(8,128)(2,1)S(1)}, u32[]{:S(2)}, u32[]{:S(2)}) collective-permute-start(bf16[192,768]{1,0:T(8,128)(2,1)} %get-tuple-element.62), channel_id=1, source_target_pairs={{0,1},{1,0},{2,3},{3,2},{4,5},{5,4},{6,7},{7,6},{8,9},{9,8},{10,11... | collective-permute-start | bytes 884744 | tf_op jit(solution)/shard_map/ppermute | solution.py:492
  68.9 21.8 %collective-permute-start.9 = (bf16[192,768]{1,0:T(8,128)(2,1)}, bf16[192,768]{1,0:T(8,128)(2,1)}, u32[]{:S(2)}, u32[]{:S(2)}) collective-permute-start(bf16[192,768]{1,0:T(8,128)(2,1)} %get-tuple-element.63), channel_id=1, source_target_pairs={{0,2},{1,3},{2,0},{3,1},{4,6},{5,7},{6,4},{7,5},{8,10},{9,11},{10,... | collective-permute-start | bytes 884744 | tf_op jit(solution)/shard_map/ppermute | solution.py:492
  106.3 33.0 %all-to-all-start.1 = ((bf16[8,192,768]{2,1,0:T(8,128)(2,1)}), bf16[8,192,768]{2,1,0:T(8,128)(2,1)S(1)}, u32[]{:S(2)}, u32[]{:S(2)}) async-start(bf16[8,192,768]{2,1,0:T(8,128)(2,1)} %get-tuple-element.70), calls=%async_computation.1 | async-start | bytes 4718592 | tf_op jit(solution)/shard_map/all_to_all | solution.py:504
  143.8 40.3 %all-to-all-start.2 = ((bf16[8,192,768]{2,1,0:T(8,128)(2,1)}), bf16[8,192,768]{2,1,0:T(8,128)(2,1)S(1)}, u32[]{:S(2)}, u32[]{:S(2)}) async-start(bf16[8,192,768]{2,1,0:T(8,128)(2,1)} %get-tuple-element.91), calls=%async_computation.2 | async-start | bytes 4718592 | tf_op jit(solution)/shard_map/all_to_all | solution.py:504
  147.7 12.3 %collective-permute-start.15 = (bf16[128,768]{1,0:T(8,128)(2,1)S(1)}, bf16[128,768]{1,0:T(8,128)(2,1)S(1)}, u32[]{:S(2)}, u32[]{:S(2)}) collective-permute-start(bf16[128,768]{1,0:T(8,128)(2,1)S(1)} %copy-done.39), channel_id=1, source_target_pairs={{0,8},{8,0},{16,24},{24,16},{1,9},{9,1},{17,25},{25,17},{2,10},{10... | collective-permute-start | bytes 589832 | tf_op jit(solution)/shard_map/ppermute | solution.py:492
  151.2 17.1 %collective-permute-start.16 = (bf16[128,768]{1,0:T(8,128)(2,1)S(1)}, bf16[128,768]{1,0:T(8,128)(2,1)S(1)}, u32[]{:S(2)}, u32[]{:S(2)}) collective-permute-start(bf16[128,768]{1,0:T(8,128)(2,1)S(1)} %copy-done.38), channel_id=1, source_target_pairs={{0,16},{8,24},{16,0},{24,8},{1,17},{9,25},{17,1},{25,9},{2,18},{10... | collective-permute-start | bytes 589832 | tf_op jit(solution)/shard_map/ppermute | solution.py:492
  152.3 16.0 %collective-permute-start.17 = (bf16[128,768]{1,0:T(8,128)(2,1)S(1)}, bf16[128,768]{1,0:T(8,128)(2,1)S(1)}, u32[]{:S(2)}, u32[]{:S(2)}) collective-permute-start(bf16[128,768]{1,0:T(8,128)(2,1)S(1)} %copy-done.37), channel_id=1, source_target_pairs={{0,24},{8,16},{16,8},{24,0},{1,25},{9,17},{17,9},{25,1},{2,26},{10... | collective-permute-start | bytes 589832 | tf_op jit(solution)/shard_map/ppermute | solution.py:492
  192.4 17.3 %collective-permute-start.22 = (bf16[112,768]{1,0:T(8,128)(2,1)S(1)}, bf16[112,768]{1,0:T(8,128)(2,1)S(1)}, u32[]{:S(2)}, u32[]{:S(2)}) collective-permute-start(bf16[112,768]{1,0:T(8,128)(2,1)S(1)} %add_convert_fusion.2), channel_id=1, source_target_pairs={{0,8},{8,0},{16,24},{24,16},{1,9},{9,1},{17,25},{25,17},{2,10},{10... | collective-permute-start | bytes 516104 | tf_op jit(solution)/shard_map/ppermute | solution.py:492
  196.1 15.2 %collective-permute-start.23 = (bf16[112,768]{1,0:T(8,128)(2,1)S(1)}, bf16[112,768]{1,0:T(8,128)(2,1)S(1)}, u32[]{:S(2)}, u32[]{:S(2)}) collective-permute-start(bf16[112,768]{1,0:T(8,128)(2,1)S(1)} %add_convert_fusion.2), channel_id=1, source_target_pairs={{0,16},{8,24},{16,0},{24,8},{1,17},{9,25},{17,1},{25,9},{2,18},{10... | collective-permute-start | bytes 516104 | tf_op jit(solution)/shard_map/ppermute | solution.py:492
  197.2 14.2 %collective-permute-start.24 = (bf16[112,768]{1,0:T(8,128)(2,1)S(1)}, bf16[112,768]{1,0:T(8,128)(2,1)S(1)}, u32[]{:S(2)}, u32[]{:S(2)}) collective-permute-start(bf16[112,768]{1,0:T(8,128)(2,1)S(1)} %add_convert_fusion.2), channel_id=1, source_target_pairs={{0,24},{8,16},{16,8},{24,0},{1,25},{9,17},{17,9},{25,1},{2,26},{10... | collective-permute-start | bytes 516104 | tf_op jit(solution)/shard_map/ppermute | solution.py:492
  211.5 25.3 %all-to-all-start.3 = ((bf16[4,128,768]{2,1,0:T(8,128)(2,1)}), bf16[4,128,768]{2,1,0:T(8,128)(2,1)S(1)}, u32[]{:S(2)}, u32[]{:S(2)}) async-start(bf16[4,128,768]{2,1,0:T(8,128)(2,1)} %collect_packs.1), calls=%async_computation.3 | async-start | bytes 1572864 | tf_op jit(solution)/shard_map/all_to_all | solution.py:504
  217.5 10.8 %collective-permute-start.28 = (bf16[112,768]{1,0:T(8,128)(2,1)S(1)}, bf16[112,768]{1,0:T(8,128)(2,1)S(1)}, u32[]{:S(2)}, u32[]{:S(2)}) collective-permute-start(bf16[112,768]{1,0:T(8,128)(2,1)S(1)} %add_convert_fusion.1.refs_0_), channel_id=1, source_target_pairs={{0,4},{1,5},{2,6},{3,7},{4,0},{5,1},{6,2},{7,3},{8,12},{9,13},{10,... | collective-permute-start | bytes 516104 | tf_op jit(solution)/shard_map/ppermute | solution.py:492
  218.1 10.3 %collective-permute-start.29 = (bf16[112,768]{1,0:T(8,128)(2,1)S(1)}, bf16[112,768]{1,0:T(8,128)(2,1)S(1)}, u32[]{:S(2)}, u32[]{:S(2)}) collective-permute-start(bf16[112,768]{1,0:T(8,128)(2,1)S(1)} %add_convert_fusion.1.refs_0_), channel_id=1, source_target_pairs={{0,6},{1,7},{2,4},{3,5},{4,2},{5,3},{6,0},{7,1},{8,14},{9,15},{10,... | collective-permute-start | bytes 516104 | tf_op jit(solution)/shard_map/ppermute | solution.py:492
  (54 other events, 296.8 us)

commit v5 on v4

--- a/solution.py
+++ b/solution.py
@@ -259,12 +259,15 @@
     return [ref.at[k] for ref, count in zip(refs, counts) for k in range(count)]
 
 
-def place_rows(where, tables, arrays, experts, capacity):
+def place_rows(where, tables, arrays, experts, capacity, paired):
     counts = [table.shape[0] for table in tables]
     groups = len(tables)
     width = arrays[0].shape[1]
     per_expert = len(arrays) * capacity
     given = groups + len(arrays)
+    held = [[k] for k in range(2 if paired else experts)]
+    if paired:
+        held += [[k, k + 1] for k in range(2, experts, 2)]
 
     def kernel(where, *refs):
         outs, scratch = refs[given:-1], refs[-1]
@@ -274,14 +277,16 @@
             for expert in range(experts):
                 piece = placed[expert * capacity : (expert + 1) * capacity]
                 scratch[expert, k * capacity : (k + 1) * capacity, :] = piece
-        for index, out in enumerate(outs):
-            out[...] = scratch[where[0] ^ index]
+        for blocks, out in zip(held, outs):
+            for low, block in enumerate(blocks):
+                rows = slice(low * per_expert, (low + 1) * per_expert)
+                out[rows, :] = scratch[where[0] ^ block]
 
     return pl.pallas_call(
         kernel,
         in_specs=[pl.BlockSpec(memory_space=pltpu.SMEM)]
         + [pl.BlockSpec(memory_space=pltpu.VMEM)] * given,
-        out_shape=[shape((per_expert, width), BF16)] * experts,
+        out_shape=[shape((len(blocks) * per_expert, width), BF16) for blocks in held],
         scratch_shapes=[pltpu.VMEM((experts, per_expert, width), BF16)],
         compiler_params=PARAMS,
         name="place_rows",
@@ -362,7 +367,7 @@
         def _():
             router_out[...] = jnp.zeros_like(router_out)
             for index, ref in enumerate(rows):
-                scratch[index] = ref[...]
+                scratch[index] = ref[:per_place, :]
 
         inside = where[0] % group
         row = jnp.concatenate([scratch[step * group + index] for index in range(group)], axis=0)
@@ -408,7 +413,7 @@
         grid_spec=pltpu.PrefetchScalarGridSpec(
             num_scalar_prefetch=1,
             grid=(places // group,),
-            in_specs=[full((per_place, width))] * places
+            in_specs=[full(array.shape) for array in rows]
             + [by_place(packs, capacity, width)]
             + [full(weight.shape) for weight in weights]
             + [full(router_weight.shape)],
@@ -504,13 +509,19 @@
     return lax.all_to_all(array, axis, split_axis=0, concat_axis=0, tiled=True)
 
 
-def to_all_blocks(arrays, axis):
-    count = len(arrays)
-    if count <= 8:
-        return to_all(arrays, axis)
-    order = jnp.arange(count, dtype=jnp.int32) ^ lax.axis_index(axis)
+def to_all_paired(arrays, axis):
+    size = arrays[0].shape[0]
+    rows = [arrays[0], swap(arrays[1], axis, 1)]
+    for k, pair in enumerate(arrays[2:], 1):
+        pair = swap(pair, axis, 2 * k)
+        rows += [pair, swap(pair[size:], axis, 1)]
+    return rows
+
+
+def to_all_at_once(arrays, axis):
+    order = jnp.arange(len(arrays), dtype=jnp.int32) ^ lax.axis_index(axis)
     moved = exchange(jnp.stack(arrays)[order], axis)[order]
-    return [moved[k] for k in range(count)]
+    return [moved[k] for k in range(len(arrays))]
 
 
 def after_all(array, others):
@@ -570,7 +581,9 @@
     placed, mixed_all[0] = lax.optimization_barrier((placed, mixed_all[0]))
     tables = [table]
     cots = exchange(placed.reshape(places, -1, width), "seq").reshape(cell)
-    rows = to_all_blocks(place_rows(where, tables, mixed_all, experts, capacity), "seq")
+    paired = places <= 8
+    placed = place_rows(where, tables, mixed_all, experts, capacity, paired)
+    rows = to_all_paired(placed, "seq") if paired else to_all_at_once(placed, "seq")
     weight_in = expert_in[0]
     weight_out = expert_out[0]
     back, gated, rows, hidden, grad_pre, grad_y, router_part = expert(

time: 239 us -> 238 us (level)
  starting transfers between devices: 73.4 us -> 56.6 us
  waiting for transfers between devices: 89.2 us -> 105 us
    ppermute x30, starting transfers between devices: 52.2 us -> 35.4 us  [swap(): return lax.ppermute(array, axis, [(i, i ^ k) for i in range(devices)])]
    ppermute x30, waiting for transfers between devices: 59.7 us -> 75 us  [swap(): return lax.ppermute(array, axis, [(i, i ^ k) for i in range(devices)])]
  transfers between devices with their start and end apart: 38 -> 38, of which waited for: 20 -> 19; matrix products, arithmetic and copies ran while one was open for 5% -> 5% of each run, Pallas kernels for 11% -> 11%
where the time goes in v5:
time: 238 us; the launch traced here: 237 us
  waiting for transfers between devices  105 us (44%)
  starting transfers between devices  56.6 us (24%)
  Pallas kernels  48.4 us (20%)
  local copies, waits for them, and re-layouts  13.4 us (6%)
  matrix products  9.47 us (4%)
  other arithmetic  3.27 us (1%)
    ppermute x30, waiting for transfers between devices, swap(): return lax.ppermute(array, axis, [(i, i ^ k) for i in range(devices)])  75 us
    ppermute x30, starting transfers between devices, swap(): return lax.ppermute(array, axis, [(i, i ^ k) for i in range(devices)])  35.4 us
    all_to_all x4, waiting for transfers between devices, exchange(): return lax.all_to_all(array, axis, split_axis=0, concat_axis=0, tiled=True)  22.6 us
    all_to_all x4, starting transfers between devices, exchange(): return lax.all_to_all(array, axis, split_axis=0, concat_axis=0, tiled=True)  16.1 us
    pallas_call x1, Pallas kernels, expert(): pl.pallas_call(kernel, grid_spec=pltpu.PrefetchScalarGridSpec(num_scalar_...  14.3 us
    unnamed x80, local copies, waits for them, and re-layouts  11.8 us
    dot_general x2, matrix products, dot_rows(): lax.dot_general(a, b, (((0,), (0,)), ((), ())), preferred_element_type=F32)  9.47 us
    ppermute x2, waiting for transfers between devices, edges(): after = lax.ppermute(array[:EDGE], axis, down)  6.91 us
  transfers between devices with their start and end apart: 38, of which 19 were waited for; matrix products, arithmetic and copies ran while one was open for 5% of the time, Pallas kernels for 11%

profile of v5, /device:TPU:0, one launch (start us, length us, event | category | flops | bytes accessed | tf_op | source)
XLA Modules:
  0.0 236.7 jit_solution(3226573007067803428)
XLA Ops:
  11.3 3.7 %collective-permute-done.1.after.refs_10_ = bf16[16,768]{1,0:T(8,128)(2,1)S(1)} collective-permute-done((bf16[16,768]{1,0:T(8,128)(2,1)S(1)}, bf16[16,768]{1,0:T(8,128)(2,1)S(1)}, u32[]{:S(2)}, u32[]{:S(2)}) %collective-permute-start.1) | collective-permute-done | bytes 24608 | tf_op jit(solution)/shard_map/ppermute | solution.py:536
  15.6 5.0 %conv_forward.1 = (f32[128,768]{1,0:T(8,128)}, bf16[128,768]{1,0:T(8,128)(2,1)}, bf16[128,768]{1,0:T(8,128)(2,1)}, f32[160,128]{1,0:T(8,128)}) custom-call(s32[1]{0:T(128)} %bitcast.place.where, bf16[16,768]{1,0:T(8,128)(2,1)} %copy-done.33, bf16[128,768]{1,0:T(8,128)(2,1)} %bitcast.39, bf16[16,768]{1,0:T(8,128)(2,1)} %copy-done.34, s32[1,1024]{1,0:T(1,128)} %segments.1, ...), custom_call_target="tpu_custom_call" | custom-call | tf_op jit(solution)/shard_map/conv_forward/pallas_call | solution.py:87
  20.6 3.5 %collective-permute-done.3.refs_2_ = bf16[144,768]{1,0:T(8,128)(2,1)S(1)} collective-permute-done((bf16[144,768]{1,0:T(8,128)(2,1)S(1)}, bf16[144,768]{1,0:T(8,128)(2,1)S(1)}, u32[]{:S(2)}, u32[]{:S(2)}) %collective-permute-start.3) | collective-permute-done | bytes 221216 | tf_op jit(solution)/shard_map/ppermute | solution.py:497
  25.5 3.9 %place_packets.1 = (bf16[1536,768]{1,0:T(8,128)(2,1)}, bf16[4,384,128]{2,1,0:T(8,128)(2,1)}) custom-call(bf16[144,768]{1,0:T(8,128)(2,1)} %copy-done.8, bf16[144,768]{1,0:T(8,128)(2,1)} %copy-done.16, bf16[144,768]{1,0:T(8,128)(2,1)} %copy-done.17, bf16[144,768]{1,0:T(8,128)(2,1)} %copy-done.18), custom_call_target="tpu_custom_call" | custom-call | tf_op jit(solution)/shard_map/place_packets/pallas_call | solution.py:247
  29.4 3.9 %all-to-all-start = ((bf16[8,192,768]{2,1,0:T(8,128)(2,1)}), bf16[8,192,768]{2,1,0:T(8,128)(2,1)S(1)}, u32[]{:S(2)}, u32[]{:S(2)}) async-start(bf16[8,192,768]{2,1,0:T(8,128)(2,1)} %bitcast.36), calls=%async_computation | async-start | bytes 4718592 | tf_op jit(solution)/shard_map/all_to_all | solution.py:509
  39.0 6.8 %collective-permute-done.5.refs_2_ = bf16[128,768]{1,0:T(8,128)(2,1)S(1)} collective-permute-done((bf16[128,768]{1,0:T(8,128)(2,1)S(1)}, bf16[128,768]{1,0:T(8,128)(2,1)S(1)}, u32[]{:S(2)}, u32[]{:S(2)}) %collective-permute-start.5) | collective-permute-done | bytes 196640 | tf_op jit(solution)/shard_map/ppermute | solution.py:497
  45.8 7.9 %collective-permute-done.6.refs_3_ = bf16[128,768]{1,0:T(8,128)(2,1)S(1)} collective-permute-done((bf16[128,768]{1,0:T(8,128)(2,1)S(1)}, bf16[128,768]{1,0:T(8,128)(2,1)S(1)}, u32[]{:S(2)}, u32[]{:S(2)}) %collective-permute-start.6) | collective-permute-done | bytes 196640 | tf_op jit(solution)/shard_map/ppermute | solution.py:497
  54.4 3.5 %place_rows.1 = (bf16[192,768]{1,0:T(8,128)(2,1)}, bf16[192,768]{1,0:T(8,128)(2,1)}, bf16[384,768]{1,0:T(8,128)(2,1)}, bf16[384,768]{1,0:T(8,128)(2,1)}, bf16[384,768]{1,0:T(8,128)(2,1)}) custom-call(s32[1]{0:T(128)} %bitcast.place.where, bf16[4,384,128]{2,1,0:T(8,128)(2,1)} %get-tuple-element.55.refs_0_.table, bf16[128,768]{1,0:T(8,128)(2,1)} %get-tuple-element.57.refs_1_, ...), custom_call_target="tpu_custom_call" | custom-call | tf_op jit(solution)/shard_map/place_rows/pallas_call | solution.py:285
  61.4 13.5 %collective-permute-done.9.refs_2_ = bf16[384,768]{1,0:T(8,128)(2,1)S(1)} collective-permute-done((bf16[384,768]{1,0:T(8,128)(2,1)}, bf16[384,768]{1,0:T(8,128)(2,1)S(1)}, u32[]{:S(2)}, u32[]{:S(2)}) %collective-permute-start.9) | collective-permute-done | bytes 589856 | tf_op jit(solution)/shard_map/ppermute | solution.py:497
  75.9 12.1 %collective-permute-done.13.refs_6_ = bf16[384,768]{1,0:T(8,128)(2,1)S(1)} collective-permute-done((bf16[384,768]{1,0:T(8,128)(2,1)}, bf16[384,768]{1,0:T(8,128)(2,1)S(1)}, u32[]{:S(2)}, u32[]{:S(2)}) %collective-permute-start.13) | collective-permute-done | bytes 589856 | tf_op jit(solution)/shard_map/ppermute | solution.py:497
  91.2 14.3 %expert.1 = (bf16[8,192,768]{2,1,0:T(8,128)(2,1)}, bf16[8,192,768]{2,1,0:T(8,128)(2,1)}, bf16[1536,768]{1,0:T(8,128)(2,1)}, bf16[1536,768]{1,0:T(8,128)(2,1)}, b...) custom-call(s32[1]{0:T(128)} %bitcast.place.where, ...), custom_call_target="tpu_custom_call" | custom-call | tf_op jit(solution)/shard_map/expert/pallas_call | solution.py:411
  105.5 3.6 %all-to-all-start.1 = ((bf16[8,192,768]{2,1,0:T(8,128)(2,1)}), bf16[8,192,768]{2,1,0:T(8,128)(2,1)S(1)}, u32[]{:S(2)}, u32[]{:S(2)}) async-start(bf16[8,192,768]{2,1,0:T(8,128)(2,1)} %get-tuple-element.64), calls=%async_computation.1 | async-start | bytes 4718592 | tf_op jit(solution)/shard_map/all_to_all | solution.py:509
  109.2 6.0 %fusion.5 = f32[768,768]{1,0:T(8,128)} fusion(bf16[1536,768]{1,0:T(8,128)(2,1)} %get-tuple-element.67, bf16[1536,768]{1,0:T(8,128)(2,1)} %get-tuple-element.68), kind=kOutput, calls=%fused_computation.14 | convolution fusion | flops 1811939328 | bytes 7077888 | tf_op jit(solution)/shard_map/dot_general | solution.py:25
  115.2 3.5 %fusion.4 = f32[768,768]{1,0:T(8,128)} fusion(bf16[1536,768]{1,0:T(8,128)(2,1)S(1)} %copy-done.3, bf16[1536,768]{1,0:T(8,128)(2,1)S(1)} %copy-done.4), kind=kOutput, calls=%fused_computation.13 | convolution fusion | flops 1811939328 | bytes 7077888 | tf_op jit(solution)/shard_map/dot_general | solution.py:25
  118.7 19.9 %all-to-all-done.1 = bf16[8,192,768]{2,1,0:T(8,128)(2,1)S(1)} async-done(((bf16[8,192,768]{2,1,0:T(8,128)(2,1)}), bf16[8,192,768]{2,1,0:T(8,128)(2,1)S(1)}, u32[]{:S(2)}, u32[]{:S(2)}) %all-to-all-start.1) | async-done | bytes 2359328 | tf_op jit(solution)/shard_map/all_to_all | solution.py:509
  143.1 3.9 %all-to-all-start.2 = ((bf16[8,192,768]{2,1,0:T(8,128)(2,1)}), bf16[8,192,768]{2,1,0:T(8,128)(2,1)S(1)}, u32[]{:S(2)}, u32[]{:S(2)}) async-start(bf16[8,192,768]{2,1,0:T(8,128)(2,1)} %get-tuple-element.85), calls=%async_computation.2 | async-start | bytes 4718592 | tf_op jit(solution)/shard_map/all_to_all | solution.py:509
  152.8 6.3 %collective-permute-done.15.refs_1_ = bf16[128,768]{1,0:T(8,128)(2,1)S(1)} collective-permute-done((bf16[128,768]{1,0:T(8,128)(2,1)S(1)}, bf16[128,768]{1,0:T(8,128)(2,1)S(1)}, u32[]{:S(2)}, u32[]{:S(2)}) %collective-permute-start.15) | collective-permute-done | bytes 196640 | tf_op jit(solution)/shard_map/ppermute | solution.py:497
  159.1 8.3 %collective-permute-done.16.refs_2_ = bf16[128,768]{1,0:T(8,128)(2,1)S(1)} collective-permute-done((bf16[128,768]{1,0:T(8,128)(2,1)S(1)}, bf16[128,768]{1,0:T(8,128)(2,1)S(1)}, u32[]{:S(2)}, u32[]{:S(2)}) %collective-permute-start.16) | collective-permute-done | bytes 196640 | tf_op jit(solution)/shard_map/ppermute | solution.py:497
  168.2 6.1 %tail.1 = (f32[128,768]{1,0:T(8,128)}, bf16[128,768]{1,0:T(8,128)(2,1)}, bf16[4,112,768]{2,1,0:T(8,128)(2,1)}, bf16[4,112,768]{2,1,0:T(8,128)(2,1)}) custom-call(s32[1]{0:T(128)} %bitcast.place.where, bf16[128,768]{1,0:T(8,128)(2,1)} %get-tuple-element.70.refs_0_, bf16[128,768]{1,0:T(8,128)(2,1)} %copy-done.19, bf16[128,768]{1,0:T(8,128)(2,1)} %copy-done.20, ...), custom_call_target="tpu_custom_call" | custom-call | tf_op jit(solution)/shard_map/tail/pallas_call | solution.py:196
  187.9 3.5 %collective-permute-done.20 = bf16[112,768]{1,0:T(8,128)(2,1)S(1)} collective-permute-done((bf16[112,768]{1,0:T(8,128)(2,1)}, bf16[112,768]{1,0:T(8,128)(2,1)S(1)}, u32[]{:S(2)}, u32[]{:S(2)}) %collective-permute-start.20) | collective-permute-done | bytes 172064 | tf_op jit(solution)/shard_map/ppermute | solution.py:497
  191.5 3.7 %collective-permute-start.22 = (bf16[112,768]{1,0:T(8,128)(2,1)S(1)}, bf16[112,768]{1,0:T(8,128)(2,1)S(1)}, u32[]{:S(2)}, u32[]{:S(2)}) collective-permute-start(bf16[112,768]{1,0:T(8,128)(2,1)S(1)} %add_convert_fusion.2), channel_id=1, source_target_pairs={{0,8},{8,0},{16,24},{24,16},{1,9},{9,1},{17,25},{25,17},{2,10},{10... | collective-permute-start | bytes 516104 | tf_op jit(solution)/shard_map/ppermute | solution.py:497
  204.8 4.0 %conv_backward.1 = bf16[128,768]{1,0:T(8,128)(2,1)} custom-call(bf16[16,768]{1,0:T(8,128)(2,1)} %copy-done.35, bf16[128,768]{1,0:T(8,128)(2,1)} %get-tuple-element.90.own, bf16[16,768]{1,0:T(8,128)(2,1)} %copy-done.36, f32[160,128]{1,0:T(8,128)} %get-tuple-element.76.refs_11_.seg, f32[31,768]{1,0:T(8,128)} %weight.3, f32[128,768]{1,0:T(8,128)} %get-tuple-element.91.grad_mixed), custom_call_target="tpu_custom_call" | custom-call | tf_op jit(solution)/shard_map/conv_backward/pallas_call | solution.py:126
  210.5 4.6 %all-to-all-start.3 = ((bf16[4,128,768]{2,1,0:T(8,128)(2,1)}), bf16[4,128,768]{2,1,0:T(8,128)(2,1)S(1)}, u32[]{:S(2)}, u32[]{:S(2)}) async-start(bf16[4,128,768]{2,1,0:T(8,128)(2,1)} %collect_packs.1), calls=%async_computation.3 | async-start | bytes 1572864 | tf_op jit(solution)/shard_map/all_to_all | solution.py:509
  222.7 4.7 %collective-permute-done.28.refs_2_ = bf16[112,768]{1,0:T(8,128)(2,1)S(1)} collective-permute-done((bf16[112,768]{1,0:T(8,128)(2,1)S(1)}, bf16[112,768]{1,0:T(8,128)(2,1)S(1)}, u32[]{:S(2)}, u32[]{:S(2)}) %collective-permute-start.28) | collective-permute-done | bytes 172064 | tf_op jit(solution)/shard_map/ppermute | solution.py:497
  (156 shorter events, 79.6 us)
Async XLA Ops:
  2.3 18.3 %collective-permute-start.2 = (bf16[144,768]{1,0:T(8,128)(2,1)S(1)}, bf16[144,768]{1,0:T(8,128)(2,1)S(1)}, u32[]{:S(2)}, u32[]{:S(2)}) collective-permute-start(bf16[144,768]{1,0:T(8,128)(2,1)S(1)} %fusion.1.refs_0_), channel_id=1, source_target_pairs={{0,8},{8,0},{16,24},{24,16},{1,9},{9,1},{17,25},{25,17},{2,10},{10... | collective-permute-start | bytes 663560 | tf_op jit(solution)/shard_map/ppermute | solution.py:497
  5.4 18.7 %collective-permute-start.3 = (bf16[144,768]{1,0:T(8,128)(2,1)S(1)}, bf16[144,768]{1,0:T(8,128)(2,1)S(1)}, u32[]{:S(2)}, u32[]{:S(2)}) collective-permute-start(bf16[144,768]{1,0:T(8,128)(2,1)S(1)} %fusion.1.refs_0_), channel_id=1, source_target_pairs={{0,16},{8,24},{16,0},{24,8},{1,17},{9,25},{17,1},{25,9},{2,18},{10... | collective-permute-start | bytes 663560 | tf_op jit(solution)/shard_map/ppermute | solution.py:497
  8.0 16.2 %collective-permute-start.4 = (bf16[144,768]{1,0:T(8,128)(2,1)S(1)}, bf16[144,768]{1,0:T(8,128)(2,1)S(1)}, u32[]{:S(2)}, u32[]{:S(2)}) collective-permute-start(bf16[144,768]{1,0:T(8,128)(2,1)S(1)} %fusion.1.refs_0_), channel_id=1, source_target_pairs={{0,24},{8,16},{16,8},{24,0},{1,25},{9,17},{17,9},{25,1},{2,26},{10... | collective-permute-start | bytes 663560 | tf_op jit(solution)/shard_map/ppermute | solution.py:497
  29.4 60.4 %all-to-all-start = ((bf16[8,192,768]{2,1,0:T(8,128)(2,1)}), bf16[8,192,768]{2,1,0:T(8,128)(2,1)S(1)}, u32[]{:S(2)}, u32[]{:S(2)}) async-start(bf16[8,192,768]{2,1,0:T(8,128)(2,1)} %bitcast.36), calls=%async_computation | async-start | bytes 4718592 | tf_op jit(solution)/shard_map/all_to_all | solution.py:509
  33.2 12.5 %collective-permute-start.5 = (bf16[128,768]{1,0:T(8,128)(2,1)S(1)}, bf16[128,768]{1,0:T(8,128)(2,1)S(1)}, u32[]{:S(2)}, u32[]{:S(2)}) collective-permute-start(bf16[128,768]{1,0:T(8,128)(2,1)S(1)} %copy-done.9), channel_id=1, source_target_pairs={{0,8},{8,0},{16,24},{24,16},{1,9},{9,1},{17,25},{25,17},{2,10},{10... | collective-permute-start | bytes 589832 | tf_op jit(solution)/shard_map/ppermute | solution.py:497
  36.5 17.1 %collective-permute-start.6 = (bf16[128,768]{1,0:T(8,128)(2,1)S(1)}, bf16[128,768]{1,0:T(8,128)(2,1)S(1)}, u32[]{:S(2)}, u32[]{:S(2)}) collective-permute-start(bf16[128,768]{1,0:T(8,128)(2,1)S(1)} %copy-done.9), channel_id=1, source_target_pairs={{0,16},{8,24},{16,0},{24,8},{1,17},{9,25},{17,1},{25,9},{2,18},{10... | collective-permute-start | bytes 589832 | tf_op jit(solution)/shard_map/ppermute | solution.py:497
  37.6 16.0 %collective-permute-start.7 = (bf16[128,768]{1,0:T(8,128)(2,1)S(1)}, bf16[128,768]{1,0:T(8,128)(2,1)S(1)}, u32[]{:S(2)}, u32[]{:S(2)}) collective-permute-start(bf16[128,768]{1,0:T(8,128)(2,1)S(1)} %copy-done.9), channel_id=1, source_target_pairs={{0,24},{8,16},{16,8},{24,0},{1,25},{9,17},{17,9},{25,1},{2,26},{10... | collective-permute-start | bytes 589832 | tf_op jit(solution)/shard_map/ppermute | solution.py:497
  57.9 17.0 %collective-permute-start.9 = (bf16[384,768]{1,0:T(8,128)(2,1)}, bf16[384,768]{1,0:T(8,128)(2,1)S(1)}, u32[]{:S(2)}, u32[]{:S(2)}) collective-permute-start(bf16[384,768]{1,0:T(8,128)(2,1)} %get-tuple-element.60), channel_id=1, source_target_pairs={{0,2},{1,3},{2,0},{3,1},{4,6},{5,7},{6,4},{7,5},{8,10},{9,11},{10,... | collective-permute-start | bytes 1769480 | tf_op jit(solution)/shard_map/ppermute | solution.py:497
  59.8 15.9 %collective-permute-start.11 = (bf16[384,768]{1,0:T(8,128)(2,1)}, bf16[384,768]{1,0:T(8,128)(2,1)S(1)}, u32[]{:S(2)}, u32[]{:S(2)}) collective-permute-start(bf16[384,768]{1,0:T(8,128)(2,1)} %get-tuple-element.61), channel_id=1, source_target_pairs={{0,4},{1,5},{2,6},{3,7},{4,0},{5,1},{6,2},{7,3},{8,12},{9,13},{10,... | collective-permute-start | bytes 1769480 | tf_op jit(solution)/shard_map/ppermute | solution.py:497
  61.3 26.7 %collective-permute-start.13 = (bf16[384,768]{1,0:T(8,128)(2,1)}, bf16[384,768]{1,0:T(8,128)(2,1)S(1)}, u32[]{:S(2)}, u32[]{:S(2)}) collective-permute-start(bf16[384,768]{1,0:T(8,128)(2,1)} %get-tuple-element.62), channel_id=1, source_target_pairs={{0,6},{1,7},{2,4},{3,5},{4,2},{5,3},{6,0},{7,1},{8,14},{9,15},{10,... | collective-permute-start | bytes 1769480 | tf_op jit(solution)/shard_map/ppermute | solution.py:497
  61.4 26.7 %collective-permute-start.8 = (bf16[192,768]{1,0:T(8,128)(2,1)}, bf16[192,768]{1,0:T(8,128)(2,1)S(1)}, u32[]{:S(2)}, u32[]{:S(2)}) collective-permute-start(bf16[192,768]{1,0:T(8,128)(2,1)} %get-tuple-element.59), channel_id=1, source_target_pairs={{0,1},{1,0},{2,3},{3,2},{4,5},{5,4},{6,7},{7,6},{8,9},{9,8},{10,11... | collective-permute-start | bytes 884744 | tf_op jit(solution)/shard_map/ppermute | solution.py:497
  74.9 13.2 %collective-permute-start.10 = (bf16[192,768]{1,0:T(8,128)(2,1)S(1)}, bf16[192,768]{1,0:T(8,128)(2,1)S(1)}, u32[]{:S(2)}, u32[]{:S(2)}) collective-permute-start(bf16[192,768]{1,0:T(8,128)(2,1)S(1)} %slice.36), channel_id=1, source_target_pairs={{0,1},{1,0},{2,3},{3,2},{4,5},{5,4},{6,7},{7,6},{8,9},{9,8},{10,11... | collective-permute-start | bytes 884744 | tf_op jit(solution)/shard_map/ppermute | solution.py:497
  75.8 12.4 %collective-permute-start.12 = (bf16[192,768]{1,0:T(8,128)(2,1)S(1)}, bf16[192,768]{1,0:T(8,128)(2,1)S(1)}, u32[]{:S(2)}, u32[]{:S(2)}) collective-permute-start(bf16[192,768]{1,0:T(8,128)(2,1)S(1)} %slice.37), channel_id=1, source_target_pairs={{0,1},{1,0},{2,3},{3,2},{4,5},{5,4},{6,7},{7,6},{8,9},{9,8},{10,11... | collective-permute-start | bytes 884744 | tf_op jit(solution)/shard_map/ppermute | solution.py:497
  105.5 33.0 %all-to-all-start.1 = ((bf16[8,192,768]{2,1,0:T(8,128)(2,1)}), bf16[8,192,768]{2,1,0:T(8,128)(2,1)S(1)}, u32[]{:S(2)}, u32[]{:S(2)}) async-start(bf16[8,192,768]{2,1,0:T(8,128)(2,1)} %get-tuple-element.64), calls=%async_computation.1 | async-start | bytes 4718592 | tf_op jit(solution)/shard_map/all_to_all | solution.py:509
  143.1 40.1 %all-to-all-start.2 = ((bf16[8,192,768]{2,1,0:T(8,128)(2,1)}), bf16[8,192,768]{2,1,0:T(8,128)(2,1)S(1)}, u32[]{:S(2)}, u32[]{:S(2)}) async-start(bf16[8,192,768]{2,1,0:T(8,128)(2,1)} %get-tuple-element.85), calls=%async_computation.2 | async-start | bytes 4718592 | tf_op jit(solution)/shard_map/all_to_all | solution.py:509
  147.0 12.1 %collective-permute-start.15 = (bf16[128,768]{1,0:T(8,128)(2,1)S(1)}, bf16[128,768]{1,0:T(8,128)(2,1)S(1)}, u32[]{:S(2)}, u32[]{:S(2)}) collective-permute-start(bf16[128,768]{1,0:T(8,128)(2,1)S(1)} %copy-done.39), channel_id=1, source_target_pairs={{0,8},{8,0},{16,24},{24,16},{1,9},{9,1},{17,25},{25,17},{2,10},{10... | collective-permute-start | bytes 589832 | tf_op jit(solution)/shard_map/ppermute | solution.py:497
  150.3 17.1 %collective-permute-start.16 = (bf16[128,768]{1,0:T(8,128)(2,1)S(1)}, bf16[128,768]{1,0:T(8,128)(2,1)S(1)}, u32[]{:S(2)}, u32[]{:S(2)}) collective-permute-start(bf16[128,768]{1,0:T(8,128)(2,1)S(1)} %copy-done.38), channel_id=1, source_target_pairs={{0,16},{8,24},{16,0},{24,8},{1,17},{9,25},{17,1},{25,9},{2,18},{10... | collective-permute-start | bytes 589832 | tf_op jit(solution)/shard_map/ppermute | solution.py:497
  151.4 16.0 %collective-permute-start.17 = (bf16[128,768]{1,0:T(8,128)(2,1)S(1)}, bf16[128,768]{1,0:T(8,128)(2,1)S(1)}, u32[]{:S(2)}, u32[]{:S(2)}) collective-permute-start(bf16[128,768]{1,0:T(8,128)(2,1)S(1)} %copy-done.37), channel_id=1, source_target_pairs={{0,24},{8,16},{16,8},{24,0},{1,25},{9,17},{17,9},{25,1},{2,26},{10... | collective-permute-start | bytes 589832 | tf_op jit(solution)/shard_map/ppermute | solution.py:497
  191.5 17.3 %collective-permute-start.22 = (bf16[112,768]{1,0:T(8,128)(2,1)S(1)}, bf16[112,768]{1,0:T(8,128)(2,1)S(1)}, u32[]{:S(2)}, u32[]{:S(2)}) collective-permute-start(bf16[112,768]{1,0:T(8,128)(2,1)S(1)} %add_convert_fusion.2), channel_id=1, source_target_pairs={{0,8},{8,0},{16,24},{24,16},{1,9},{9,1},{17,25},{25,17},{2,10},{10... | collective-permute-start | bytes 516104 | tf_op jit(solution)/shard_map/ppermute | solution.py:497
  195.2 15.2 %collective-permute-start.23 = (bf16[112,768]{1,0:T(8,128)(2,1)S(1)}, bf16[112,768]{1,0:T(8,128)(2,1)S(1)}, u32[]{:S(2)}, u32[]{:S(2)}) collective-permute-start(bf16[112,768]{1,0:T(8,128)(2,1)S(1)} %add_convert_fusion.2), channel_id=1, source_target_pairs={{0,16},{8,24},{16,0},{24,8},{1,17},{9,25},{17,1},{25,9},{2,18},{10... | collective-permute-start | bytes 516104 | tf_op jit(solution)/shard_map/ppermute | solution.py:497
  196.2 14.2 %collective-permute-start.24 = (bf16[112,768]{1,0:T(8,128)(2,1)S(1)}, bf16[112,768]{1,0:T(8,128)(2,1)S(1)}, u32[]{:S(2)}, u32[]{:S(2)}) collective-permute-start(bf16[112,768]{1,0:T(8,128)(2,1)S(1)} %add_convert_fusion.2), channel_id=1, source_target_pairs={{0,24},{8,16},{16,8},{24,0},{1,25},{9,17},{17,9},{25,1},{2,26},{10... | collective-permute-start | bytes 516104 | tf_op jit(solution)/shard_map/ppermute | solution.py:497
  210.5 25.3 %all-to-all-start.3 = ((bf16[4,128,768]{2,1,0:T(8,128)(2,1)}), bf16[4,128,768]{2,1,0:T(8,128)(2,1)S(1)}, u32[]{:S(2)}, u32[]{:S(2)}) async-start(bf16[4,128,768]{2,1,0:T(8,128)(2,1)} %collect_packs.1), calls=%async_computation.3 | async-start | bytes 1572864 | tf_op jit(solution)/shard_map/all_to_all | solution.py:509
  216.6 10.8 %collective-permute-start.28 = (bf16[112,768]{1,0:T(8,128)(2,1)S(1)}, bf16[112,768]{1,0:T(8,128)(2,1)S(1)}, u32[]{:S(2)}, u32[]{:S(2)}) collective-permute-start(bf16[112,768]{1,0:T(8,128)(2,1)S(1)} %add_convert_fusion.1.refs_0_), channel_id=1, source_target_pairs={{0,4},{1,5},{2,6},{3,7},{4,0},{5,1},{6,2},{7,3},{8,12},{9,13},{10,... | collective-permute-start | bytes 516104 | tf_op jit(solution)/shard_map/ppermute | solution.py:497
  217.2 10.3 %collective-permute-start.29 = (bf16[112,768]{1,0:T(8,128)(2,1)S(1)}, bf16[112,768]{1,0:T(8,128)(2,1)S(1)}, u32[]{:S(2)}, u32[]{:S(2)}) collective-permute-start(bf16[112,768]{1,0:T(8,128)(2,1)S(1)} %add_convert_fusion.1.refs_0_), channel_id=1, source_target_pairs={{0,6},{1,7},{2,4},{3,5},{4,2},{5,3},{6,0},{7,1},{8,14},{9,15},{10,... | collective-permute-start | bytes 516104 | tf_op jit(solution)/shard_map/ppermute | solution.py:497
  (54 other events, 268.4 us)

commit v6 on v5

--- a/solution.py
+++ b/solution.py
@@ -149,6 +149,7 @@
         cot, conv, act, point_w, before, own, after, seg, router_part = refs[count : count + 9]
         grad_mixed, grad_conv, mine, theirs, scratch, shared = refs[count + 9 :]
         core = where[0] % 2
+        here = where[0] // 2
         total = cot[...].astype(F32)
         for part in parts:
             total = total + part[...].astype(F32)
@@ -190,8 +191,9 @@
             return carry
 
         lax.fori_loop(0, width // LANES, column, 0)
-        mine[...] = shared[core]
-        theirs[...] = shared[1 - core]
+        for index in range(groups):
+            mine[index] = shared[core, here ^ index]
+            theirs[index] = shared[1 - core, here ^ index]
 
     return pl.pallas_call(
         kernel,
@@ -442,24 +444,6 @@
     )(where, *rows, cots, *weights, router_weight)
 
 
-def add_pieces(mine, theirs, group):
-    groups, size, width = mine.shape
-
-    def kernel(group, mine, theirs, *outs):
-        for index, out in enumerate(outs):
-            here = group[0] ^ index
-            out[...] = (mine[here].astype(F32) + theirs[here].astype(F32)).astype(BF16)
-
-    return pl.pallas_call(
-        kernel,
-        in_specs=[pl.BlockSpec(memory_space=pltpu.SMEM)]
-        + [pl.BlockSpec(memory_space=pltpu.VMEM)] * 2,
-        out_shape=[shape((size, width), BF16)] * groups,
-        compiler_params=PARAMS,
-        name="add_pieces",
-    )(group, mine, theirs)
-
-
 def spread(own, other, group, core, used, taps, experts):
     count = len(own)
     size, width = own[0].shape
@@ -598,7 +582,7 @@
     grad_win = dot_rows(rows, grad_pre)
     back_home, grad_wout, grad_win = lax.optimization_barrier((back_home, grad_wout, grad_win))
     back_parts = collect(tables, back_home.reshape(-1, width), experts, capacity)
-    gated_home = exchange(after_all(gated, back_parts), "seq")
+    gated_home = exchange(after_all(gated, (back_home,)), "seq")
     back_own = to_all(back_parts, "dp")
 
     core = place_here % 2
@@ -620,7 +604,8 @@
         taps,
         experts,
     )
-    pieces = add_pieces(mine, swap(theirs, "seq", 1), group[None])
+    theirs = swap(theirs, "seq", 1)
+    pieces = [sum_parts([mine[m], theirs[m]]).astype(BF16) for m in range(groups)]
     pieces = [pieces[0]] + [swap(pieces[m], "seq", 2 * m) for m in range(1, groups)]
     pack_here = lax.axis_index("dp")[None]
     gated_parts = collect_packs(

time: 238 us -> 237 us (level)
    unnamed x80 -> x70, local copies, waits for them, and re-layouts: 11.8 us -> 11 us
  transfers between devices with their start and end apart: 38 -> 38, of which waited for: 19 -> 21; matrix products, arithmetic and copies ran while one was open for 5% -> 6% of each run, Pallas kernels for 11% -> 12%
where the time goes in v6:
time: 237 us; the launch traced here: 236 us
  waiting for transfers between devices  105 us (44%)
  starting transfers between devices  55.8 us (24%)
  Pallas kernels  46.3 us (20%)
  local copies, waits for them, and re-layouts  12.6 us (5%)
  matrix products  9.47 us (4%)
  other arithmetic  5.26 us (2%)
    ppermute x30, waiting for transfers between devices, swap(): return lax.ppermute(array, axis, [(i, i ^ k) for i in range(devices)])  75.8 us
    ppermute x30, starting transfers between devices, swap(): return lax.ppermute(array, axis, [(i, i ^ k) for i in range(devices)])  34.7 us
    all_to_all x4, waiting for transfers between devices, exchange(): return lax.all_to_all(array, axis, split_axis=0, concat_axis=0, tiled=True)  22.4 us
    all_to_all x4, starting transfers between devices, exchange(): return lax.all_to_all(array, axis, split_axis=0, concat_axis=0, tiled=True)  15.9 us
    pallas_call x1, Pallas kernels, expert(): pl.pallas_call(kernel, grid_spec=pltpu.PrefetchScalarGridSpec(num_scalar_...  14.3 us
    unnamed x70, local copies, waits for them, and re-layouts  11 us
    dot_general x2, matrix products, dot_rows(): lax.dot_general(a, b, (((0,), (0,)), ((), ())), preferred_element_type=F32)  9.47 us
    ppermute x2, waiting for transfers between devices, edges(): after = lax.ppermute(array[:EDGE], axis, down)  7.12 us
  transfers between devices with their start and end apart: 38, of which 21 were waited for; matrix products, arithmetic and copies ran while one was open for 6% of the time, Pallas kernels for 12%

profile of v6, /device:TPU:0, one launch (start us, length us, event | category | flops | bytes accessed | tf_op | source)
XLA Modules:
  0.0 235.8 jit_solution(5525773113864212804)
XLA Ops:
  11.3 3.7 %collective-permute-done.1.after.refs_10_ = bf16[16,768]{1,0:T(8,128)(2,1)S(1)} collective-permute-done((bf16[16,768]{1,0:T(8,128)(2,1)S(1)}, bf16[16,768]{1,0:T(8,128)(2,1)S(1)}, u32[]{:S(2)}, u32[]{:S(2)}) %collective-permute-start.1) | collective-permute-done | bytes 24608 | tf_op jit(solution)/shard_map/ppermute | solution.py:520
  15.6 5.0 %conv_forward.1 = (f32[128,768]{1,0:T(8,128)}, bf16[128,768]{1,0:T(8,128)(2,1)}, bf16[128,768]{1,0:T(8,128)(2,1)}, f32[160,128]{1,0:T(8,128)}) custom-call(s32[1]{0:T(128)} %bitcast.place.where, bf16[16,768]{1,0:T(8,128)(2,1)} %copy-done.31, bf16[128,768]{1,0:T(8,128)(2,1)} %bitcast.47, bf16[16,768]{1,0:T(8,128)(2,1)} %copy-done.32, s32[1,1024]{1,0:T(1,128)} %segments.1, ...), custom_call_target="tpu_custom_call" | custom-call | tf_op jit(solution)/shard_map/conv_forward/pallas_call | solution.py:87
  20.6 3.5 %collective-permute-done.3.refs_2_ = bf16[144,768]{1,0:T(8,128)(2,1)S(1)} collective-permute-done((bf16[144,768]{1,0:T(8,128)(2,1)S(1)}, bf16[144,768]{1,0:T(8,128)(2,1)S(1)}, u32[]{:S(2)}, u32[]{:S(2)}) %collective-permute-start.3) | collective-permute-done | bytes 221216 | tf_op jit(solution)/shard_map/ppermute | solution.py:481
  25.5 3.9 %place_packets.1 = (bf16[1536,768]{1,0:T(8,128)(2,1)}, bf16[4,384,128]{2,1,0:T(8,128)(2,1)}) custom-call(bf16[144,768]{1,0:T(8,128)(2,1)} %copy-done.8, bf16[144,768]{1,0:T(8,128)(2,1)} %copy-done.15, bf16[144,768]{1,0:T(8,128)(2,1)} %copy-done.16, bf16[144,768]{1,0:T(8,128)(2,1)} %copy-done.17), custom_call_target="tpu_custom_call" | custom-call | tf_op jit(solution)/shard_map/place_packets/pallas_call | solution.py:249
  29.4 3.9 %all-to-all-start = ((bf16[8,192,768]{2,1,0:T(8,128)(2,1)}), bf16[8,192,768]{2,1,0:T(8,128)(2,1)S(1)}, u32[]{:S(2)}, u32[]{:S(2)}) async-start(bf16[8,192,768]{2,1,0:T(8,128)(2,1)} %bitcast.44), calls=%async_computation | async-start | bytes 4718592 | tf_op jit(solution)/shard_map/all_to_all | solution.py:493
  39.0 6.8 %collective-permute-done.5.refs_2_ = bf16[128,768]{1,0:T(8,128)(2,1)S(1)} collective-permute-done((bf16[128,768]{1,0:T(8,128)(2,1)S(1)}, bf16[128,768]{1,0:T(8,128)(2,1)S(1)}, u32[]{:S(2)}, u32[]{:S(2)}) %collective-permute-start.5) | collective-permute-done | bytes 196640 | tf_op jit(solution)/shard_map/ppermute | solution.py:481
  45.8 7.8 %collective-permute-done.6.refs_3_ = bf16[128,768]{1,0:T(8,128)(2,1)S(1)} collective-permute-done((bf16[128,768]{1,0:T(8,128)(2,1)S(1)}, bf16[128,768]{1,0:T(8,128)(2,1)S(1)}, u32[]{:S(2)}, u32[]{:S(2)}) %collective-permute-start.6) | collective-permute-done | bytes 196640 | tf_op jit(solution)/shard_map/ppermute | solution.py:481
  54.4 3.5 %place_rows.1 = (bf16[192,768]{1,0:T(8,128)(2,1)}, bf16[192,768]{1,0:T(8,128)(2,1)}, bf16[384,768]{1,0:T(8,128)(2,1)}, bf16[384,768]{1,0:T(8,128)(2,1)}, bf16[384,768]{1,0:T(8,128)(2,1)}) custom-call(s32[1]{0:T(128)} %bitcast.place.where, bf16[4,384,128]{2,1,0:T(8,128)(2,1)} %get-tuple-element.51.refs_0_.table, bf16[128,768]{1,0:T(8,128)(2,1)} %get-tuple-element.53.refs_1_, ...), custom_call_target="tpu_custom_call" | custom-call | tf_op jit(solution)/shard_map/place_rows/pallas_call | solution.py:287
  61.4 13.6 %collective-permute-done.9.refs_2_ = bf16[384,768]{1,0:T(8,128)(2,1)S(1)} collective-permute-done((bf16[384,768]{1,0:T(8,128)(2,1)}, bf16[384,768]{1,0:T(8,128)(2,1)S(1)}, u32[]{:S(2)}, u32[]{:S(2)}) %collective-permute-start.9) | collective-permute-done | bytes 589856 | tf_op jit(solution)/shard_map/ppermute | solution.py:481
  75.9 12.2 %collective-permute-done.13.refs_6_ = bf16[384,768]{1,0:T(8,128)(2,1)S(1)} collective-permute-done((bf16[384,768]{1,0:T(8,128)(2,1)}, bf16[384,768]{1,0:T(8,128)(2,1)S(1)}, u32[]{:S(2)}, u32[]{:S(2)}) %collective-permute-start.13) | collective-permute-done | bytes 589856 | tf_op jit(solution)/shard_map/ppermute | solution.py:481
  91.3 14.3 %expert.1 = (bf16[8,192,768]{2,1,0:T(8,128)(2,1)}, bf16[8,192,768]{2,1,0:T(8,128)(2,1)}, bf16[1536,768]{1,0:T(8,128)(2,1)}, bf16[1536,768]{1,0:T(8,128)(2,1)}, b...) custom-call(s32[1]{0:T(128)} %bitcast.place.where, ...), custom_call_target="tpu_custom_call" | custom-call | tf_op jit(solution)/shard_map/expert/pallas_call | solution.py:413
  105.6 3.6 %all-to-all-start.1 = ((bf16[8,192,768]{2,1,0:T(8,128)(2,1)}), bf16[8,192,768]{2,1,0:T(8,128)(2,1)S(1)}, u32[]{:S(2)}, u32[]{:S(2)}) async-start(bf16[8,192,768]{2,1,0:T(8,128)(2,1)} %get-tuple-element.60), calls=%async_computation.1 | async-start | bytes 4718592 | tf_op jit(solution)/shard_map/all_to_all | solution.py:493
  109.2 6.0 %fusion.9 = f32[768,768]{1,0:T(8,128)} fusion(bf16[1536,768]{1,0:T(8,128)(2,1)} %get-tuple-element.63, bf16[1536,768]{1,0:T(8,128)(2,1)} %get-tuple-element.64), kind=kOutput, calls=%fused_computation.22 | convolution fusion | flops 1811939328 | bytes 7077888 | tf_op jit(solution)/shard_map/dot_general | solution.py:25
  115.2 3.5 %fusion.8 = f32[768,768]{1,0:T(8,128)} fusion(bf16[1536,768]{1,0:T(8,128)(2,1)S(1)} %copy-done.3, bf16[1536,768]{1,0:T(8,128)(2,1)S(1)} %copy-done.4), kind=kOutput, calls=%fused_computation.21 | convolution fusion | flops 1811939328 | bytes 7077888 | tf_op jit(solution)/shard_map/dot_general | solution.py:25
  118.7 19.9 %all-to-all-done.1 = bf16[8,192,768]{2,1,0:T(8,128)(2,1)S(1)} async-done(((bf16[8,192,768]{2,1,0:T(8,128)(2,1)}), bf16[8,192,768]{2,1,0:T(8,128)(2,1)S(1)}, u32[]{:S(2)}, u32[]{:S(2)}) %all-to-all-start.1) | async-done | bytes 2359328 | tf_op jit(solution)/shard_map/all_to_all | solution.py:493
  140.0 3.8 %all-to-all-start.2 = ((bf16[8,192,768]{2,1,0:T(8,128)(2,1)}), bf16[8,192,768]{2,1,0:T(8,128)(2,1)S(1)}, u32[]{:S(2)}, u32[]{:S(2)}) async-start(bf16[8,192,768]{2,1,0:T(8,128)(2,1)} %get-tuple-element.77), calls=%async_computation.2 | async-start | bytes 4718592 | tf_op jit(solution)/shard_map/all_to_all | solution.py:493
  152.6 6.7 %collective-permute-done.15.refs_1_ = bf16[128,768]{1,0:T(8,128)(2,1)S(1)} collective-permute-done((bf16[128,768]{1,0:T(8,128)(2,1)}, bf16[128,768]{1,0:T(8,128)(2,1)S(1)}, u32[]{:S(2)}, u32[]{:S(2)}) %collective-permute-start.15) | collective-permute-done | bytes 196640 | tf_op jit(solution)/shard_map/ppermute | solution.py:481
  159.2 8.1 %collective-permute-done.16.refs_2_ = bf16[128,768]{1,0:T(8,128)(2,1)S(1)} collective-permute-done((bf16[128,768]{1,0:T(8,128)(2,1)}, bf16[128,768]{1,0:T(8,128)(2,1)S(1)}, u32[]{:S(2)}, u32[]{:S(2)}) %collective-permute-start.16) | collective-permute-done | bytes 196640 | tf_op jit(solution)/shard_map/ppermute | solution.py:481
  168.2 6.2 %tail.1 = (f32[128,768]{1,0:T(8,128)}, bf16[128,768]{1,0:T(8,128)(2,1)}, bf16[4,112,768]{2,1,0:T(8,128)(2,1)}, bf16[4,112,768]{2,1,0:T(8,128)(2,1)}) custom-call(s32[1]{0:T(128)} %bitcast.place.where, bf16[128,768]{1,0:T(8,128)(2,1)} %get-tuple-element.66.refs_0_, bf16[128,768]{1,0:T(8,128)(2,1)} %copy-done.18, bf16[128,768]{1,0:T(8,128)(2,1)} %copy-done.19, ...), custom_call_target="tpu_custom_call" | custom-call | tf_op jit(solution)/shard_map/tail/pallas_call | solution.py:198
  190.4 3.7 %collective-permute-start.22 = (bf16[112,768]{1,0:T(8,128)(2,1)S(1)}, bf16[112,768]{1,0:T(8,128)(2,1)S(1)}, u32[]{:S(2)}, u32[]{:S(2)}) collective-permute-start(bf16[112,768]{1,0:T(8,128)(2,1)S(1)} %add_convert_fusion.2), channel_id=1, source_target_pairs={{0,8},{8,0},{16,24},{24,16},{1,9},{9,1},{17,25},{25,17},{2,10},{10... | collective-permute-start | bytes 516104 | tf_op jit(solution)/shard_map/ppermute | solution.py:481
  203.9 4.0 %conv_backward.1 = bf16[128,768]{1,0:T(8,128)(2,1)} custom-call(bf16[16,768]{1,0:T(8,128)(2,1)} %copy-done.33, bf16[128,768]{1,0:T(8,128)(2,1)} %get-tuple-element.82.own, bf16[16,768]{1,0:T(8,128)(2,1)} %copy-done.34, f32[160,128]{1,0:T(8,128)} %get-tuple-element.72.refs_11_.seg, f32[31,768]{1,0:T(8,128)} %weight.3, f32[128,768]{1,0:T(8,128)} %get-tuple-element.83.grad_mixed), custom_call_target="tpu_custom_call" | custom-call | tf_op jit(solution)/shard_map/conv_backward/pallas_call | solution.py:126
  209.6 4.7 %all-to-all-start.3 = ((bf16[4,128,768]{2,1,0:T(8,128)(2,1)}), bf16[4,128,768]{2,1,0:T(8,128)(2,1)S(1)}, u32[]{:S(2)}, u32[]{:S(2)}) async-start(bf16[4,128,768]{2,1,0:T(8,128)(2,1)} %collect_packs.1), calls=%async_computation.3 | async-start | bytes 1572864 | tf_op jit(solution)/shard_map/all_to_all | solution.py:493
  217.9 3.6 %collective-permute-done.27.refs_1_ = bf16[112,768]{1,0:T(8,128)(2,1)S(1)} collective-permute-done((bf16[112,768]{1,0:T(8,128)(2,1)S(1)}, bf16[112,768]{1,0:T(8,128)(2,1)S(1)}, u32[]{:S(2)}, u32[]{:S(2)}) %collective-permute-start.27) | collective-permute-done | bytes 172064 | tf_op jit(solution)/shard_map/ppermute | solution.py:481
  221.6 5.0 %collective-permute-done.28.refs_2_ = bf16[112,768]{1,0:T(8,128)(2,1)S(1)} collective-permute-done((bf16[112,768]{1,0:T(8,128)(2,1)S(1)}, bf16[112,768]{1,0:T(8,128)(2,1)S(1)}, u32[]{:S(2)}, u32[]{:S(2)}) %collective-permute-start.28) | collective-permute-done | bytes 172064 | tf_op jit(solution)/shard_map/ppermute | solution.py:481
  (146 shorter events, 78.0 us)
Async XLA Ops:
  2.3 18.3 %collective-permute-start.2 = (bf16[144,768]{1,0:T(8,128)(2,1)S(1)}, bf16[144,768]{1,0:T(8,128)(2,1)S(1)}, u32[]{:S(2)}, u32[]{:S(2)}) collective-permute-start(bf16[144,768]{1,0:T(8,128)(2,1)S(1)} %fusion.1.refs_0_), channel_id=1, source_target_pairs={{0,8},{8,0},{16,24},{24,16},{1,9},{9,1},{17,25},{25,17},{2,10},{10... | collective-permute-start | bytes 663560 | tf_op jit(solution)/shard_map/ppermute | solution.py:481
  5.4 18.7 %collective-permute-start.3 = (bf16[144,768]{1,0:T(8,128)(2,1)S(1)}, bf16[144,768]{1,0:T(8,128)(2,1)S(1)}, u32[]{:S(2)}, u32[]{:S(2)}) collective-permute-start(bf16[144,768]{1,0:T(8,128)(2,1)S(1)} %fusion.1.refs_0_), channel_id=1, source_target_pairs={{0,16},{8,24},{16,0},{24,8},{1,17},{9,25},{17,1},{25,9},{2,18},{10... | collective-permute-start | bytes 663560 | tf_op jit(solution)/shard_map/ppermute | solution.py:481
  8.0 16.2 %collective-permute-start.4 = (bf16[144,768]{1,0:T(8,128)(2,1)S(1)}, bf16[144,768]{1,0:T(8,128)(2,1)S(1)}, u32[]{:S(2)}, u32[]{:S(2)}) collective-permute-start(bf16[144,768]{1,0:T(8,128)(2,1)S(1)} %fusion.1.refs_0_), channel_id=1, source_target_pairs={{0,24},{8,16},{16,8},{24,0},{1,25},{9,17},{17,9},{25,1},{2,26},{10... | collective-permute-start | bytes 663560 | tf_op jit(solution)/shard_map/ppermute | solution.py:481
  29.4 60.4 %all-to-all-start = ((bf16[8,192,768]{2,1,0:T(8,128)(2,1)}), bf16[8,192,768]{2,1,0:T(8,128)(2,1)S(1)}, u32[]{:S(2)}, u32[]{:S(2)}) async-start(bf16[8,192,768]{2,1,0:T(8,128)(2,1)} %bitcast.44), calls=%async_computation | async-start | bytes 4718592 | tf_op jit(solution)/shard_map/all_to_all | solution.py:493
  33.3 12.5 %collective-permute-start.5 = (bf16[128,768]{1,0:T(8,128)(2,1)S(1)}, bf16[128,768]{1,0:T(8,128)(2,1)S(1)}, u32[]{:S(2)}, u32[]{:S(2)}) collective-permute-start(bf16[128,768]{1,0:T(8,128)(2,1)S(1)} %copy-done.9), channel_id=1, source_target_pairs={{0,8},{8,0},{16,24},{24,16},{1,9},{9,1},{17,25},{25,17},{2,10},{10... | collective-permute-start | bytes 589832 | tf_op jit(solution)/shard_map/ppermute | solution.py:481
  36.5 17.1 %collective-permute-start.6 = (bf16[128,768]{1,0:T(8,128)(2,1)S(1)}, bf16[128,768]{1,0:T(8,128)(2,1)S(1)}, u32[]{:S(2)}, u32[]{:S(2)}) collective-permute-start(bf16[128,768]{1,0:T(8,128)(2,1)S(1)} %copy-done.9), channel_id=1, source_target_pairs={{0,16},{8,24},{16,0},{24,8},{1,17},{9,25},{17,1},{25,9},{2,18},{10... | collective-permute-start | bytes 589832 | tf_op jit(solution)/shard_map/ppermute | solution.py:481
  37.6 16.0 %collective-permute-start.7 = (bf16[128,768]{1,0:T(8,128)(2,1)S(1)}, bf16[128,768]{1,0:T(8,128)(2,1)S(1)}, u32[]{:S(2)}, u32[]{:S(2)}) collective-permute-start(bf16[128,768]{1,0:T(8,128)(2,1)S(1)} %copy-done.9), channel_id=1, source_target_pairs={{0,24},{8,16},{16,8},{24,0},{1,25},{9,17},{17,9},{25,1},{2,26},{10... | collective-permute-start | bytes 589832 | tf_op jit(solution)/shard_map/ppermute | solution.py:481
  57.9 17.0 %collective-permute-start.9 = (bf16[384,768]{1,0:T(8,128)(2,1)}, bf16[384,768]{1,0:T(8,128)(2,1)S(1)}, u32[]{:S(2)}, u32[]{:S(2)}) collective-permute-start(bf16[384,768]{1,0:T(8,128)(2,1)} %get-tuple-element.56), channel_id=1, source_target_pairs={{0,2},{1,3},{2,0},{3,1},{4,6},{5,7},{6,4},{7,5},{8,10},{9,11},{10,... | collective-permute-start | bytes 1769480 | tf_op jit(solution)/shard_map/ppermute | solution.py:481
  59.8 16.0 %collective-permute-start.11 = (bf16[384,768]{1,0:T(8,128)(2,1)}, bf16[384,768]{1,0:T(8,128)(2,1)S(1)}, u32[]{:S(2)}, u32[]{:S(2)}) collective-permute-start(bf16[384,768]{1,0:T(8,128)(2,1)} %get-tuple-element.57), channel_id=1, source_target_pairs={{0,4},{1,5},{2,6},{3,7},{4,0},{5,1},{6,2},{7,3},{8,12},{9,13},{10,... | collective-permute-start | bytes 1769480 | tf_op jit(solution)/shard_map/ppermute | solution.py:481
  61.3 26.8 %collective-permute-start.13 = (bf16[384,768]{1,0:T(8,128)(2,1)}, bf16[384,768]{1,0:T(8,128)(2,1)S(1)}, u32[]{:S(2)}, u32[]{:S(2)}) collective-permute-start(bf16[384,768]{1,0:T(8,128)(2,1)} %get-tuple-element.58), channel_id=1, source_target_pairs={{0,6},{1,7},{2,4},{3,5},{4,2},{5,3},{6,0},{7,1},{8,14},{9,15},{10,... | collective-permute-start | bytes 1769480 | tf_op jit(solution)/shard_map/ppermute | solution.py:481
  61.4 26.8 %collective-permute-start.8 = (bf16[192,768]{1,0:T(8,128)(2,1)}, bf16[192,768]{1,0:T(8,128)(2,1)S(1)}, u32[]{:S(2)}, u32[]{:S(2)}) collective-permute-start(bf16[192,768]{1,0:T(8,128)(2,1)} %get-tuple-element.55), channel_id=1, source_target_pairs={{0,1},{1,0},{2,3},{3,2},{4,5},{5,4},{6,7},{7,6},{8,9},{9,8},{10,11... | collective-permute-start | bytes 884744 | tf_op jit(solution)/shard_map/ppermute | solution.py:481
  74.9 13.2 %collective-permute-start.10 = (bf16[192,768]{1,0:T(8,128)(2,1)S(1)}, bf16[192,768]{1,0:T(8,128)(2,1)S(1)}, u32[]{:S(2)}, u32[]{:S(2)}) collective-permute-start(bf16[192,768]{1,0:T(8,128)(2,1)S(1)} %slice.68), channel_id=1, source_target_pairs={{0,1},{1,0},{2,3},{3,2},{4,5},{5,4},{6,7},{7,6},{8,9},{9,8},{10,11... | collective-permute-start | bytes 884744 | tf_op jit(solution)/shard_map/ppermute | solution.py:481
  75.8 12.4 %collective-permute-start.12 = (bf16[192,768]{1,0:T(8,128)(2,1)S(1)}, bf16[192,768]{1,0:T(8,128)(2,1)S(1)}, u32[]{:S(2)}, u32[]{:S(2)}) collective-permute-start(bf16[192,768]{1,0:T(8,128)(2,1)S(1)} %slice.69), channel_id=1, source_target_pairs={{0,1},{1,0},{2,3},{3,2},{4,5},{5,4},{6,7},{7,6},{8,9},{9,8},{10,11... | collective-permute-start | bytes 884744 | tf_op jit(solution)/shard_map/ppermute | solution.py:481
  105.6 33.0 %all-to-all-start.1 = ((bf16[8,192,768]{2,1,0:T(8,128)(2,1)}), bf16[8,192,768]{2,1,0:T(8,128)(2,1)S(1)}, u32[]{:S(2)}, u32[]{:S(2)}) async-start(bf16[8,192,768]{2,1,0:T(8,128)(2,1)} %get-tuple-element.60), calls=%async_computation.1 | async-start | bytes 4718592 | tf_op jit(solution)/shard_map/all_to_all | solution.py:493
  140.0 42.2 %all-to-all-start.2 = ((bf16[8,192,768]{2,1,0:T(8,128)(2,1)}), bf16[8,192,768]{2,1,0:T(8,128)(2,1)S(1)}, u32[]{:S(2)}, u32[]{:S(2)}) async-start(bf16[8,192,768]{2,1,0:T(8,128)(2,1)} %get-tuple-element.77), calls=%async_computation.2 | async-start | bytes 4718592 | tf_op jit(solution)/shard_map/all_to_all | solution.py:493
  146.9 12.3 %collective-permute-start.15 = (bf16[128,768]{1,0:T(8,128)(2,1)}, bf16[128,768]{1,0:T(8,128)(2,1)S(1)}, u32[]{:S(2)}, u32[]{:S(2)}) collective-permute-start(bf16[128,768]{1,0:T(8,128)(2,1)} %get-tuple-element.67), channel_id=1, source_target_pairs={{0,8},{8,0},{16,24},{24,16},{1,9},{9,1},{17,25},{25,17},{2,10},{10... | collective-permute-start | bytes 589832 | tf_op jit(solution)/shard_map/ppermute | solution.py:481
  150.1 17.3 %collective-permute-start.16 = (bf16[128,768]{1,0:T(8,128)(2,1)}, bf16[128,768]{1,0:T(8,128)(2,1)S(1)}, u32[]{:S(2)}, u32[]{:S(2)}) collective-permute-start(bf16[128,768]{1,0:T(8,128)(2,1)} %get-tuple-element.68), channel_id=1, source_target_pairs={{0,16},{8,24},{16,0},{24,8},{1,17},{9,25},{17,1},{25,9},{2,18},{10... | collective-permute-start | bytes 589832 | tf_op jit(solution)/shard_map/ppermute | solution.py:481
  151.1 16.3 %collective-permute-start.17 = (bf16[128,768]{1,0:T(8,128)(2,1)}, bf16[128,768]{1,0:T(8,128)(2,1)S(1)}, u32[]{:S(2)}, u32[]{:S(2)}) collective-permute-start(bf16[128,768]{1,0:T(8,128)(2,1)} %get-tuple-element.69), channel_id=1, source_target_pairs={{0,24},{8,16},{16,8},{24,0},{1,25},{9,17},{17,9},{25,1},{2,26},{10... | collective-permute-start | bytes 589832 | tf_op jit(solution)/shard_map/ppermute | solution.py:481
  190.4 17.6 %collective-permute-start.22 = (bf16[112,768]{1,0:T(8,128)(2,1)S(1)}, bf16[112,768]{1,0:T(8,128)(2,1)S(1)}, u32[]{:S(2)}, u32[]{:S(2)}) collective-permute-start(bf16[112,768]{1,0:T(8,128)(2,1)S(1)} %add_convert_fusion.2), channel_id=1, source_target_pairs={{0,8},{8,0},{16,24},{24,16},{1,9},{9,1},{17,25},{25,17},{2,10},{10... | collective-permute-start | bytes 516104 | tf_op jit(solution)/shard_map/ppermute | solution.py:481
  194.1 15.4 %collective-permute-start.23 = (bf16[112,768]{1,0:T(8,128)(2,1)S(1)}, bf16[112,768]{1,0:T(8,128)(2,1)S(1)}, u32[]{:S(2)}, u32[]{:S(2)}) collective-permute-start(bf16[112,768]{1,0:T(8,128)(2,1)S(1)} %add_convert_fusion.2), channel_id=1, source_target_pairs={{0,16},{8,24},{16,0},{24,8},{1,17},{9,25},{17,1},{25,9},{2,18},{10... | collective-permute-start | bytes 516104 | tf_op jit(solution)/shard_map/ppermute | solution.py:481
  195.2 14.3 %collective-permute-start.24 = (bf16[112,768]{1,0:T(8,128)(2,1)S(1)}, bf16[112,768]{1,0:T(8,128)(2,1)S(1)}, u32[]{:S(2)}, u32[]{:S(2)}) collective-permute-start(bf16[112,768]{1,0:T(8,128)(2,1)S(1)} %add_convert_fusion.2), channel_id=1, source_target_pairs={{0,24},{8,16},{16,8},{24,0},{1,25},{9,17},{17,9},{25,1},{2,26},{10... | collective-permute-start | bytes 516104 | tf_op jit(solution)/shard_map/ppermute | solution.py:481
  209.6 25.4 %all-to-all-start.3 = ((bf16[4,128,768]{2,1,0:T(8,128)(2,1)}), bf16[4,128,768]{2,1,0:T(8,128)(2,1)S(1)}, u32[]{:S(2)}, u32[]{:S(2)}) async-start(bf16[4,128,768]{2,1,0:T(8,128)(2,1)} %collect_packs.1), calls=%async_computation.3 | async-start | bytes 1572864 | tf_op jit(solution)/shard_map/all_to_all | solution.py:493
  215.7 10.9 %collective-permute-start.28 = (bf16[112,768]{1,0:T(8,128)(2,1)S(1)}, bf16[112,768]{1,0:T(8,128)(2,1)S(1)}, u32[]{:S(2)}, u32[]{:S(2)}) collective-permute-start(bf16[112,768]{1,0:T(8,128)(2,1)S(1)} %add_convert_fusion.1.refs_0_), channel_id=1, source_target_pairs={{0,4},{1,5},{2,6},{3,7},{4,0},{5,1},{6,2},{7,3},{8,12},{9,13},{10,... | collective-permute-start | bytes 516104 | tf_op jit(solution)/shard_map/ppermute | solution.py:481
  216.3 10.4 %collective-permute-start.29 = (bf16[112,768]{1,0:T(8,128)(2,1)S(1)}, bf16[112,768]{1,0:T(8,128)(2,1)S(1)}, u32[]{:S(2)}, u32[]{:S(2)}) collective-permute-start(bf16[112,768]{1,0:T(8,128)(2,1)S(1)} %add_convert_fusion.1.refs_0_), channel_id=1, source_target_pairs={{0,6},{1,7},{2,4},{3,5},{4,2},{5,3},{6,0},{7,1},{8,14},{9,15},{10,... | collective-permute-start | bytes 516104 | tf_op jit(solution)/shard_map/ppermute | solution.py:481
  (49 other events, 236.0 us)

commit v7 on v6

--- a/solution.py
+++ b/solution.py
@@ -228,6 +228,23 @@
         slot = jnp.sum(named[j] * counts, axis=0, keepdims=True)
         table = jnp.where(row == ids[j : j + 1, :] * capacity + slot, 1.0, table)
     return table.astype(BF16)
+
+
+def pack(cot, ids):
+    rows, width = cot.shape
+
+    def kernel(cot, ids, out):
+        out[:rows, :] = cot[...]
+        low = jnp.concatenate([ids[...].astype(F32), jnp.zeros((EDGE - 2, rows), F32)], axis=0)
+        out[rows:, :] = jnp.zeros((EDGE, width), BF16)
+        out[rows:, 0:rows] = low.astype(BF16)
+
+    return pl.pallas_call(
+        kernel,
+        out_shape=shape((rows + EDGE, width), BF16),
+        compiler_params=PARAMS,
+        name="pack",
+    )(cot, ids)
 
 
 def place_packets(packets, experts, capacity):
@@ -552,8 +569,7 @@
 
     where = place_here[None]
 
-    ids = jnp.pad(expert_ids[0].T.astype(BF16), ((0, EDGE - 2), (0, width - rows_here)))
-    packet = jnp.concatenate([own_cot, ids], axis=0)
+    packet = pack(own_cot, expert_ids[0].T)
     packets = from_all(packet, "dp")
     conv, activated, mixed, seg = conv_forward(
         before, own_frames, after, segments, conv_weight, point_weight, where

time: 237 us -> 237 us (level)
    unnamed x70 -> x68, local copies, waits for them, and re-layouts: 11 us -> 11 us
where the time goes in v7:
time: 237 us; the launch traced here: 236 us
  waiting for transfers between devices  106 us (45%)
  starting transfers between devices  55.6 us (23%)
  Pallas kernels  48 us (20%)
  local copies, waits for them, and re-layouts  12.6 us (5%)
  matrix products  9.47 us (4%)
  other arithmetic  3.58 us (2%)
    ppermute x30, waiting for transfers between devices, swap(): return lax.ppermute(array, axis, [(i, i ^ k) for i in range(devices)])  76.1 us
    ppermute x30, starting transfers between devices, swap(): return lax.ppermute(array, axis, [(i, i ^ k) for i in range(devices)])  34.6 us
    all_to_all x4, waiting for transfers between devices, exchange(): return lax.all_to_all(array, axis, split_axis=0, concat_axis=0, tiled=True)  22.4 us
    all_to_all x4, starting transfers between devices, exchange(): return lax.all_to_all(array, axis, split_axis=0, concat_axis=0, tiled=True)  15.9 us
    pallas_call x1, Pallas kernels, expert(): pl.pallas_call(kernel, grid_spec=pltpu.PrefetchScalarGridSpec(num_scalar_...  14.3 us
    unnamed x68, local copies, waits for them, and re-layouts  11 us
    dot_general x2, matrix products, dot_rows(): lax.dot_general(a, b, (((0,), (0,)), ((), ())), preferred_element_type=F32)  9.47 us
    ppermute x2, waiting for transfers between devices, edges(): after = lax.ppermute(array[:EDGE], axis, down)  7.12 us
  transfers between devices with their start and end apart: 38, of which 21 were waited for; matrix products, arithmetic and copies ran while one was open for 6% of the time, Pallas kernels for 12%

profile of v7, /device:TPU:0, one launch (start us, length us, event | category | flops | bytes accessed | tf_op | source)
XLA Modules:
  0.0 235.9 jit_solution(18306761802349679785)
XLA Ops:
  11.3 3.7 %collective-permute-done.1.after.refs_10_ = bf16[16,768]{1,0:T(8,128)(2,1)S(1)} collective-permute-done((bf16[16,768]{1,0:T(8,128)(2,1)S(1)}, bf16[16,768]{1,0:T(8,128)(2,1)S(1)}, u32[]{:S(2)}, u32[]{:S(2)}) %collective-permute-start.1) | collective-permute-done | bytes 24608 | tf_op jit(solution)/shard_map/ppermute | solution.py:537
  15.6 5.0 %conv_forward.1 = (f32[128,768]{1,0:T(8,128)}, bf16[128,768]{1,0:T(8,128)(2,1)}, bf16[128,768]{1,0:T(8,128)(2,1)}, f32[160,128]{1,0:T(8,128)}) custom-call(s32[1]{0:T(128)} %bitcast.place.where, bf16[16,768]{1,0:T(8,128)(2,1)} %copy-done.30, bf16[128,768]{1,0:T(8,128)(2,1)} %bitcast.46, bf16[16,768]{1,0:T(8,128)(2,1)} %copy-done.31, s32[1,1024]{1,0:T(1,128)} %segments.1, ...), custom_call_target="tpu_custom_call" | custom-call | tf_op jit(solution)/shard_map/conv_forward/pallas_call | solution.py:87
  20.5 3.7 %collective-permute-done.3.refs_2_ = bf16[144,768]{1,0:T(8,128)(2,1)S(1)} collective-permute-done((bf16[144,768]{1,0:T(8,128)(2,1)}, bf16[144,768]{1,0:T(8,128)(2,1)S(1)}, u32[]{:S(2)}, u32[]{:S(2)}) %collective-permute-start.3) | collective-permute-done | bytes 221216 | tf_op jit(solution)/shard_map/ppermute | solution.py:498
  25.6 3.9 %place_packets.1 = (bf16[1536,768]{1,0:T(8,128)(2,1)}, bf16[4,384,128]{2,1,0:T(8,128)(2,1)}) custom-call(bf16[144,768]{1,0:T(8,128)(2,1)} %pack.1.refs_0_, bf16[144,768]{1,0:T(8,128)(2,1)} %copy-done.14, bf16[144,768]{1,0:T(8,128)(2,1)} %copy-done.15, bf16[144,768]{1,0:T(8,128)(2,1)} %copy-done.16), custom_call_target="tpu_custom_call" | custom-call | tf_op jit(solution)/shard_map/place_packets/pallas_call | solution.py:266
  29.5 3.9 %all-to-all-start = ((bf16[8,192,768]{2,1,0:T(8,128)(2,1)}), bf16[8,192,768]{2,1,0:T(8,128)(2,1)S(1)}, u32[]{:S(2)}, u32[]{:S(2)}) async-start(bf16[8,192,768]{2,1,0:T(8,128)(2,1)} %bitcast.43), calls=%async_computation | async-start | bytes 4718592 | tf_op jit(solution)/shard_map/all_to_all | solution.py:510
  39.1 6.8 %collective-permute-done.5.refs_2_ = bf16[128,768]{1,0:T(8,128)(2,1)S(1)} collective-permute-done((bf16[128,768]{1,0:T(8,128)(2,1)S(1)}, bf16[128,768]{1,0:T(8,128)(2,1)S(1)}, u32[]{:S(2)}, u32[]{:S(2)}) %collective-permute-start.5) | collective-permute-done | bytes 196640 | tf_op jit(solution)/shard_map/ppermute | solution.py:498
  45.9 7.9 %collective-permute-done.6.refs_3_ = bf16[128,768]{1,0:T(8,128)(2,1)S(1)} collective-permute-done((bf16[128,768]{1,0:T(8,128)(2,1)S(1)}, bf16[128,768]{1,0:T(8,128)(2,1)S(1)}, u32[]{:S(2)}, u32[]{:S(2)}) %collective-permute-start.6) | collective-permute-done | bytes 196640 | tf_op jit(solution)/shard_map/ppermute | solution.py:498
  54.5 3.5 %place_rows.1 = (bf16[192,768]{1,0:T(8,128)(2,1)}, bf16[192,768]{1,0:T(8,128)(2,1)}, bf16[384,768]{1,0:T(8,128)(2,1)}, bf16[384,768]{1,0:T(8,128)(2,1)}, bf16[384,768]{1,0:T(8,128)(2,1)}) custom-call(s32[1]{0:T(128)} %bitcast.place.where, bf16[4,384,128]{2,1,0:T(8,128)(2,1)} %get-tuple-element.51.refs_0_.table, bf16[128,768]{1,0:T(8,128)(2,1)} %get-tuple-element.53.refs_1_, ...), custom_call_target="tpu_custom_call" | custom-call | tf_op jit(solution)/shard_map/place_rows/pallas_call | solution.py:304
  61.5 13.5 %collective-permute-done.9.refs_2_ = bf16[384,768]{1,0:T(8,128)(2,1)S(1)} collective-permute-done((bf16[384,768]{1,0:T(8,128)(2,1)}, bf16[384,768]{1,0:T(8,128)(2,1)S(1)}, u32[]{:S(2)}, u32[]{:S(2)}) %collective-permute-start.9) | collective-permute-done | bytes 589856 | tf_op jit(solution)/shard_map/ppermute | solution.py:498
  76.0 12.2 %collective-permute-done.13.refs_6_ = bf16[384,768]{1,0:T(8,128)(2,1)S(1)} collective-permute-done((bf16[384,768]{1,0:T(8,128)(2,1)}, bf16[384,768]{1,0:T(8,128)(2,1)S(1)}, u32[]{:S(2)}, u32[]{:S(2)}) %collective-permute-start.13) | collective-permute-done | bytes 589856 | tf_op jit(solution)/shard_map/ppermute | solution.py:498
  91.4 14.3 %expert.1 = (bf16[8,192,768]{2,1,0:T(8,128)(2,1)}, bf16[8,192,768]{2,1,0:T(8,128)(2,1)}, bf16[1536,768]{1,0:T(8,128)(2,1)}, bf16[1536,768]{1,0:T(8,128)(2,1)}, b...) custom-call(s32[1]{0:T(128)} %bitcast.place.where, ...), custom_call_target="tpu_custom_call" | custom-call | tf_op jit(solution)/shard_map/expert/pallas_call | solution.py:430
  105.7 3.6 %all-to-all-start.1 = ((bf16[8,192,768]{2,1,0:T(8,128)(2,1)}), bf16[8,192,768]{2,1,0:T(8,128)(2,1)S(1)}, u32[]{:S(2)}, u32[]{:S(2)}) async-start(bf16[8,192,768]{2,1,0:T(8,128)(2,1)} %get-tuple-element.60), calls=%async_computation.1 | async-start | bytes 4718592 | tf_op jit(solution)/shard_map/all_to_all | solution.py:510
  109.4 6.0 %fusion.7 = f32[768,768]{1,0:T(8,128)} fusion(bf16[1536,768]{1,0:T(8,128)(2,1)} %get-tuple-element.63, bf16[1536,768]{1,0:T(8,128)(2,1)} %get-tuple-element.64), kind=kOutput, calls=%fused_computation.18 | convolution fusion | flops 1811939328 | bytes 7077888 | tf_op jit(solution)/shard_map/dot_general | solution.py:25
  115.4 3.5 %fusion.6 = f32[768,768]{1,0:T(8,128)} fusion(bf16[1536,768]{1,0:T(8,128)(2,1)S(1)} %copy-done.3, bf16[1536,768]{1,0:T(8,128)(2,1)S(1)} %copy-done.4), kind=kOutput, calls=%fused_computation.17 | convolution fusion | flops 1811939328 | bytes 7077888 | tf_op jit(solution)/shard_map/dot_general | solution.py:25
  118.9 19.9 %all-to-all-done.1 = bf16[8,192,768]{2,1,0:T(8,128)(2,1)S(1)} async-done(((bf16[8,192,768]{2,1,0:T(8,128)(2,1)}), bf16[8,192,768]{2,1,0:T(8,128)(2,1)S(1)}, u32[]{:S(2)}, u32[]{:S(2)}) %all-to-all-start.1) | async-done | bytes 2359328 | tf_op jit(solution)/shard_map/all_to_all | solution.py:510
  140.1 3.8 %all-to-all-start.2 = ((bf16[8,192,768]{2,1,0:T(8,128)(2,1)}), bf16[8,192,768]{2,1,0:T(8,128)(2,1)S(1)}, u32[]{:S(2)}, u32[]{:S(2)}) async-start(bf16[8,192,768]{2,1,0:T(8,128)(2,1)} %get-tuple-element.77), calls=%async_computation.2 | async-start | bytes 4718592 | tf_op jit(solution)/shard_map/all_to_all | solution.py:510
  152.7 6.7 %collective-permute-done.15.refs_1_ = bf16[128,768]{1,0:T(8,128)(2,1)S(1)} collective-permute-done((bf16[128,768]{1,0:T(8,128)(2,1)}, bf16[128,768]{1,0:T(8,128)(2,1)S(1)}, u32[]{:S(2)}, u32[]{:S(2)}) %collective-permute-start.15) | collective-permute-done | bytes 196640 | tf_op jit(solution)/shard_map/ppermute | solution.py:498
  159.4 8.2 %collective-permute-done.16.refs_2_ = bf16[128,768]{1,0:T(8,128)(2,1)S(1)} collective-permute-done((bf16[128,768]{1,0:T(8,128)(2,1)}, bf16[128,768]{1,0:T(8,128)(2,1)S(1)}, u32[]{:S(2)}, u32[]{:S(2)}) %collective-permute-start.16) | collective-permute-done | bytes 196640 | tf_op jit(solution)/shard_map/ppermute | solution.py:498
  168.3 6.2 %tail.1 = (f32[128,768]{1,0:T(8,128)}, bf16[128,768]{1,0:T(8,128)(2,1)}, bf16[4,112,768]{2,1,0:T(8,128)(2,1)}, bf16[4,112,768]{2,1,0:T(8,128)(2,1)}) custom-call(s32[1]{0:T(128)} %bitcast.place.where, bf16[128,768]{1,0:T(8,128)(2,1)} %get-tuple-element.66.refs_0_, bf16[128,768]{1,0:T(8,128)(2,1)} %copy-done.17, bf16[128,768]{1,0:T(8,128)(2,1)} %copy-done.18, ...), custom_call_target="tpu_custom_call" | custom-call | tf_op jit(solution)/shard_map/tail/pallas_call | solution.py:198
  190.5 3.7 %collective-permute-start.22 = (bf16[112,768]{1,0:T(8,128)(2,1)S(1)}, bf16[112,768]{1,0:T(8,128)(2,1)S(1)}, u32[]{:S(2)}, u32[]{:S(2)}) collective-permute-start(bf16[112,768]{1,0:T(8,128)(2,1)S(1)} %add_convert_fusion.2), channel_id=1, source_target_pairs={{0,8},{8,0},{16,24},{24,16},{1,9},{9,1},{17,25},{25,17},{2,10},{10... | collective-permute-start | bytes 516104 | tf_op jit(solution)/shard_map/ppermute | solution.py:498
  204.1 4.0 %conv_backward.1 = bf16[128,768]{1,0:T(8,128)(2,1)} custom-call(bf16[16,768]{1,0:T(8,128)(2,1)} %copy-done.32, bf16[128,768]{1,0:T(8,128)(2,1)} %get-tuple-element.82.own, bf16[16,768]{1,0:T(8,128)(2,1)} %copy-done.33, f32[160,128]{1,0:T(8,128)} %get-tuple-element.72.refs_11_.seg, f32[31,768]{1,0:T(8,128)} %weight.3, f32[128,768]{1,0:T(8,128)} %get-tuple-element.83.grad_mixed), custom_call_target="tpu_custom_call" | custom-call | tf_op jit(solution)/shard_map/conv_backward/pallas_call | solution.py:126
  209.7 4.6 %all-to-all-start.3 = ((bf16[4,128,768]{2,1,0:T(8,128)(2,1)}), bf16[4,128,768]{2,1,0:T(8,128)(2,1)S(1)}, u32[]{:S(2)}, u32[]{:S(2)}) async-start(bf16[4,128,768]{2,1,0:T(8,128)(2,1)} %collect_packs.1), calls=%async_computation.3 | async-start | bytes 1572864 | tf_op jit(solution)/shard_map/all_to_all | solution.py:510
  218.1 3.6 %collective-permute-done.27.refs_1_ = bf16[112,768]{1,0:T(8,128)(2,1)S(1)} collective-permute-done((bf16[112,768]{1,0:T(8,128)(2,1)S(1)}, bf16[112,768]{1,0:T(8,128)(2,1)S(1)}, u32[]{:S(2)}, u32[]{:S(2)}) %collective-permute-start.27) | collective-permute-done | bytes 172064 | tf_op jit(solution)/shard_map/ppermute | solution.py:498
  221.7 5.0 %collective-permute-done.28.refs_2_ = bf16[112,768]{1,0:T(8,128)(2,1)S(1)} collective-permute-done((bf16[112,768]{1,0:T(8,128)(2,1)S(1)}, bf16[112,768]{1,0:T(8,128)(2,1)S(1)}, u32[]{:S(2)}, u32[]{:S(2)}) %collective-permute-start.28) | collective-permute-done | bytes 172064 | tf_op jit(solution)/shard_map/ppermute | solution.py:498
  (143 shorter events, 77.9 us)
Async XLA Ops:
  2.3 18.3 %collective-permute-start.2 = (bf16[144,768]{1,0:T(8,128)(2,1)}, bf16[144,768]{1,0:T(8,128)(2,1)S(1)}, u32[]{:S(2)}, u32[]{:S(2)}) collective-permute-start(bf16[144,768]{1,0:T(8,128)(2,1)} %pack.1.refs_0_), channel_id=1, source_target_pairs={{0,8},{8,0},{16,24},{24,16},{1,9},{9,1},{17,25},{25,17},{2,10},{10... | collective-permute-start | bytes 663560 | tf_op jit(solution)/shard_map/ppermute | solution.py:498
  5.3 18.9 %collective-permute-start.3 = (bf16[144,768]{1,0:T(8,128)(2,1)}, bf16[144,768]{1,0:T(8,128)(2,1)S(1)}, u32[]{:S(2)}, u32[]{:S(2)}) collective-permute-start(bf16[144,768]{1,0:T(8,128)(2,1)} %pack.1.refs_0_), channel_id=1, source_target_pairs={{0,16},{8,24},{16,0},{24,8},{1,17},{9,25},{17,1},{25,9},{2,18},{10... | collective-permute-start | bytes 663560 | tf_op jit(solution)/shard_map/ppermute | solution.py:498
  7.9 16.4 %collective-permute-start.4 = (bf16[144,768]{1,0:T(8,128)(2,1)}, bf16[144,768]{1,0:T(8,128)(2,1)S(1)}, u32[]{:S(2)}, u32[]{:S(2)}) collective-permute-start(bf16[144,768]{1,0:T(8,128)(2,1)} %pack.1.refs_0_), channel_id=1, source_target_pairs={{0,24},{8,16},{16,8},{24,0},{1,25},{9,17},{17,9},{25,1},{2,26},{10... | collective-permute-start | bytes 663560 | tf_op jit(solution)/shard_map/ppermute | solution.py:498
  29.5 60.4 %all-to-all-start = ((bf16[8,192,768]{2,1,0:T(8,128)(2,1)}), bf16[8,192,768]{2,1,0:T(8,128)(2,1)S(1)}, u32[]{:S(2)}, u32[]{:S(2)}) async-start(bf16[8,192,768]{2,1,0:T(8,128)(2,1)} %bitcast.43), calls=%async_computation | async-start | bytes 4718592 | tf_op jit(solution)/shard_map/all_to_all | solution.py:510
  33.4 12.5 %collective-permute-start.5 = (bf16[128,768]{1,0:T(8,128)(2,1)S(1)}, bf16[128,768]{1,0:T(8,128)(2,1)S(1)}, u32[]{:S(2)}, u32[]{:S(2)}) collective-permute-start(bf16[128,768]{1,0:T(8,128)(2,1)S(1)} %copy-done.8), channel_id=1, source_target_pairs={{0,8},{8,0},{16,24},{24,16},{1,9},{9,1},{17,25},{25,17},{2,10},{10... | collective-permute-start | bytes 589832 | tf_op jit(solution)/shard_map/ppermute | solution.py:498
  36.7 17.1 %collective-permute-start.6 = (bf16[128,768]{1,0:T(8,128)(2,1)S(1)}, bf16[128,768]{1,0:T(8,128)(2,1)S(1)}, u32[]{:S(2)}, u32[]{:S(2)}) collective-permute-start(bf16[128,768]{1,0:T(8,128)(2,1)S(1)} %copy-done.8), channel_id=1, source_target_pairs={{0,16},{8,24},{16,0},{24,8},{1,17},{9,25},{17,1},{25,9},{2,18},{10... | collective-permute-start | bytes 589832 | tf_op jit(solution)/shard_map/ppermute | solution.py:498
  37.7 16.1 %collective-permute-start.7 = (bf16[128,768]{1,0:T(8,128)(2,1)S(1)}, bf16[128,768]{1,0:T(8,128)(2,1)S(1)}, u32[]{:S(2)}, u32[]{:S(2)}) collective-permute-start(bf16[128,768]{1,0:T(8,128)(2,1)S(1)} %copy-done.8), channel_id=1, source_target_pairs={{0,24},{8,16},{16,8},{24,0},{1,25},{9,17},{17,9},{25,1},{2,26},{10... | collective-permute-start | bytes 589832 | tf_op jit(solution)/shard_map/ppermute | solution.py:498
  58.0 17.0 %collective-permute-start.9 = (bf16[384,768]{1,0:T(8,128)(2,1)}, bf16[384,768]{1,0:T(8,128)(2,1)S(1)}, u32[]{:S(2)}, u32[]{:S(2)}) collective-permute-start(bf16[384,768]{1,0:T(8,128)(2,1)} %get-tuple-element.56), channel_id=1, source_target_pairs={{0,2},{1,3},{2,0},{3,1},{4,6},{5,7},{6,4},{7,5},{8,10},{9,11},{10,... | collective-permute-start | bytes 1769480 | tf_op jit(solution)/shard_map/ppermute | solution.py:498
  60.0 15.9 %collective-permute-start.11 = (bf16[384,768]{1,0:T(8,128)(2,1)}, bf16[384,768]{1,0:T(8,128)(2,1)S(1)}, u32[]{:S(2)}, u32[]{:S(2)}) collective-permute-start(bf16[384,768]{1,0:T(8,128)(2,1)} %get-tuple-element.57), channel_id=1, source_target_pairs={{0,4},{1,5},{2,6},{3,7},{4,0},{5,1},{6,2},{7,3},{8,12},{9,13},{10,... | collective-permute-start | bytes 1769480 | tf_op jit(solution)/shard_map/ppermute | solution.py:498
  61.4 26.7 %collective-permute-start.13 = (bf16[384,768]{1,0:T(8,128)(2,1)}, bf16[384,768]{1,0:T(8,128)(2,1)S(1)}, u32[]{:S(2)}, u32[]{:S(2)}) collective-permute-start(bf16[384,768]{1,0:T(8,128)(2,1)} %get-tuple-element.58), channel_id=1, source_target_pairs={{0,6},{1,7},{2,4},{3,5},{4,2},{5,3},{6,0},{7,1},{8,14},{9,15},{10,... | collective-permute-start | bytes 1769480 | tf_op jit(solution)/shard_map/ppermute | solution.py:498
  61.5 26.7 %collective-permute-start.8 = (bf16[192,768]{1,0:T(8,128)(2,1)}, bf16[192,768]{1,0:T(8,128)(2,1)S(1)}, u32[]{:S(2)}, u32[]{:S(2)}) collective-permute-start(bf16[192,768]{1,0:T(8,128)(2,1)} %get-tuple-element.55), channel_id=1, source_target_pairs={{0,1},{1,0},{2,3},{3,2},{4,5},{5,4},{6,7},{7,6},{8,9},{9,8},{10,11... | collective-permute-start | bytes 884744 | tf_op jit(solution)/shard_map/ppermute | solution.py:498
  75.1 13.2 %collective-permute-start.10 = (bf16[192,768]{1,0:T(8,128)(2,1)S(1)}, bf16[192,768]{1,0:T(8,128)(2,1)S(1)}, u32[]{:S(2)}, u32[]{:S(2)}) collective-permute-start(bf16[192,768]{1,0:T(8,128)(2,1)S(1)} %slice.68), channel_id=1, source_target_pairs={{0,1},{1,0},{2,3},{3,2},{4,5},{5,4},{6,7},{7,6},{8,9},{9,8},{10,11... | collective-permute-start | bytes 884744 | tf_op jit(solution)/shard_map/ppermute | solution.py:498
  75.9 12.4 %collective-permute-start.12 = (bf16[192,768]{1,0:T(8,128)(2,1)S(1)}, bf16[192,768]{1,0:T(8,128)(2,1)S(1)}, u32[]{:S(2)}, u32[]{:S(2)}) collective-permute-start(bf16[192,768]{1,0:T(8,128)(2,1)S(1)} %slice.69), channel_id=1, source_target_pairs={{0,1},{1,0},{2,3},{3,2},{4,5},{5,4},{6,7},{7,6},{8,9},{9,8},{10,11... | collective-permute-start | bytes 884744 | tf_op jit(solution)/shard_map/ppermute | solution.py:498
  105.7 33.0 %all-to-all-start.1 = ((bf16[8,192,768]{2,1,0:T(8,128)(2,1)}), bf16[8,192,768]{2,1,0:T(8,128)(2,1)S(1)}, u32[]{:S(2)}, u32[]{:S(2)}) async-start(bf16[8,192,768]{2,1,0:T(8,128)(2,1)} %get-tuple-element.60), calls=%async_computation.1 | async-start | bytes 4718592 | tf_op jit(solution)/shard_map/all_to_all | solution.py:510
  140.1 42.2 %all-to-all-start.2 = ((bf16[8,192,768]{2,1,0:T(8,128)(2,1)}), bf16[8,192,768]{2,1,0:T(8,128)(2,1)S(1)}, u32[]{:S(2)}, u32[]{:S(2)}) async-start(bf16[8,192,768]{2,1,0:T(8,128)(2,1)} %get-tuple-element.77), calls=%async_computation.2 | async-start | bytes 4718592 | tf_op jit(solution)/shard_map/all_to_all | solution.py:510
  147.1 12.3 %collective-permute-start.15 = (bf16[128,768]{1,0:T(8,128)(2,1)}, bf16[128,768]{1,0:T(8,128)(2,1)S(1)}, u32[]{:S(2)}, u32[]{:S(2)}) collective-permute-start(bf16[128,768]{1,0:T(8,128)(2,1)} %get-tuple-element.67), channel_id=1, source_target_pairs={{0,8},{8,0},{16,24},{24,16},{1,9},{9,1},{17,25},{25,17},{2,10},{10... | collective-permute-start | bytes 589832 | tf_op jit(solution)/shard_map/ppermute | solution.py:498
  150.2 17.3 %collective-permute-start.16 = (bf16[128,768]{1,0:T(8,128)(2,1)}, bf16[128,768]{1,0:T(8,128)(2,1)S(1)}, u32[]{:S(2)}, u32[]{:S(2)}) collective-permute-start(bf16[128,768]{1,0:T(8,128)(2,1)} %get-tuple-element.68), channel_id=1, source_target_pairs={{0,16},{8,24},{16,0},{24,8},{1,17},{9,25},{17,1},{25,9},{2,18},{10... | collective-permute-start | bytes 589832 | tf_op jit(solution)/shard_map/ppermute | solution.py:498
  151.2 16.3 %collective-permute-start.17 = (bf16[128,768]{1,0:T(8,128)(2,1)}, bf16[128,768]{1,0:T(8,128)(2,1)S(1)}, u32[]{:S(2)}, u32[]{:S(2)}) collective-permute-start(bf16[128,768]{1,0:T(8,128)(2,1)} %get-tuple-element.69), channel_id=1, source_target_pairs={{0,24},{8,16},{16,8},{24,0},{1,25},{9,17},{17,9},{25,1},{2,26},{10... | collective-permute-start | bytes 589832 | tf_op jit(solution)/shard_map/ppermute | solution.py:498
  190.5 17.6 %collective-permute-start.22 = (bf16[112,768]{1,0:T(8,128)(2,1)S(1)}, bf16[112,768]{1,0:T(8,128)(2,1)S(1)}, u32[]{:S(2)}, u32[]{:S(2)}) collective-permute-start(bf16[112,768]{1,0:T(8,128)(2,1)S(1)} %add_convert_fusion.2), channel_id=1, source_target_pairs={{0,8},{8,0},{16,24},{24,16},{1,9},{9,1},{17,25},{25,17},{2,10},{10... | collective-permute-start | bytes 516104 | tf_op jit(solution)/shard_map/ppermute | solution.py:498
  194.2 15.4 %collective-permute-start.23 = (bf16[112,768]{1,0:T(8,128)(2,1)S(1)}, bf16[112,768]{1,0:T(8,128)(2,1)S(1)}, u32[]{:S(2)}, u32[]{:S(2)}) collective-permute-start(bf16[112,768]{1,0:T(8,128)(2,1)S(1)} %add_convert_fusion.2), channel_id=1, source_target_pairs={{0,16},{8,24},{16,0},{24,8},{1,17},{9,25},{17,1},{25,9},{2,18},{10... | collective-permute-start | bytes 516104 | tf_op jit(solution)/shard_map/ppermute | solution.py:498
  195.3 14.3 %collective-permute-start.24 = (bf16[112,768]{1,0:T(8,128)(2,1)S(1)}, bf16[112,768]{1,0:T(8,128)(2,1)S(1)}, u32[]{:S(2)}, u32[]{:S(2)}) collective-permute-start(bf16[112,768]{1,0:T(8,128)(2,1)S(1)} %add_convert_fusion.2), channel_id=1, source_target_pairs={{0,24},{8,16},{16,8},{24,0},{1,25},{9,17},{17,9},{25,1},{2,26},{10... | collective-permute-start | bytes 516104 | tf_op jit(solution)/shard_map/ppermute | solution.py:498
  209.7 25.3 %all-to-all-start.3 = ((bf16[4,128,768]{2,1,0:T(8,128)(2,1)}), bf16[4,128,768]{2,1,0:T(8,128)(2,1)S(1)}, u32[]{:S(2)}, u32[]{:S(2)}) async-start(bf16[4,128,768]{2,1,0:T(8,128)(2,1)} %collect_packs.1), calls=%async_computation.3 | async-start | bytes 1572864 | tf_op jit(solution)/shard_map/all_to_all | solution.py:510
  215.8 10.9 %collective-permute-start.28 = (bf16[112,768]{1,0:T(8,128)(2,1)S(1)}, bf16[112,768]{1,0:T(8,128)(2,1)S(1)}, u32[]{:S(2)}, u32[]{:S(2)}) collective-permute-start(bf16[112,768]{1,0:T(8,128)(2,1)S(1)} %add_convert_fusion.1.refs_0_), channel_id=1, source_target_pairs={{0,4},{1,5},{2,6},{3,7},{4,0},{5,1},{6,2},{7,3},{8,12},{9,13},{10,... | collective-permute-start | bytes 516104 | tf_op jit(solution)/shard_map/ppermute | solution.py:498
  216.4 10.4 %collective-permute-start.29 = (bf16[112,768]{1,0:T(8,128)(2,1)S(1)}, bf16[112,768]{1,0:T(8,128)(2,1)S(1)}, u32[]{:S(2)}, u32[]{:S(2)}) collective-permute-start(bf16[112,768]{1,0:T(8,128)(2,1)S(1)} %add_convert_fusion.1.refs_0_), channel_id=1, source_target_pairs={{0,6},{1,7},{2,4},{3,5},{4,2},{5,3},{6,0},{7,1},{8,14},{9,15},{10,... | collective-permute-start | bytes 516104 | tf_op jit(solution)/shard_map/ppermute | solution.py:498
  (48 other events, 214.3 us)
